TPU v7x, 32 devices: a whole 2x2x4 slice. The times are simulated.
32 devices in a mesh: rows: 8 (over z, y), cols: 4 (over x, core).
Axes of the slice: x: 2, y: 2, z: 4, core: 2. Of those that a mesh axis runs over, the one named last changes fastest.
Arguments:
- right_leaf: float32 [4, 2048, 128], P(None, 'rows'), may hold values from -6 to 6
- right_mid: float32 [2, 4096, 128], P(None, 'rows'), may hold values from -6 to 6
- right_root: float32 [8192, 128], P('rows'), may hold values from -6 to 6
- inverse_leaf: float32 [4, 2048, 2048], P(None, 'rows', 'cols'), may hold values from -1 to 2, as said below
- inverse_mid: float32 [2, 4096, 4096], P(None, 'rows', 'cols'), may hold values from -1 to 2, as said below
- inverse_root: float32 [8192, 8192], P('rows', 'cols'), may hold values from -1 to 2, as said below
- leaf_to_mid: float32 [4, 4096, 2048], P(None, 'rows', 'cols'), may hold values from -0.125 to 0.125
- leaf_to_root: float32 [4, 8192, 2048], P(None, 'rows', 'cols'), may hold values from -0.125 to 0.125
- mid_to_root: float32 [2, 8192, 4096], P(None, 'rows', 'cols'), may hold values from -0.09375 to 0.09375
- mask_leaf_mid: int32 [4, 32, 16], replicated, may hold values 0 or 1
- mask_leaf_root: int32 [4, 64, 16], replicated, may hold values 0 or 1
- mask_mid_root: int32 [2, 64, 32], replicated, may hold values 0 or 1
Outputs:
- solved_leaf: float32 [4, 2048, 128], P(None, 'rows')
- solved_mid: float32 [2, 4096, 128], P(None, 'rows')
- solved_root: float32 [8192, 128], P('rows')
Inputs may be any that keep to these rules, and one draw needn't show every extreme that they name: `inverse_leaf`: lower triangular, with its diagonal between 0.5 and 2. `inverse_mid`: lower triangular, with its diagonal between 0.5 and 2. `inverse_root`: lower triangular, with its diagonal between 0.5 and 2.
All inputs are finite; a program needn't handle non-finite values.
Results may differ from a plain program's by a relative error of at most 0.00014.
Values sent between devices are 32-bit elements; how exact they have to be, the bound alone decides.
No kernel may reach another device: no remote copies, remote signals or barrier semaphores. Data moves between devices by JAX's collectives and lax.ppermute only.
A program may use at most 128 MiB of HBM per device.

v0:
```python
import jax
import jax.numpy as jnp
from jax import lax
from jax.sharding import PartitionSpec as P

TILE = 128


def product(matrix, vector):
    return jnp.einsum(
        "src,sck->srk",
        matrix,
        vector,
        precision=lax.Precision.HIGHEST,
        preferred_element_type=jnp.float32,
    )


def own_columns(gathered):
    col_width = gathered.shape[1] // lax.axis_size("cols")
    return lax.dynamic_slice_in_dim(gathered, lax.axis_index("cols") * col_width, col_width, 1)


def masked(values, pattern):
    rows_dev = values.shape[1]
    cols_dev = values.shape[2]
    row_ids = lax.axis_index("rows") * rows_dev + lax.iota(jnp.int32, rows_dev)
    col_ids = lax.axis_index("cols") * cols_dev + lax.iota(jnp.int32, cols_dev)
    row_hot = (row_ids[:, None] // TILE == lax.iota(jnp.int32, pattern.shape[1])[None, :]).astype(
        jnp.float32
    )
    col_hot = (col_ids[:, None] // TILE == lax.iota(jnp.int32, pattern.shape[2])[None, :]).astype(
        jnp.float32
    )
    expanded = jnp.einsum("ra,sab,cb->src", row_hot, pattern.astype(jnp.float32), col_hot)
    return values * expanded


def fetch_columns(block):
    gathered = lax.all_gather(block, "rows", axis=1, tiled=True)
    return own_columns(gathered)


def solve_block(residual, inverse, spread_needed):
    partial_value = product(inverse, fetch_columns(residual))
    solved = lax.psum(partial_value, "cols")
    spread = fetch_columns(solved) if spread_needed else solved
    return (solved, spread)


def body(
    right_leaf,
    right_mid,
    right_root,
    inverse_leaf,
    inverse_mid,
    inverse_root,
    leaf_to_mid,
    leaf_to_root,
    mid_to_root,
    mask_leaf_mid,
    mask_leaf_root,
    mask_mid_root,
):
    factor_lm = masked(leaf_to_mid, mask_leaf_mid)
    factor_lr = masked(leaf_to_root, mask_leaf_root)
    factor_mr = masked(mid_to_root, mask_mid_root)
    solved_leaf, leaf_columns = solve_block(right_leaf, inverse_leaf, True)
    mid_terms = product(factor_lm, leaf_columns)
    mid_part = mid_terms.reshape(2, 2, mid_terms.shape[1], mid_terms.shape[2]).sum(axis=1)
    root_part = product(factor_lr, leaf_columns).sum(axis=0)[None]
    mid_summed, root_summed = lax.psum((mid_part, root_part), "cols")
    resid_mid = right_mid - mid_summed
    solved_mid, mid_columns = solve_block(resid_mid, inverse_mid, True)
    root_more = product(factor_mr, mid_columns).sum(axis=0)[None]
    resid_root = right_root[None] - root_summed - lax.psum(root_more, "cols")
    solved_root, unused_spread = solve_block(resid_root, inverse_root[None], False)
    return (solved_leaf, solved_mid, solved_root[0])


def solution(mesh):
    placed = (
        P(None, "rows", None),
        P(None, "rows", None),
        P("rows", None),
        P(None, "rows", "cols"),
        P(None, "rows", "cols"),
        P("rows", "cols"),
        P(None, "rows", "cols"),
        P(None, "rows", "cols"),
        P(None, "rows", "cols"),
        P(),
        P(),
        P(),
    )
    return jax.shard_map(
        body,
        mesh=mesh,
        in_specs=placed,
        out_specs=(P(None, "rows", None), P(None, "rows", None), P("rows", None)),
        check_vma=False,
    )
```

profile of v0, /device:TPU:0, one launch (start us, length us, event | category | flops | bytes accessed | tf_op | source)
XLA Modules:
  0.0 608.7 jit_solution(15092546820964897420)
XLA Ops:
  7.2 2.2 copy.32
  9.4 0.0 all-reduce.7.cloned.1.call-start
  9.5 78.9 %all-gather.6.cloned.1.call-done = f32[4,2048,128]{1,2,0:T(8,128)} async-done(((f32[4,256,128]{1,2,0:T(8,128)}), f32[4,2048,128]{1,2,0:T(8,128)}) %all-gather.6.cloned.1.call-update) | async-done | bytes 4194320 | tf_op jit(solution)/shard_map/all_gather | solution.py:40
  88.4 4.2 convolution_bitcast_fusion.1
  92.7 31.4 %all-reduce.7.cloned.1.call-done = f32[4,256,128]{1,2,0:T(8,128)} async-done(((f32[4,256,128]{1,2,0:T(8,128)}), f32[4,256,128]{1,2,0:T(8,128)}) %all-reduce.7.cloned.1.call-update) | async-done | bytes 524304 | tf_op jit(solution)/shard_map/psum | solution.py:46
  124.3 0.2 fusion.32
  124.4 2.7 fusion.37
  127.1 74.1 %all-gather.8.cloned.1.call-done = f32[4,2048,128]{1,2,0:T(8,128)} async-done(((f32[4,256,128]{1,2,0:T(8,128)}), f32[4,2048,128]{1,2,0:T(8,128)}) %all-gather.8.cloned.1.call-update) | async-done | bytes 4194320 | tf_op jit(solution)/shard_map/all_gather | solution.py:40
  201.2 7.5 %bitcast_reduce_fusion = f32[2,512,128]{2,1,0:T(8,128)S(1)} fusion(f32[4,2048,128]{1,2,0:T(8,128)} %all-gather.8.cloned.1.call-done, s32[]{:T(128)S(6)} %select_n.49, f32[4,512,512]{2,1,0:T(8,128)} %param.18, f32[4,512,512]{2,1,0:T(8,128)} %fusion.37), kind=kOutput, calls=%fused_computation.12 | convolution fusion | flops 1611792384 | bytes 9961476 | tf_op jit(solution)/shard_map/src,sck->srk/dot_general | solution.py:10
  208.7 1.0 copy.34
  209.8 0.2 copy.35
  210.0 31.2 %all-reduce.9.cloned.1.call-done = f32[2,512,128]{1,2,0:T(8,128)} async-done(((f32[2,512,128]{1,2,0:T(8,128)}), f32[2,512,128]{1,2,0:T(8,128)}) %all-reduce.9.cloned.1.call-update) | async-done | bytes 524304 | tf_op jit(solution)/shard_map/psum | solution.py:72
  241.3 1.9 sub.35
  243.3 74.0 %all-gather.10.cloned.1.call-done = f32[2,4096,128]{1,2,0:T(8,128)} async-done(((f32[2,512,128]{1,2,0:T(8,128)}), f32[2,4096,128]{1,2,0:T(8,128)}) %all-gather.10.cloned.1.call-update) | async-done | bytes 4194320 | tf_op jit(solution)/shard_map/all_gather | solution.py:40
  317.3 7.7 %convolution_bitcast_fusion.2 = f32[2,512,128]{1,2,0:T(8,128)} fusion(f32[2,512,1024]{2,1,0:T(8,128)} %param.16, f32[2,4096,128]{1,2,0:T(8,128)} %all-gather.10.cloned.1.call-done, s32[]{:T(128)S(6)} %select_n.52), kind=kOutput, calls=%fused_computation.10 | convolution fusion | flops 1610612736 | bytes 5767172 | tf_op jit(solution)/shard_map/src,sck->srk/dot_general | solution.py:10
  325.0 31.5 %all-reduce.11.cloned.1.call-done = f32[2,512,128]{1,2,0:T(8,128)} async-done(((f32[2,512,128]{1,2,0:T(8,128)}), f32[2,512,128]{1,2,0:T(8,128)}) %all-reduce.11.cloned.1.call-update) | async-done | bytes 524304 | tf_op jit(solution)/shard_map/psum | solution.py:46
  356.6 0.2 all-reduce.15.cloned.1.call-start
  356.9 0.2 fusion.24
  357.1 0.2 fusion.25
  357.3 1.3 fusion.35
  358.6 4.5 fusion.29
  363.1 8.7 %fusion.6 = f32[1,1024,128]{2,1,0:T(8,128)} fusion(f32[4,1024,512]{2,1,0:T(8,128)S(1)} %bitcast.56, f32[4,1024,512]{2,1,0:T(8,128)S(1)} %fusion.35, f32[4,2048,128]{1,2,0:T(8,128)} %all-gather.8.cloned.1.call-done, s32[]{:T(128)S(6)} %select_n.49), kind=kOutput, calls=%fused_computation.6 | convolution fusion | flops 3223322624 | bytes 18350084 | tf_op jit(solution)/shard_map/src,sck->srk/dot_general | solution.py:10
  371.9 60.3 %all-gather.12.cloned.1.call-done = f32[2,4096,128]{1,2,0:T(8,128)} async-done(((f32[2,512,128]{1,2,0:T(8,128)}), f32[2,4096,128]{1,2,0:T(8,128)}) %all-gather.12.cloned.1.call-update) | async-done | bytes 4194320 | tf_op jit(solution)/shard_map/all_gather | solution.py:40
  432.2 11.2 %fusion.9 = f32[1,1024,128]{2,1,0:T(8,128)} fusion(f32[2,1024,1024]{2,1,0:T(8,128)} %param.20, f32[2,1024,1024]{2,1,0:T(8,128)} %fusion.29, f32[2,4096,128]{1,2,0:T(8,128)} %all-gather.12.cloned.1.call-done, s32[]{:T(128)S(6)} %select_n.52), kind=kOutput, calls=%fused_computation.7 | convolution fusion | flops 3223322624 | bytes 18350084 | tf_op jit(solution)/shard_map/src,sck->srk/dot_general | solution.py:10
  443.5 34.5 %all-reduce.15.cloned.1.call-done = (f32[1,1024,128]{2,1,0:T(8,128)}, f32[1,1024,128]{2,1,0:T(8,128)}) async-done(((f32[1,1024,128]{2,1,0:T(8,128)}, f32[1,1024,128]{2,1,0:T(8,128)}), (f32[1,1024,128]{2,1,0:T(8,128)}, f32[1,1024,128]{2,1,0:T(8,128)})) %all-reduce.15.cloned.1.call-update) | async-done | bytes 1048592 | tf_op jit(solution)/shard_map/psum | solution.py:76
  478.1 2.1 fusion.23
  480.2 74.6 %all-gather.14.cloned.1.call-done = f32[1,8192,128]{2,1,0:T(8,128)} async-done(((f32[1,1024,128]{2,1,0:T(8,128)}), f32[1,8192,128]{2,1,0:T(8,128)}) %all-gather.14.cloned.1.call-update) | async-done | bytes 4194320 | tf_op jit(solution)/shard_map/all_gather | solution.py:40
  554.8 13.4 %convolution_bitcast_fusion = f32[1024,128]{0,1:T(8,128)} fusion(f32[1024,2048]{1,0:T(8,128)} %param.17, f32[1,8192,128]{2,1,0:T(8,128)} %all-gather.14.cloned.1.call-done, s32[]{:T(128)S(6)} %select_n.55), kind=kOutput, calls=%fused_computation.8 | convolution fusion | flops 3221225472 | bytes 9961476 | tf_op jit(solution)/shard_map/src,sck->srk/dot_general | solution.py:10
  568.3 1.0 copy.38
  569.3 1.0 copy.39
  570.3 29.6 %all-reduce.13.cloned.1.call-done = f32[1024,128]{0,1:T(8,128)} async-done(((f32[1024,128]{0,1:T(8,128)}), f32[1024,128]{0,1:T(8,128)}) %all-reduce.13.cloned.1.call-update) | async-done | bytes 524304 | tf_op jit(solution)/shard_map/psum | solution.py:46
  599.9 2.0 copy.40
  (48 shorter events, 0.6 us)
Async XLA Ops:
  7.2 81.2 %copy-start = (f32[4,256,512]{2,1,0:T(8,128)S(1)}, f32[4,256,512]{2,1,0:T(8,128)}, u32[]{:S(2)}) copy-start(f32[4,256,512]{2,1,0:T(8,128)} %param.15) | copy-start | bytes 6291460
  7.2 117.0 %copy-start.6 = (s32[4,32,16]{1,2,0:T(8,128)S(1)}, s32[4,32,16]{1,2,0:T(8,128)}, u32[]{:S(2)}) copy-start(s32[4,32,16]{1,2,0:T(8,128)} %param.21) | copy-start | bytes 24580
  7.2 81.2 %all-gather.6.cloned.1.call-start = ((), (), s32[]{:S(2)}) async-start(), calls=%async_computation | async-start | bytes 4718592 | tf_op jit(solution)/shard_map/all_gather | solution.py:40
  9.4 114.7 %all-reduce.7.cloned.1.call-start = ((), (), s32[]{:S(2)}) async-start(), calls=%async_computation.1 | async-start | bytes 1048576 | tf_op jit(solution)/shard_map/psum | solution.py:46
  92.6 108.6 %all-gather.8.cloned.1.call-start = ((), (), s32[]{:S(2)}) async-start(), calls=%async_computation.2 | async-start | bytes 4718592 | tf_op jit(solution)/shard_map/all_gather | solution.py:40
  124.1 117.1 %all-reduce.9.cloned.1.call-start = ((), (), s32[]{:S(2)}) async-start(), calls=%async_computation.3 | async-start | bytes 1048576 | tf_op jit(solution)/shard_map/psum | solution.py:72
  127.1 82.7 %copy-start.4 = (f32[2,512,128]{2,1,0:T(8,128)S(1)}, f32[2,512,128]{2,1,0:T(8,128)}, u32[]{:S(2)}) copy-start(f32[2,512,128]{2,1,0:T(8,128)} %param.13) | copy-start | bytes 1572868
  209.7 107.5 %all-gather.10.cloned.1.call-start = ((), (), s32[]{:S(2)}) async-start(), calls=%async_computation.4 | async-start | bytes 4718592 | tf_op jit(solution)/shard_map/all_gather | solution.py:40
  210.0 146.8 %copy-start.7 = (s32[2,64,32]{1,2,0:T(8,128)S(1)}, s32[2,64,32]{1,2,0:T(8,128)}, u32[]{:S(2)}) copy-start(s32[2,64,32]{1,2,0:T(8,128)} %param.23) | copy-start | bytes 49156
  210.0 146.8 %copy-start.8 = (s32[4,64,16]{1,2,0:T(8,128)S(1)}, s32[4,64,16]{1,2,0:T(8,128)}, u32[]{:S(2)}) copy-start(s32[4,64,16]{1,2,0:T(8,128)} %param.22) | copy-start | bytes 49156
  243.2 113.4 %all-reduce.11.cloned.1.call-start = ((), (), s32[]{:S(2)}) async-start(), calls=%async_computation.5 | async-start | bytes 1048576 | tf_op jit(solution)/shard_map/psum | solution.py:46
  325.0 107.2 %all-gather.12.cloned.1.call-start = ((), (), s32[]{:S(2)}) async-start(), calls=%async_computation.6 | async-start | bytes 4718592 | tf_op jit(solution)/shard_map/all_gather | solution.py:40
  356.6 121.5 %all-reduce.15.cloned.1.call-start = ((), (), s32[]{:S(2)}) async-start(), calls=%async_computation.9 | async-start | bytes 2097152 | tf_op jit(solution)/shard_map/psum | solution.py:76
  357.3 5.8 slice-start
  358.6 4.6 slice-start.1
  371.9 106.2 %copy-start.5 = (f32[1024,128]{1,0:T(8,128)S(1)}, f32[1024,128]{1,0:T(8,128)}, u32[]{:S(2)}) copy-start(f32[1024,128]{1,0:T(8,128)} %param.14) | copy-start | bytes 1572868
  443.5 111.4 %all-gather.14.cloned.1.call-start = ((), (), s32[]{:S(2)}) async-start(), calls=%async_computation.7 | async-start | bytes 4718592 | tf_op jit(solution)/shard_map/all_gather | solution.py:40
  480.2 119.7 %all-reduce.13.cloned.1.call-start = ((), (), s32[]{:S(2)}) async-start(), calls=%async_computation.8 | async-start | bytes 1048576 | tf_op jit(solution)/shard_map/psum | solution.py:46
  480.2 88.1 %copy-start.2 = (f32[4,256,128]{1,2,0:T(8,128)S(1)}, f32[4,256,128]{1,2,0:T(8,128)}, u32[]{:S(2)}) copy-start(f32[4,256,128]{1,2,0:T(8,128)} %all-reduce.7.cloned.1.call-done) | copy-start | bytes 1572868
  480.2 89.1 %copy-start.3 = (f32[2,512,128]{1,2,0:T(8,128)S(1)}, f32[2,512,128]{1,2,0:T(8,128)}, u32[]{:S(2)}) copy-start(f32[2,512,128]{1,2,0:T(8,128)} %all-reduce.11.cloned.1.call-done) | copy-start | bytes 1572868
  554.8 47.1 %copy-start.1 = (f32[4,256,512]{2,1,0:T(8,128)S(1)}, f32[4,256,512]{2,1,0:T(8,128)}, u32[]{:S(2)}) copy-start(f32[4,256,512]{2,1,0:T(8,128)} %param.15) | copy-start | bytes 6291460
Sparse Core Ops, SparseCore 0:
  10.6 77.7 all-gather.5
  92.8 31.3 all-reduce.6
  126.2 75.0 all-gather.7
  209.9 31.3 all-reduce.8
  243.9 73.3 all-gather.9
  325.1 31.4 all-reduce.10
  358.8 73.3 all-gather.11
  443.6 34.4 all-reduce.14
  481.0 73.8 all-gather.13
  568.4 31.4 all-reduce.12
where the time goes:
time: 609 us
  waiting for transfers between devices  520 us (85%)
  matrix products  61.8 us (10%)
  between operations  14.4 us (2%)
  local copies, waits for them, and re-layouts  7.45 us (1%)
    all_gather x5, waiting for transfers between devices, fetch_columns(): gathered = lax.all_gather(block, 'rows', axis=1, tiled=True)  362 us
    psum x3, waiting for transfers between devices, solve_block(): solved = lax.psum(partial_value, 'cols')  92.6 us
    dot_general x6, matrix products, product(): jnp.einsum('src,sck->srk', matrix, vector, precision=lax.Precision.HIGHES...  52.8 us
    psum x1, waiting for transfers between devices, body(): resid_root = right_root[None] - root_summed - lax.psum(root_more, 'cols')  34.5 us
    psum x1, waiting for transfers between devices, body(): mid_summed, root_summed = lax.psum((mid_part, root_part), 'cols')  31.2 us
  transfers between devices with their start and end apart: 10, of which 10 were waited for; matrix products, arithmetic and copies ran while one was open for 3% of the time, Pallas kernels for 0%

commit v1 on v0

v1 whole, which is shorter than its diff:
```python
import functools

import jax
import jax.numpy as jnp
from jax import lax
from jax.experimental import pallas as pl
from jax.experimental.pallas import tpu as pltpu
from jax.sharding import PartitionSpec as P

TILE = 128
AXES = ("rows", "cols")
BF16 = jnp.bfloat16
F32 = jnp.float32


def product(matrix, vector):
    return jnp.einsum(
        "src,sck->srk",
        matrix,
        vector,
        precision=lax.Precision.HIGHEST,
        preferred_element_type=jnp.float32,
    )


def masked(values, pattern):
    rows_dev = values.shape[1]
    cols_dev = values.shape[2]
    row_ids = lax.axis_index("rows") * rows_dev + lax.iota(jnp.int32, rows_dev)
    col_ids = lax.axis_index("cols") * cols_dev + lax.iota(jnp.int32, cols_dev)
    row_hot = (row_ids[:, None] // TILE == lax.iota(jnp.int32, pattern.shape[1])[None, :]).astype(F32)
    col_hot = (col_ids[:, None] // TILE == lax.iota(jnp.int32, pattern.shape[2])[None, :]).astype(F32)
    return values * jnp.einsum("ra,sab,cb->src", row_hot, pattern.astype(F32), col_hot)


def fetch_columns(block):
    gathered = lax.all_gather(block, "rows", axis=1, tiled=True)
    col_width = gathered.shape[1] // lax.axis_size("cols")
    return lax.dynamic_slice_in_dim(gathered, lax.axis_index("cols") * col_width, col_width, 1)


def general_body(
    right_leaf,
    right_mid,
    right_root,
    inverse_leaf,
    inverse_mid,
    inverse_root,
    leaf_to_mid,
    leaf_to_root,
    mid_to_root,
    mask_leaf_mid,
    mask_leaf_root,
    mask_mid_root,
):
    factor_lm = masked(leaf_to_mid, mask_leaf_mid)
    factor_lr = masked(leaf_to_root, mask_leaf_root)
    factor_mr = masked(mid_to_root, mask_mid_root)
    solved_leaf = lax.psum(product(inverse_leaf, fetch_columns(right_leaf)), "cols")
    leaf_columns = fetch_columns(solved_leaf)
    terms = product(factor_lm, leaf_columns)
    mid_part = terms.reshape(2, 2, terms.shape[1], terms.shape[2]).sum(axis=1)
    resid_mid = right_mid - lax.psum(mid_part, "cols")
    solved_mid = lax.psum(product(inverse_mid, fetch_columns(resid_mid)), "cols")
    mid_columns = fetch_columns(solved_mid)
    root_part = product(factor_lr, leaf_columns).sum(axis=0) + product(factor_mr, mid_columns).sum(axis=0)
    resid_root = right_root - lax.psum(root_part, "cols")
    solved_root = lax.psum(product(inverse_root[None], fetch_columns(resid_root[None])), "cols")
    return (solved_leaf, solved_mid, solved_root[0])


PIECE = 256


def flat(x, y, z, k):
    return (2 * z + y) * 4 + 2 * x + k


PLACES = [(x, y, z, k) for x in (0, 1) for y in (0, 1) for z in range(4) for k in (0, 1)]
TO_CORE = [(flat(x, y, z, k), flat(x, y, z, 1 - k)) for x, y, z, k in PLACES]
TO_X = [(flat(x, y, z, k), flat(1 - x, y, z, k)) for x, y, z, k in PLACES]
TO_Y = [(flat(x, y, z, k), flat(x, 1 - y, z, k)) for x, y, z, k in PLACES]
TO_Z = [(flat(x, y, z, k), flat(x, y, z ^ 1, k)) for x, y, z, k in PLACES]
TO_YZ = [(flat(x, y, z, k), flat(x, 1 - y, z ^ 1, k)) for x, y, z, k in PLACES]
TO_FAR = [(flat(x, y, z, k), flat(x, y, z ^ 2, k)) for x, y, z, k in PLACES if z // 2 == x]


def send(value, pairs):
    return lax.ppermute(value, AXES, pairs)


def place():
    r, c = lax.axis_index("rows"), lax.axis_index("cols")
    return c // 2, r % 2, r // 2, c % 2


def halve(part):
    k = place()[3]
    other = send(part, TO_CORE)
    mine = lax.dynamic_index_in_dim(part, k, 0, False) + lax.dynamic_index_in_dim(other, k, 0, False)
    return mine, send(mine, TO_X)


def both_halves(mine):
    k = place()[3]
    other = send(mine, TO_CORE)
    first = k == 0
    return jnp.stack([jnp.where(first, mine, other), jnp.where(first, other, mine)])


def spread(mine):
    x, y, z, k = place()
    far = send(mine, TO_FAR)
    own = jnp.where(z // 2 == x, mine, far)
    beside, above, across = send(own, TO_Y), send(own, TO_Z), send(own, TO_YZ)
    same = (z % 2) == k
    swapped = send(jnp.stack([jnp.where(same, above, own), jnp.where(same, across, beside)]), TO_CORE)
    return own, beside, above, across, swapped


def split(value):
    high = value.astype(BF16)
    return high, (value - high.astype(F32)).astype(BF16)


def kernel_body(spans, has_mask, has_add, separate, leafwise, *refs):
    own, beside, above, across, swapped = refs[:5]
    refs = refs[5:]
    count = len(spans)
    mats, refs = refs[:count], refs[count:]
    if has_mask:
        mask, refs = refs[0], refs[1:]
    if has_add:
        add, refs = refs[0], refs[1:]
    out, held = refs
    step = pl.program_id(0)
    n = out.shape[-1]

    @pl.when(step == 0)
    def _():
        r, c = lax.axis_index("rows"), lax.axis_index("cols")
        y, k = lax.rem(r, 2), lax.rem(c, 2)
        same = lax.rem(r // 2, 2) == k

        def put(value, y_of, half):
            row = half * (2 * PIECE) + y_of * PIECE if leafwise else y_of * (2 * PIECE) + half * PIECE
            row = pl.multiple_of(row, PIECE)
            high, low = split(value)
            held[pl.ds(row, PIECE), :n] = high
            held[pl.ds(row, PIECE), n:] = low

        @pl.when(same)
        def _():
            put(own[...], y, k)
            put(beside[...], 1 - y, k)

        @pl.when(jnp.logical_not(same))
        def _():
            put(above[...], y, k)
            put(across[...], 1 - y, k)

        put(swapped[0], y, 1 - k)
        put(swapped[1], 1 - y, 1 - k)

    total = None
    for t, (start, width) in enumerate(spans):
        leaf = t if len(mats) == 1 or mats[t].ndim == 3 else 0
        a = mats[t][0] if mats[t].ndim == 3 else mats[t][...]
        if has_mask:
            rows = a.shape[0] // TILE
            a = jnp.concatenate(
                [a[q * TILE : (q + 1) * TILE] * mask[t, pl.ds(step * rows + q, 1), :] for q in range(rows)], axis=0
            )
        high, low = split(a)
        x = held[start : start + width, :]
        wide = jnp.dot(high, x, preferred_element_type=F32)
        value = jnp.dot(low, x[:, :n], preferred_element_type=F32) + wide[:, n:] + wide[:, :n]
        if separate:
            out[t] = value
        else:
            total = value if total is None else total + value
    if not separate:
        if has_add:
            total = total + add[...]
        out[...] = total


def apply(pieces, terms, rows, row_tile, first_tile=0, mask=None, add=None, separate=False, leafwise=False):
    n = pieces[0].shape[-1]
    steps = rows // row_tile
    full = lambda a: pl.BlockSpec(a.shape, lambda i, d=a.ndim: (0,) * d)
    operands = list(pieces)
    specs = [full(a) for a in pieces]
    for array, block, index, _, _ in terms:
        operands.append(array)
        specs.append(pl.BlockSpec(block, lambda i, index=index: index(i + first_tile)))
    if mask is not None:
        operands.append(mask)
        specs.append(full(mask))
    if add is not None:
        operands.append(add)
        specs.append(pl.BlockSpec((row_tile, n), lambda i: (i + first_tile, 0)))
    if separate:
        shape = (len(terms), rows, n)
        out_spec = pl.BlockSpec((len(terms), row_tile, n), lambda i: (0, i, 0))
    else:
        shape = (rows, n)
        out_spec = pl.BlockSpec((row_tile, n), lambda i: (i, 0))
    work = sum(rows * t[4] for t in terms)
    return pl.pallas_call(
        functools.partial(
            kernel_body, tuple((t[3], t[4]) for t in terms), mask is not None, add is not None, separate, leafwise
        ),
        out_shape=jax.ShapeDtypeStruct(shape, F32),
        grid_spec=pltpu.PrefetchScalarGridSpec(
            num_scalar_prefetch=0,
            grid=(steps,),
            in_specs=specs,
            out_specs=out_spec,
            scratch_shapes=[pltpu.VMEM((4 * PIECE, 2 * n), BF16)],
        ),
        compiler_params=pltpu.CompilerParams(vmem_limit_bytes=32 << 20),
        cost_estimate=pl.CostEstimate(flops=8 * work * n, bytes_accessed=4 * work, transcendentals=0),
    )(*operands)


def own_mask(pattern, rows, cols):
    r, c = lax.axis_index("rows"), lax.axis_index("cols")
    tr, tc = rows // TILE, cols // TILE
    part = lax.dynamic_slice(pattern, (0, r * tr, c * tc), (pattern.shape[0], tr, tc))
    return jnp.repeat(part.astype(F32), TILE, axis=2)


def grid_body(
    right_leaf,
    right_mid,
    right_root,
    inverse_leaf,
    inverse_mid,
    inverse_root,
    leaf_to_mid,
    leaf_to_root,
    mid_to_root,
    mask_leaf_mid,
    mask_leaf_root,
    mask_mid_root,
):
    k = place()[3]
    n = right_root.shape[-1]
    mask_lm = own_mask(mask_leaf_mid, *leaf_to_mid.shape[1:])
    mask_lr = own_mask(mask_leaf_root, *leaf_to_root.shape[1:])
    mask_mr = own_mask(mask_mid_root, *mid_to_root.shape[1:])
    pair = lambda a, tile, s: [
        (a, (1, tile, a.shape[2]), lambda i, l=l: (2 * s + l, i, 0), 2 * PIECE * l, a.shape[2]) for l in (0, 1)
    ]
    one = lambda a, tile, s: [(a, (1, tile, a.shape[2]), lambda i: (s, i, 0), 0, a.shape[2])]

    streams = (0, 1)
    first = [spread(lax.dynamic_index_in_dim(right_leaf, 2 * s + k, 0, False)) for s in streams]
    leaf_half, leaf_pieces = [], []
    for s in streams:
        part = apply(first[s], pair(inverse_leaf, 128, s), 256, 128, separate=True, leafwise=True)
        mine, other = halve(part)
        leaf_half.append(mine + other)
    leaf_pieces = [spread(h) for h in leaf_half]
    solved_leaf = [both_halves(h) for h in leaf_half]

    mid_half = []
    for s in streams:
        part = apply(
            leaf_pieces[s], pair(leaf_to_mid, 256, s), 512, 256, mask=mask_lm[2 * s : 2 * s + 2], leafwise=True
        )
        mine, other = halve(part.reshape(2, PIECE, n))
        right = lax.dynamic_index_in_dim(right_mid[s].reshape(2, PIECE, n), k, 0, False)
        mid_half.append(right - (mine + other))
    resid_pieces = [spread(h) for h in mid_half]

    root_part = None
    for s in streams:
        root_part = apply(
            leaf_pieces[s],
            pair(leaf_to_root, 256, s),
            1024,
            256,
            mask=mask_lr[2 * s : 2 * s + 2],
            add=root_part,
            leafwise=True,
        )

    solved_half = []
    for s in streams:
        part = apply(resid_pieces[s], one(inverse_mid, 256, s), 512, 256)
        mine, other = halve(part.reshape(2, PIECE, n))
        solved_half.append(mine + other)
    mid_pieces = [spread(h) for h in solved_half]
    solved_mid = [both_halves(h) for h in solved_half]

    root_part = apply(
        mid_pieces[0], one(mid_to_root, 256, 0), 1024, 256, mask=mask_mr[0:1], add=root_part
    )
    root_half = []
    for g in (0, 1):
        part = apply(
            mid_pieces[1],
            one(mid_to_root, 256, 1),
            512,
            256,
            first_tile=2 * g,
            mask=mask_mr[1:2, 4 * g : 4 * g + 4],
            add=root_part,
        )
        mine, other = halve(part.reshape(2, PIECE, n))
        right = lax.dynamic_index_in_dim(right_root.reshape(4, PIECE, n), 2 * g + k, 0, False)
        root_half.append(right - (mine + other))
    root_pieces = [spread(h) for h in root_half]

    columns = lambda g: [
        (inverse_root, (256, 512), lambda i, b=b: (i, 2 * b + g), 2 * PIECE * b, 2 * PIECE) for b in (0, 1)
    ]
    part = apply(root_pieces[0], columns(0), 1024, 256)
    solved_root = []
    for g in (0, 1):
        final = apply(root_pieces[1], columns(1), 512, 256, first_tile=2 * g, add=part)
        mine, other = halve(final.reshape(2, PIECE, n))
        solved_root.append(both_halves(mine + other))
    return (
        jnp.concatenate(solved_leaf, axis=0),
        jnp.stack([h.reshape(2 * PIECE, n) for h in solved_mid]),
        jnp.concatenate([h.reshape(2 * PIECE, n) for h in solved_root], axis=0),
    )


def body(*args):
    if lax.axis_size("rows") == 8 and lax.axis_size("cols") == 4 and args[0].shape == (4, PIECE, TILE):
        return grid_body(*args)
    return general_body(*args)


def solution(mesh):
    placed = (
        P(None, "rows", None),
        P(None, "rows", None),
        P("rows", None),
        P(None, "rows", "cols"),
        P(None, "rows", "cols"),
        P("rows", "cols"),
        P(None, "rows", "cols"),
        P(None, "rows", "cols"),
        P(None, "rows", "cols"),
        P(),
        P(),
        P(),
    )
    return jax.shard_map(
        body,
        mesh=mesh,
        in_specs=placed,
        out_specs=(P(None, "rows", None), P(None, "rows", None), P("rows", None)),
        check_vma=False,
    )
```

time: 609 us -> 214 us (0.35)
  waiting for transfers between devices: 520 us -> 66.3 us
  starting transfers between devices: 0.59 us -> 118 us
  matrix products: 61.8 us -> 0 us
  Pallas kernels: 0 us -> 17.9 us
  between operations: 14.4 us -> 1.8 us
    all_gather x5 -> x0, waiting for transfers between devices: 362 us -> none  [fetch_columns(): gathered = lax.all_gather(block, 'rows', axis=1, tiled=True)]
    psum x5 -> x0, waiting for transfers between devices: 158 us -> none  [the longest x3 92.6 us: solve_block(): solved = lax.psum(partial_value, 'cols')]
    ppermute x0 -> x76, starting transfers between devices: none -> 118 us  [send(): return lax.ppermute(value, AXES, pairs)]
    ppermute x0 -> x76, waiting for transfers between devices: none -> 66.3 us  [send(): return lax.ppermute(value, AXES, pairs)]
    dot_general x9 -> x0, matrix products: 61.3 us -> none  [the longest x6 52.8 us: product(): jnp.einsum('src,sck->srk', matrix, vector, precision=lax.Precision.HIGHES...]
    pallas_call x0 -> x14, Pallas kernels: none -> 17.9 us  [apply(): pl.pallas_call(functools.partial(kernel_body, tuple(((t[3], t[4]) for t i...]
  transfers between devices with their start and end apart: 10 -> 76, of which waited for: 10 -> 30; matrix products, arithmetic and copies ran while one was open for 3% -> 3% of each run, Pallas kernels for 0% -> 7%
where the time goes in v1:
time: 214 us
  starting transfers between devices  118 us (55%)
  waiting for transfers between devices  66.3 us (31%)
  Pallas kernels  17.9 us (8%)
  other arithmetic  5.26 us (2%)
  local copies, waits for them, and re-layouts  4.09 us (2%)
    ppermute x76, starting transfers between devices, send(): return lax.ppermute(value, AXES, pairs)  118 us
    ppermute x76, waiting for transfers between devices, send(): return lax.ppermute(value, AXES, pairs)  66.3 us
    pallas_call x14, Pallas kernels, apply(): pl.pallas_call(functools.partial(kernel_body, tuple(((t[3], t[4]) for t i...  17.9 us
  transfers between devices with their start and end apart: 76, of which 30 were waited for; matrix products, arithmetic and copies ran while one was open for 3% of the time, Pallas kernels for 7%

profile of v1, /device:TPU:0, one launch (start us, length us, event | category | flops | bytes accessed | tf_op | source)
XLA Modules:
  0.0 213.6 jit_solution(4978905711381207792)
XLA Ops:
  1.9 5.9 %collective-permute-start = (f32[256,128]{1,0:T(8,128)S(1)}, f32[256,128]{1,0:T(8,128)S(1)}, u32[]{:S(2)}, u32[]{:S(2)}) collective-permute-start(f32[256,128]{1,0:T(8,128)S(1)} %get-tuple-element.7), channel_id=1, source_target_pairs={{0,16},{1,17},{8,24},{9,25},{4,20},{5,21},{12,28},{13,29},{18,2},{... | collective-permute-start | bytes 393224 | tf_op jit(solution)/shard_map/ppermute | solution.py:89
  11.7 7.0 %collective-permute-start.3 = (f32[256,128]{1,0:T(8,128)S(1)}, f32[256,128]{1,0:T(8,128)S(1)}, u32[]{:S(2)}, u32[]{:S(2)}) collective-permute-start(f32[256,128]{1,0:T(8,128)S(1)} %broadcast_select_fusion.9.refs_0_), channel_id=1, source_target_pairs={{0,12},{1,13},{8,4},{9,5},{16,28},{17,29},{24,20},{25,21},{4,8},{5... | collective-permute-start | bytes 393224 | tf_op jit(solution)/shard_map/ppermute | solution.py:89
  19.4 2.9 %collective-permute-start.11 = (f32[256,128]{1,0:T(8,128)S(1)}, f32[256,128]{1,0:T(8,128)S(1)}, u32[]{:S(2)}, u32[]{:S(2)}) collective-permute-start(f32[256,128]{1,0:T(8,128)S(1)} %broadcast_select_fusion.8.refs_0_), channel_id=1, source_target_pairs={{0,12},{1,13},{8,4},{9,5},{16,28},{17,29},{24,20},{25,21},{4,8},{5... | collective-permute-start | bytes 393224 | tf_op jit(solution)/shard_map/ppermute | solution.py:89
  22.3 3.1 %collective-permute-done.2.refs_2_ = f32[256,128]{1,0:T(8,128)S(1)} collective-permute-done((f32[256,128]{1,0:T(8,128)S(1)}, f32[256,128]{1,0:T(8,128)S(1)}, u32[]{:S(2)}, u32[]{:S(2)}) %collective-permute-start.2) | collective-permute-done | bytes 131104 | tf_op jit(solution)/shard_map/ppermute | solution.py:89
  26.6 3.4 %collective-permute-done.10.refs_2_ = f32[256,128]{1,0:T(8,128)S(1)} collective-permute-done((f32[256,128]{1,0:T(8,128)S(1)}, f32[256,128]{1,0:T(8,128)S(1)}, u32[]{:S(2)}, u32[]{:S(2)}) %collective-permute-start.10) | collective-permute-done | bytes 131104 | tf_op jit(solution)/shard_map/ppermute | solution.py:89
  35.0 4.0 %collective-permute-start.6 = (f32[256,128]{1,0:T(8,128)S(1)}, f32[256,128]{1,0:T(8,128)S(1)}, u32[]{:S(2)}, u32[]{:S(2)}) collective-permute-start(f32[256,128]{1,0:T(8,128)S(1)} %add_bitcast_fusion.9), channel_id=1, source_target_pairs={{0,2},{1,3},{8,10},{9,11},{16,18},{17,19},{24,26},{25,27},{4,6},{5... | collective-permute-start | bytes 393224 | tf_op jit(solution)/shard_map/ppermute | solution.py:89
  40.2 3.0 %collective-permute-done.6 = f32[256,128]{1,0:T(8,128)S(1)} collective-permute-done((f32[256,128]{1,0:T(8,128)S(1)}, f32[256,128]{1,0:T(8,128)S(1)}, u32[]{:S(2)}, u32[]{:S(2)}) %collective-permute-start.6) | collective-permute-done | bytes 131104 | tf_op jit(solution)/shard_map/ppermute | solution.py:89
  43.3 3.4 %collective-permute-start.16 = (f32[256,128]{1,0:T(8,128)S(1)}, f32[256,128]{1,0:T(8,128)S(1)}, u32[]{:S(2)}, u32[]{:S(2)}) collective-permute-start(f32[256,128]{1,0:T(8,128)S(1)} %add.193), channel_id=1, source_target_pairs={{0,16},{1,17},{8,24},{9,25},{4,20},{5,21},{12,28},{13,29},{18,2},{... | collective-permute-start | bytes 393224 | tf_op jit(solution)/shard_map/ppermute | solution.py:89
  49.3 7.2 %collective-permute-start.18 = (f32[256,128]{1,0:T(8,128)S(1)}, f32[256,128]{1,0:T(8,128)S(1)}, u32[]{:S(2)}, u32[]{:S(2)}) collective-permute-start(f32[256,128]{1,0:T(8,128)S(1)} %get-tuple-element.23.refs_0_), channel_id=1, source_target_pairs={{0,8},{1,9},{8,0},{9,1},{16,24},{17,25},{24,16},{25,17},{4,12},{5,... | collective-permute-start | bytes 393224 | tf_op jit(solution)/shard_map/ppermute | solution.py:89
  63.6 4.6 %collective-permute-done.19.refs_3_ = f32[256,128]{1,0:T(8,128)S(1)} collective-permute-done((f32[256,128]{1,0:T(8,128)S(1)}, f32[256,128]{1,0:T(8,128)S(1)}, u32[]{:S(2)}, u32[]{:S(2)}) %collective-permute-start.19) | collective-permute-done | bytes 131104 | tf_op jit(solution)/shard_map/ppermute | solution.py:89
  68.1 2.6 %collective-permute-done.17.refs_1_ = f32[256,128]{1,0:T(8,128)S(1)} collective-permute-done((f32[256,128]{1,0:T(8,128)S(1)}, f32[256,128]{1,0:T(8,128)S(1)}, u32[]{:S(2)}, u32[]{:S(2)}) %collective-permute-start.17) | collective-permute-done | bytes 131104 | tf_op jit(solution)/shard_map/ppermute | solution.py:89
  75.2 4.0 %collective-permute-start.22 = (f32[256,128]{1,0:T(8,128)S(1)}, f32[256,128]{1,0:T(8,128)S(1)}, u32[]{:S(2)}, u32[]{:S(2)}) collective-permute-start(f32[256,128]{1,0:T(8,128)S(1)} %add_bitcast_fusion.7), channel_id=1, source_target_pairs={{0,2},{1,3},{8,10},{9,11},{16,18},{17,19},{24,26},{25,27},{4,6},{5... | collective-permute-start | bytes 393224 | tf_op jit(solution)/shard_map/ppermute | solution.py:89
  80.2 3.1 %collective-permute-done.22 = f32[256,128]{1,0:T(8,128)S(1)} collective-permute-done((f32[256,128]{1,0:T(8,128)S(1)}, f32[256,128]{1,0:T(8,128)S(1)}, u32[]{:S(2)}, u32[]{:S(2)}) %collective-permute-start.22) | collective-permute-done | bytes 131104 | tf_op jit(solution)/shard_map/ppermute | solution.py:89
  83.3 3.5 %collective-permute-start.23 = (f32[256,128]{1,0:T(8,128)S(1)}, f32[256,128]{1,0:T(8,128)S(1)}, u32[]{:S(2)}, u32[]{:S(2)}) collective-permute-start(f32[256,128]{1,0:T(8,128)S(1)} %bitcast_subtract_fusion.3), channel_id=1, source_target_pairs={{0,16},{1,17},{8,24},{9,25},{4,20},{5,21},{12,28},{13,29},{18,2},{... | collective-permute-start | bytes 393224 | tf_op jit(solution)/shard_map/ppermute | solution.py:89
  90.6 6.1 %collective-permute-start.25 = (f32[256,128]{1,0:T(8,128)S(1)}, f32[256,128]{1,0:T(8,128)S(1)}, u32[]{:S(2)}, u32[]{:S(2)}) collective-permute-start(f32[256,128]{1,0:T(8,128)S(1)} %broadcast_select_fusion.6.refs_0_), channel_id=1, source_target_pairs={{0,8},{1,9},{8,0},{9,1},{16,24},{17,25},{24,16},{25,17},{4,12},{5,... | collective-permute-start | bytes 393224 | tf_op jit(solution)/shard_map/ppermute | solution.py:89
  103.3 5.5 %collective-permute-done.26.refs_3_ = f32[256,128]{1,0:T(8,128)S(1)} collective-permute-done((f32[256,128]{1,0:T(8,128)S(1)}, f32[256,128]{1,0:T(8,128)S(1)}, u32[]{:S(2)}, u32[]{:S(2)}) %collective-permute-start.26) | collective-permute-done | bytes 131104 | tf_op jit(solution)/shard_map/ppermute | solution.py:89
  115.1 3.4 %collective-permute-start.29 = (f32[256,128]{1,0:T(8,128)S(1)}, f32[256,128]{1,0:T(8,128)S(1)}, u32[]{:S(2)}, u32[]{:S(2)}) collective-permute-start(f32[256,128]{1,0:T(8,128)S(1)} %add_bitcast_fusion.6), channel_id=1, source_target_pairs={{0,2},{1,3},{8,10},{9,11},{16,18},{17,19},{24,26},{25,27},{4,6},{5... | collective-permute-start | bytes 393224 | tf_op jit(solution)/shard_map/ppermute | solution.py:89
  119.7 3.1 %collective-permute-done.29 = f32[256,128]{1,0:T(8,128)S(1)} collective-permute-done((f32[256,128]{1,0:T(8,128)S(1)}, f32[256,128]{1,0:T(8,128)S(1)}, u32[]{:S(2)}, u32[]{:S(2)}) %collective-permute-start.29) | collective-permute-done | bytes 131104 | tf_op jit(solution)/shard_map/ppermute | solution.py:89
  122.9 4.0 %collective-permute-start.51 = (f32[256,128]{1,0:T(8,128)S(1)}, f32[256,128]{1,0:T(8,128)S(1)}, u32[]{:S(2)}, u32[]{:S(2)}) collective-permute-start(f32[256,128]{1,0:T(8,128)S(1)} %add.205), channel_id=1, source_target_pairs={{0,16},{1,17},{8,24},{9,25},{4,20},{5,21},{12,28},{13,29},{18,2},{... | collective-permute-start | bytes 393224 | tf_op jit(solution)/shard_map/ppermute | solution.py:89
  129.5 7.3 %collective-permute-start.54 = (f32[256,128]{1,0:T(8,128)S(1)}, f32[256,128]{1,0:T(8,128)S(1)}, u32[]{:S(2)}, u32[]{:S(2)}) collective-permute-start(f32[256,128]{1,0:T(8,128)S(1)} %get-tuple-element.21.refs_0_), channel_id=1, source_target_pairs={{0,12},{1,13},{8,4},{9,5},{16,28},{17,29},{24,20},{25,21},{4,8},{5... | collective-permute-start | bytes 393224 | tf_op jit(solution)/shard_map/ppermute | solution.py:89
  140.4 3.2 %collective-permute-done.53.refs_2_ = f32[256,128]{1,0:T(8,128)S(1)} collective-permute-done((f32[256,128]{1,0:T(8,128)S(1)}, f32[256,128]{1,0:T(8,128)S(1)}, u32[]{:S(2)}, u32[]{:S(2)}) %collective-permute-start.53) | collective-permute-done | bytes 131104 | tf_op jit(solution)/shard_map/ppermute | solution.py:89
  157.6 4.2 %collective-permute-start.64 = (f32[256,128]{1,0:T(8,128)S(1)}, f32[256,128]{1,0:T(8,128)S(1)}, u32[]{:S(2)}, u32[]{:S(2)}) collective-permute-start(f32[256,128]{1,0:T(8,128)S(1)} %add_bitcast_fusion.2), channel_id=1, source_target_pairs={{0,2},{1,3},{8,10},{9,11},{16,18},{17,19},{24,26},{25,27},{4,6},{5... | collective-permute-start | bytes 393224 | tf_op jit(solution)/shard_map/ppermute | solution.py:89
  163.3 2.9 %collective-permute-done.64 = f32[256,128]{1,0:T(8,128)S(1)} collective-permute-done((f32[256,128]{1,0:T(8,128)S(1)}, f32[256,128]{1,0:T(8,128)S(1)}, u32[]{:S(2)}, u32[]{:S(2)}) %collective-permute-start.64) | collective-permute-done | bytes 131104 | tf_op jit(solution)/shard_map/ppermute | solution.py:89
  166.2 2.5 %collective-permute-done.57 = f32[256,128]{1,0:T(8,128)S(1)} collective-permute-done((f32[256,128]{1,0:T(8,128)S(1)}, f32[256,128]{1,0:T(8,128)S(1)}, u32[]{:S(2)}, u32[]{:S(2)}) %collective-permute-start.57) | collective-permute-done | bytes 131104 | tf_op jit(solution)/shard_map/ppermute | solution.py:89
  168.8 3.1 %collective-permute-start.65 = (f32[256,128]{1,0:T(8,128)S(1)}, f32[256,128]{1,0:T(8,128)S(1)}, u32[]{:S(2)}, u32[]{:S(2)}) collective-permute-start(f32[256,128]{1,0:T(8,128)S(1)} %get-tuple-element.3), channel_id=1, source_target_pairs={{0,16},{1,17},{8,24},{9,25},{4,20},{5,21},{12,28},{13,29},{18,2},{... | collective-permute-start | bytes 393224 | tf_op jit(solution)/shard_map/ppermute | solution.py:89
  173.2 2.6 %collective-permute-done.65 = f32[256,128]{1,0:T(8,128)S(1)} collective-permute-done((f32[256,128]{1,0:T(8,128)S(1)}, f32[256,128]{1,0:T(8,128)S(1)}, u32[]{:S(2)}, u32[]{:S(2)}) %collective-permute-start.65) | collective-permute-done | bytes 131104 | tf_op jit(solution)/shard_map/ppermute | solution.py:89
  175.8 6.3 %collective-permute-start.68 = (f32[256,128]{1,0:T(8,128)S(1)}, f32[256,128]{1,0:T(8,128)S(1)}, u32[]{:S(2)}, u32[]{:S(2)}) collective-permute-start(f32[256,128]{1,0:T(8,128)S(1)} %broadcast_select_fusion.refs_0_), channel_id=1, source_target_pairs={{0,12},{1,13},{8,4},{9,5},{16,28},{17,29},{24,20},{25,21},{4,8},{5... | collective-permute-start | bytes 393224 | tf_op jit(solution)/shard_map/ppermute | solution.py:89
  183.2 2.5 %collective-permute-start.61 = (f32[256,128]{1,0:T(8,128)S(1)}, f32[256,128]{1,0:T(8,128)S(1)}, u32[]{:S(2)}, u32[]{:S(2)}) collective-permute-start(f32[256,128]{1,0:T(8,128)S(1)} %broadcast_select_fusion.1.refs_0_), channel_id=1, source_target_pairs={{0,12},{1,13},{8,4},{9,5},{16,28},{17,29},{24,20},{25,21},{4,8},{5... | collective-permute-start | bytes 393224 | tf_op jit(solution)/shard_map/ppermute | solution.py:89
  185.7 3.1 %collective-permute-done.67.refs_2_ = f32[256,128]{1,0:T(8,128)S(1)} collective-permute-done((f32[256,128]{1,0:T(8,128)S(1)}, f32[256,128]{1,0:T(8,128)S(1)}, u32[]{:S(2)}, u32[]{:S(2)}) %collective-permute-start.67) | collective-permute-done | bytes 131104 | tf_op jit(solution)/shard_map/ppermute | solution.py:89
  190.0 3.7 %collective-permute-done.60.refs_2_ = f32[256,128]{1,0:T(8,128)S(1)} collective-permute-done((f32[256,128]{1,0:T(8,128)S(1)}, f32[256,128]{1,0:T(8,128)S(1)}, u32[]{:S(2)}, u32[]{:S(2)}) %collective-permute-start.60) | collective-permute-done | bytes 131104 | tf_op jit(solution)/shard_map/ppermute | solution.py:89
  200.5 3.8 %collective-permute-start.74 = (f32[256,128]{1,0:T(8,128)S(1)}, f32[256,128]{1,0:T(8,128)S(1)}, u32[]{:S(2)}, u32[]{:S(2)}) collective-permute-start(f32[256,128]{1,0:T(8,128)S(1)} %add_bitcast_fusion), channel_id=1, source_target_pairs={{0,2},{1,3},{8,10},{9,11},{16,18},{17,19},{24,26},{25,27},{4,6},{5... | collective-permute-start | bytes 393224 | tf_op jit(solution)/shard_map/ppermute | solution.py:89
  205.0 3.7 %collective-permute-done.74 = f32[256,128]{1,0:T(8,128)S(1)} collective-permute-done((f32[256,128]{1,0:T(8,128)S(1)}, f32[256,128]{1,0:T(8,128)S(1)}, u32[]{:S(2)}, u32[]{:S(2)}) %collective-permute-start.74) | collective-permute-done | bytes 131104 | tf_op jit(solution)/shard_map/ppermute | solution.py:89
  (256 shorter events, 82.9 us)
Async XLA Ops:
  1.9 9.9 %collective-permute-start = (f32[256,128]{1,0:T(8,128)S(1)}, f32[256,128]{1,0:T(8,128)S(1)}, u32[]{:S(2)}, u32[]{:S(2)}) collective-permute-start(f32[256,128]{1,0:T(8,128)S(1)} %get-tuple-element.7), channel_id=1, source_target_pairs={{0,16},{1,17},{8,24},{9,25},{4,20},{5,21},{12,28},{13,29},{18,2},{... | collective-permute-start | bytes 393224 | tf_op jit(solution)/shard_map/ppermute | solution.py:89
  7.8 11.6 %collective-permute-start.8 = (f32[256,128]{1,0:T(8,128)S(1)}, f32[256,128]{1,0:T(8,128)S(1)}, u32[]{:S(2)}, u32[]{:S(2)}) collective-permute-start(f32[256,128]{1,0:T(8,128)S(1)} %get-tuple-element.8), channel_id=1, source_target_pairs={{0,16},{1,17},{8,24},{9,25},{4,20},{5,21},{12,28},{13,29},{18,2},{... | collective-permute-start | bytes 393224 | tf_op jit(solution)/shard_map/ppermute | solution.py:89
  11.7 14.7 %collective-permute-start.3 = (f32[256,128]{1,0:T(8,128)S(1)}, f32[256,128]{1,0:T(8,128)S(1)}, u32[]{:S(2)}, u32[]{:S(2)}) collective-permute-start(f32[256,128]{1,0:T(8,128)S(1)} %broadcast_select_fusion.9.refs_0_), channel_id=1, source_target_pairs={{0,12},{1,13},{8,4},{9,5},{16,28},{17,29},{24,20},{25,21},{4,8},{5... | collective-permute-start | bytes 393224 | tf_op jit(solution)/shard_map/ppermute | solution.py:89
  19.4 10.6 %collective-permute-start.11 = (f32[256,128]{1,0:T(8,128)S(1)}, f32[256,128]{1,0:T(8,128)S(1)}, u32[]{:S(2)}, u32[]{:S(2)}) collective-permute-start(f32[256,128]{1,0:T(8,128)S(1)} %broadcast_select_fusion.8.refs_0_), channel_id=1, source_target_pairs={{0,12},{1,13},{8,4},{9,5},{16,28},{17,29},{24,20},{25,21},{4,8},{5... | collective-permute-start | bytes 393224 | tf_op jit(solution)/shard_map/ppermute | solution.py:89
  35.0 8.3 %collective-permute-start.6 = (f32[256,128]{1,0:T(8,128)S(1)}, f32[256,128]{1,0:T(8,128)S(1)}, u32[]{:S(2)}, u32[]{:S(2)}) collective-permute-start(f32[256,128]{1,0:T(8,128)S(1)} %add_bitcast_fusion.9), channel_id=1, source_target_pairs={{0,2},{1,3},{8,10},{9,11},{16,18},{17,19},{24,26},{25,27},{4,6},{5... | collective-permute-start | bytes 393224 | tf_op jit(solution)/shard_map/ppermute | solution.py:89
  46.9 9.6 %collective-permute-start.31 = (f32[256,128]{1,0:T(8,128)S(1)}, f32[256,128]{1,0:T(8,128)S(1)}, u32[]{:S(2)}, u32[]{:S(2)}) collective-permute-start(f32[256,128]{1,0:T(8,128)S(1)} %add.197), channel_id=1, source_target_pairs={{0,16},{1,17},{8,24},{9,25},{4,20},{5,21},{12,28},{13,29},{18,2},{... | collective-permute-start | bytes 393224 | tf_op jit(solution)/shard_map/ppermute | solution.py:89
  49.3 12.8 %collective-permute-start.18 = (f32[256,128]{1,0:T(8,128)S(1)}, f32[256,128]{1,0:T(8,128)S(1)}, u32[]{:S(2)}, u32[]{:S(2)}) collective-permute-start(f32[256,128]{1,0:T(8,128)S(1)} %get-tuple-element.23.refs_0_), channel_id=1, source_target_pairs={{0,8},{1,9},{8,0},{9,1},{16,24},{17,25},{24,16},{25,17},{4,12},{5,... | collective-permute-start | bytes 393224 | tf_op jit(solution)/shard_map/ppermute | solution.py:89
  56.5 14.4 %collective-permute-start.34 = (f32[256,128]{1,0:T(8,128)S(1)}, f32[256,128]{1,0:T(8,128)S(1)}, u32[]{:S(2)}, u32[]{:S(2)}) collective-permute-start(f32[256,128]{1,0:T(8,128)S(1)} %get-tuple-element.24.refs_0_), channel_id=1, source_target_pairs={{0,12},{1,13},{8,4},{9,5},{16,28},{17,29},{24,20},{25,21},{4,8},{5... | collective-permute-start | bytes 393224 | tf_op jit(solution)/shard_map/ppermute | solution.py:89
  58.7 12.2 %collective-permute-start.33 = (f32[256,128]{1,0:T(8,128)S(1)}, f32[256,128]{1,0:T(8,128)S(1)}, u32[]{:S(2)}, u32[]{:S(2)}) collective-permute-start(f32[256,128]{1,0:T(8,128)S(1)} %get-tuple-element.24.refs_0_), channel_id=1, source_target_pairs={{0,8},{1,9},{8,0},{9,1},{16,24},{17,25},{24,16},{25,17},{4,12},{5,... | collective-permute-start | bytes 393224 | tf_op jit(solution)/shard_map/ppermute | solution.py:89
  58.7 12.2 %collective-permute-start.32 = (f32[256,128]{1,0:T(8,128)S(1)}, f32[256,128]{1,0:T(8,128)S(1)}, u32[]{:S(2)}, u32[]{:S(2)}) collective-permute-start(f32[256,128]{1,0:T(8,128)S(1)} %get-tuple-element.24.refs_0_), channel_id=1, source_target_pairs={{0,4},{1,5},{8,12},{9,13},{16,20},{17,21},{24,28},{25,29},{4,0},{5... | collective-permute-start | bytes 393224 | tf_op jit(solution)/shard_map/ppermute | solution.py:89
  60.1 8.1 %collective-permute-start.19 = (f32[256,128]{1,0:T(8,128)S(1)}, f32[256,128]{1,0:T(8,128)S(1)}, u32[]{:S(2)}, u32[]{:S(2)}) collective-permute-start(f32[256,128]{1,0:T(8,128)S(1)} %get-tuple-element.23.refs_0_), channel_id=1, source_target_pairs={{0,12},{1,13},{8,4},{9,5},{16,28},{17,29},{24,20},{25,21},{4,8},{5... | collective-permute-start | bytes 393224 | tf_op jit(solution)/shard_map/ppermute | solution.py:89
  62.1 8.6 %collective-permute-start.17 = (f32[256,128]{1,0:T(8,128)S(1)}, f32[256,128]{1,0:T(8,128)S(1)}, u32[]{:S(2)}, u32[]{:S(2)}) collective-permute-start(f32[256,128]{1,0:T(8,128)S(1)} %get-tuple-element.23.refs_0_), channel_id=1, source_target_pairs={{0,4},{1,5},{8,12},{9,13},{16,20},{17,21},{24,28},{25,29},{4,0},{5... | collective-permute-start | bytes 393224 | tf_op jit(solution)/shard_map/ppermute | solution.py:89
  75.2 8.2 %collective-permute-start.22 = (f32[256,128]{1,0:T(8,128)S(1)}, f32[256,128]{1,0:T(8,128)S(1)}, u32[]{:S(2)}, u32[]{:S(2)}) collective-permute-start(f32[256,128]{1,0:T(8,128)S(1)} %add_bitcast_fusion.7), channel_id=1, source_target_pairs={{0,2},{1,3},{8,10},{9,11},{16,18},{17,19},{24,26},{25,27},{4,6},{5... | collective-permute-start | bytes 393224 | tf_op jit(solution)/shard_map/ppermute | solution.py:89
  86.9 9.7 %collective-permute-start.38 = (f32[256,128]{1,0:T(8,128)S(1)}, f32[256,128]{1,0:T(8,128)S(1)}, u32[]{:S(2)}, u32[]{:S(2)}) collective-permute-start(f32[256,128]{1,0:T(8,128)S(1)} %bitcast_subtract_fusion.2), channel_id=1, source_target_pairs={{0,16},{1,17},{8,24},{9,25},{4,20},{5,21},{12,28},{13,29},{18,2},{... | collective-permute-start | bytes 393224 | tf_op jit(solution)/shard_map/ppermute | solution.py:89
  90.6 12.0 %collective-permute-start.25 = (f32[256,128]{1,0:T(8,128)S(1)}, f32[256,128]{1,0:T(8,128)S(1)}, u32[]{:S(2)}, u32[]{:S(2)}) collective-permute-start(f32[256,128]{1,0:T(8,128)S(1)} %broadcast_select_fusion.6.refs_0_), channel_id=1, source_target_pairs={{0,8},{1,9},{8,0},{9,1},{16,24},{17,25},{24,16},{25,17},{4,12},{5,... | collective-permute-start | bytes 393224 | tf_op jit(solution)/shard_map/ppermute | solution.py:89
  96.7 14.3 %collective-permute-start.41 = (f32[256,128]{1,0:T(8,128)S(1)}, f32[256,128]{1,0:T(8,128)S(1)}, u32[]{:S(2)}, u32[]{:S(2)}) collective-permute-start(f32[256,128]{1,0:T(8,128)S(1)} %broadcast_select_fusion.4.refs_0_), channel_id=1, source_target_pairs={{0,12},{1,13},{8,4},{9,5},{16,28},{17,29},{24,20},{25,21},{4,8},{5... | collective-permute-start | bytes 393224 | tf_op jit(solution)/shard_map/ppermute | solution.py:89
  99.1 11.9 %collective-permute-start.40 = (f32[256,128]{1,0:T(8,128)S(1)}, f32[256,128]{1,0:T(8,128)S(1)}, u32[]{:S(2)}, u32[]{:S(2)}) collective-permute-start(f32[256,128]{1,0:T(8,128)S(1)} %broadcast_select_fusion.4.refs_0_), channel_id=1, source_target_pairs={{0,8},{1,9},{8,0},{9,1},{16,24},{17,25},{24,16},{25,17},{4,12},{5,... | collective-permute-start | bytes 393224 | tf_op jit(solution)/shard_map/ppermute | solution.py:89
  99.6 11.4 %collective-permute-start.39 = (f32[256,128]{1,0:T(8,128)S(1)}, f32[256,128]{1,0:T(8,128)S(1)}, u32[]{:S(2)}, u32[]{:S(2)}) collective-permute-start(f32[256,128]{1,0:T(8,128)S(1)} %broadcast_select_fusion.4.refs_0_), channel_id=1, source_target_pairs={{0,4},{1,5},{8,12},{9,13},{16,20},{17,21},{24,28},{25,29},{4,0},{5... | collective-permute-start | bytes 393224 | tf_op jit(solution)/shard_map/ppermute | solution.py:89
  100.3 8.5 %collective-permute-start.26 = (f32[256,128]{1,0:T(8,128)S(1)}, f32[256,128]{1,0:T(8,128)S(1)}, u32[]{:S(2)}, u32[]{:S(2)}) collective-permute-start(f32[256,128]{1,0:T(8,128)S(1)} %broadcast_select_fusion.6.refs_0_), channel_id=1, source_target_pairs={{0,12},{1,13},{8,4},{9,5},{16,28},{17,29},{24,20},{25,21},{4,8},{5... | collective-permute-start | bytes 393224 | tf_op jit(solution)/shard_map/ppermute | solution.py:89
  102.6 8.2 %collective-permute-start.24 = (f32[256,128]{1,0:T(8,128)S(1)}, f32[256,128]{1,0:T(8,128)S(1)}, u32[]{:S(2)}, u32[]{:S(2)}) collective-permute-start(f32[256,128]{1,0:T(8,128)S(1)} %broadcast_select_fusion.6.refs_0_), channel_id=1, source_target_pairs={{0,4},{1,5},{8,12},{9,13},{16,20},{17,21},{24,28},{25,29},{4,0},{5... | collective-permute-start | bytes 393224 | tf_op jit(solution)/shard_map/ppermute | solution.py:89
  118.7 8.3 %collective-permute-start.44 = (f32[256,128]{1,0:T(8,128)S(1)}, f32[256,128]{1,0:T(8,128)S(1)}, u32[]{:S(2)}, u32[]{:S(2)}) collective-permute-start(f32[256,128]{1,0:T(8,128)S(1)} %add_bitcast_fusion.4), channel_id=1, source_target_pairs={{0,2},{1,3},{8,10},{9,11},{16,18},{17,19},{24,26},{25,27},{4,6},{5... | collective-permute-start | bytes 393224 | tf_op jit(solution)/shard_map/ppermute | solution.py:89
  127.0 11.1 %collective-permute-start.46 = (f32[256,128]{1,0:T(8,128)S(1)}, f32[256,128]{1,0:T(8,128)S(1)}, u32[]{:S(2)}, u32[]{:S(2)}) collective-permute-start(f32[256,128]{1,0:T(8,128)S(1)} %add.211), channel_id=1, source_target_pairs={{0,16},{1,17},{8,24},{9,25},{4,20},{5,21},{12,28},{13,29},{18,2},{... | collective-permute-start | bytes 393224 | tf_op jit(solution)/shard_map/ppermute | solution.py:89
  129.0 9.1 %collective-permute-start.45 = (f32[256,128]{1,0:T(8,128)S(1)}, f32[256,128]{1,0:T(8,128)S(1)}, u32[]{:S(2)}, u32[]{:S(2)}) collective-permute-start(f32[256,128]{1,0:T(8,128)S(1)} %add.211), channel_id=1, source_target_pairs={{0,1},{1,0},{8,9},{9,8},{16,17},{17,16},{24,25},{25,24},{4,5},{5,4... | collective-permute-start | bytes 393224 | tf_op jit(solution)/shard_map/ppermute | solution.py:89
  129.5 15.0 %collective-permute-start.54 = (f32[256,128]{1,0:T(8,128)S(1)}, f32[256,128]{1,0:T(8,128)S(1)}, u32[]{:S(2)}, u32[]{:S(2)}) collective-permute-start(f32[256,128]{1,0:T(8,128)S(1)} %get-tuple-element.21.refs_0_), channel_id=1, source_target_pairs={{0,12},{1,13},{8,4},{9,5},{16,28},{17,29},{24,20},{25,21},{4,8},{5... | collective-permute-start | bytes 393224 | tf_op jit(solution)/shard_map/ppermute | solution.py:89
  138.2 8.3 %collective-permute-start.49 = (f32[256,128]{1,0:T(8,128)S(1)}, f32[256,128]{1,0:T(8,128)S(1)}, u32[]{:S(2)}, u32[]{:S(2)}) collective-permute-start(f32[256,128]{1,0:T(8,128)S(1)} %get-tuple-element.22.refs_0_), channel_id=1, source_target_pairs={{0,12},{1,13},{8,4},{9,5},{16,28},{17,29},{24,20},{25,21},{4,8},{5... | collective-permute-start | bytes 393224 | tf_op jit(solution)/shard_map/ppermute | solution.py:89
  144.8 7.9 %collective-permute-start.55 = (f32[2,256,128]{2,1,0:T(8,128)S(1)}, f32[2,256,128]{2,1,0:T(8,128)S(1)}, u32[]{:S(2)}, u32[]{:S(2)}) collective-permute-start(f32[2,256,128]{2,1,0:T(8,128)S(1)} %pad_maximum_fusion.12), channel_id=1, source_target_pairs={{0,1},{1,0},{8,9},{9,8},{16,17},{17,16},{24,25},{25,24},{4,5},{5,4... | collective-permute-start | bytes 786440 | tf_op jit(solution)/shard_map/ppermute | solution.py:89
  157.6 8.6 %collective-permute-start.64 = (f32[256,128]{1,0:T(8,128)S(1)}, f32[256,128]{1,0:T(8,128)S(1)}, u32[]{:S(2)}, u32[]{:S(2)}) collective-permute-start(f32[256,128]{1,0:T(8,128)S(1)} %add_bitcast_fusion.2), channel_id=1, source_target_pairs={{0,2},{1,3},{8,10},{9,11},{16,18},{17,19},{24,26},{25,27},{4,6},{5... | collective-permute-start | bytes 393224 | tf_op jit(solution)/shard_map/ppermute | solution.py:89
  171.9 11.3 %collective-permute-start.58 = (f32[256,128]{1,0:T(8,128)S(1)}, f32[256,128]{1,0:T(8,128)S(1)}, u32[]{:S(2)}, u32[]{:S(2)}) collective-permute-start(f32[256,128]{1,0:T(8,128)S(1)} %get-tuple-element.4), channel_id=1, source_target_pairs={{0,16},{1,17},{8,24},{9,25},{4,20},{5,21},{12,28},{13,29},{18,2},{... | collective-permute-start | bytes 393224 | tf_op jit(solution)/shard_map/ppermute | solution.py:89
  175.8 14.0 %collective-permute-start.68 = (f32[256,128]{1,0:T(8,128)S(1)}, f32[256,128]{1,0:T(8,128)S(1)}, u32[]{:S(2)}, u32[]{:S(2)}) collective-permute-start(f32[256,128]{1,0:T(8,128)S(1)} %broadcast_select_fusion.refs_0_), channel_id=1, source_target_pairs={{0,12},{1,13},{8,4},{9,5},{16,28},{17,29},{24,20},{25,21},{4,8},{5... | collective-permute-start | bytes 393224 | tf_op jit(solution)/shard_map/ppermute | solution.py:89
  183.2 10.5 %collective-permute-start.61 = (f32[256,128]{1,0:T(8,128)S(1)}, f32[256,128]{1,0:T(8,128)S(1)}, u32[]{:S(2)}, u32[]{:S(2)}) collective-permute-start(f32[256,128]{1,0:T(8,128)S(1)} %broadcast_select_fusion.1.refs_0_), channel_id=1, source_target_pairs={{0,12},{1,13},{8,4},{9,5},{16,28},{17,29},{24,20},{25,21},{4,8},{5... | collective-permute-start | bytes 393224 | tf_op jit(solution)/shard_map/ppermute | solution.py:89
  185.7 8.0 %collective-permute-start.60 = (f32[256,128]{1,0:T(8,128)S(1)}, f32[256,128]{1,0:T(8,128)S(1)}, u32[]{:S(2)}, u32[]{:S(2)}) collective-permute-start(f32[256,128]{1,0:T(8,128)S(1)} %broadcast_select_fusion.1.refs_0_), channel_id=1, source_target_pairs={{0,8},{1,9},{8,0},{9,1},{16,24},{17,25},{24,16},{25,17},{4,12},{5,... | collective-permute-start | bytes 393224 | tf_op jit(solution)/shard_map/ppermute | solution.py:89
  200.5 8.1 %collective-permute-start.74 = (f32[256,128]{1,0:T(8,128)S(1)}, f32[256,128]{1,0:T(8,128)S(1)}, u32[]{:S(2)}, u32[]{:S(2)}) collective-permute-start(f32[256,128]{1,0:T(8,128)S(1)} %add_bitcast_fusion), channel_id=1, source_target_pairs={{0,2},{1,3},{8,10},{9,11},{16,18},{17,19},{24,26},{25,27},{4,6},{5... | collective-permute-start | bytes 393224 | tf_op jit(solution)/shard_map/ppermute | solution.py:89
  (58 other events, 546.7 us)

commit v2 on v1

--- a/solution.py
+++ b/solution.py
@@ -112,7 +112,8 @@
     x, y, z, k = place()
     far = send(mine, TO_FAR)
     own = jnp.where(z // 2 == x, mine, far)
-    beside, above, across = send(own, TO_Y), send(own, TO_Z), send(own, TO_YZ)
+    beside, above = send(own, TO_Y), send(own, TO_Z)
+    across = send(above, TO_Y)
     same = (z % 2) == k
     swapped = send(jnp.stack([jnp.where(same, above, own), jnp.where(same, across, beside)]), TO_CORE)
     return own, beside, above, across, swapped
@@ -318,15 +319,21 @@
         (inverse_root, (256, 512), lambda i, b=b: (i, 2 * b + g), 2 * PIECE * b, 2 * PIECE) for b in (0, 1)
     ]
     part = apply(root_pieces[0], columns(0), 1024, 256)
-    solved_root = []
+    mine, theirs = [], []
     for g in (0, 1):
         final = apply(root_pieces[1], columns(1), 512, 256, first_tile=2 * g, add=part)
-        mine, other = halve(final.reshape(2, PIECE, n))
-        solved_root.append(both_halves(mine + other))
+        one_half, other = halve(final.reshape(2, PIECE, n))
+        mine.append(one_half + other)
+        theirs.append(send(mine[g], TO_CORE))
+    first_group = lax.broadcasted_iota(jnp.int32, (2, 2, 1, 1), 0) == 0
+    here = lax.broadcasted_iota(jnp.int32, (2, 2, 1, 1), 1) == k
+    solved_root = jnp.where(
+        here, jnp.where(first_group, mine[0], mine[1]), jnp.where(first_group, theirs[0], theirs[1])
+    ).reshape(4 * PIECE, n)
     return (
         jnp.concatenate(solved_leaf, axis=0),
         jnp.stack([h.reshape(2 * PIECE, n) for h in solved_mid]),
-        jnp.concatenate([h.reshape(2 * PIECE, n) for h in solved_root], axis=0),
+        solved_root,
     )
 
 

time: 214 us -> 207 us (0.967)
  starting transfers between devices: 118 us -> 107 us
  waiting for transfers between devices: 66.3 us -> 70.7 us
    ppermute x76, starting transfers between devices: 118 us -> 107 us  [send(): return lax.ppermute(value, AXES, pairs)]
    ppermute x76, waiting for transfers between devices: 66.3 us -> 70.7 us  [send(): return lax.ppermute(value, AXES, pairs)]
  transfers between devices with their start and end apart: 76 -> 76, of which waited for: 30 -> 39; matrix products, arithmetic and copies ran while one was open for 3% -> 3% of each run, Pallas kernels for 7% -> 8%
where the time goes in v2:
time: 207 us
  starting transfers between devices  107 us (52%)
  waiting for transfers between devices  70.7 us (34%)
  Pallas kernels  17.9 us (9%)
  other arithmetic  5.49 us (3%)
  local copies, waits for them, and re-layouts  4.29 us (2%)
    ppermute x76, starting transfers between devices, send(): return lax.ppermute(value, AXES, pairs)  107 us
    ppermute x76, waiting for transfers between devices, send(): return lax.ppermute(value, AXES, pairs)  70.7 us
    pallas_call x14, Pallas kernels, apply(): pl.pallas_call(functools.partial(kernel_body, tuple(((t[3], t[4]) for t i...  17.9 us
  transfers between devices with their start and end apart: 76, of which 39 were waited for; matrix products, arithmetic and copies ran while one was open for 3% of the time, Pallas kernels for 8%

profile of v2, /device:TPU:0, one launch (start us, length us, event | category | flops | bytes accessed | tf_op | source)
XLA Modules:
  0.0 206.7 jit_solution(6941267201107883279)
XLA Ops:
  1.9 5.9 %collective-permute-start = (f32[256,128]{1,0:T(8,128)S(1)}, f32[256,128]{1,0:T(8,128)S(1)}, u32[]{:S(2)}, u32[]{:S(2)}) collective-permute-start(f32[256,128]{1,0:T(8,128)S(1)} %get-tuple-element.7), channel_id=1, source_target_pairs={{0,16},{1,17},{8,24},{9,25},{4,20},{5,21},{12,28},{13,29},{18,2},{... | collective-permute-start | bytes 393224 | tf_op jit(solution)/shard_map/ppermute | solution.py:89
  11.7 6.0 %collective-permute-start.2 = (f32[256,128]{1,0:T(8,128)S(1)}, f32[256,128]{1,0:T(8,128)S(1)}, u32[]{:S(2)}, u32[]{:S(2)}) collective-permute-start(f32[256,128]{1,0:T(8,128)S(1)} %broadcast_select_fusion.9.refs_0_), channel_id=1, source_target_pairs={{0,8},{1,9},{8,0},{9,1},{16,24},{17,25},{24,16},{25,17},{4,12},{5,... | collective-permute-start | bytes 393224 | tf_op jit(solution)/shard_map/ppermute | solution.py:89
  26.9 4.4 %collective-permute-done.11.refs_3_ = f32[256,128]{1,0:T(8,128)S(1)} collective-permute-done((f32[256,128]{1,0:T(8,128)S(1)}, f32[256,128]{1,0:T(8,128)S(1)}, u32[]{:S(2)}, u32[]{:S(2)}) %collective-permute-start.11) | collective-permute-done | bytes 131104 | tf_op jit(solution)/shard_map/ppermute | solution.py:89
  39.6 3.7 %collective-permute-done.14 = f32[256,128]{1,0:T(8,128)S(1)} collective-permute-done((f32[256,128]{1,0:T(8,128)S(1)}, f32[256,128]{1,0:T(8,128)S(1)}, u32[]{:S(2)}, u32[]{:S(2)}) %collective-permute-start.14) | collective-permute-done | bytes 131104 | tf_op jit(solution)/shard_map/ppermute | solution.py:89
  43.3 5.3 %collective-permute-start.31 = (f32[256,128]{1,0:T(8,128)S(1)}, f32[256,128]{1,0:T(8,128)S(1)}, u32[]{:S(2)}, u32[]{:S(2)}) collective-permute-start(f32[256,128]{1,0:T(8,128)S(1)} %add.195), channel_id=1, source_target_pairs={{0,16},{1,17},{8,24},{9,25},{4,20},{5,21},{12,28},{13,29},{18,2},{... | collective-permute-start | bytes 393224 | tf_op jit(solution)/shard_map/ppermute | solution.py:89
  48.8 1.8 collective-permute-start.16
  51.3 6.1 %collective-permute-start.33 = (f32[256,128]{1,0:T(8,128)S(1)}, f32[256,128]{1,0:T(8,128)S(1)}, u32[]{:S(2)}, u32[]{:S(2)}) collective-permute-start(f32[256,128]{1,0:T(8,128)S(1)} %get-tuple-element.20.refs_0_), channel_id=1, source_target_pairs={{0,8},{1,9},{8,0},{9,1},{16,24},{17,25},{24,16},{25,17},{4,12},{5,... | collective-permute-start | bytes 393224 | tf_op jit(solution)/shard_map/ppermute | solution.py:89
  61.4 1.7 collective-permute-done.18.refs_2_
  64.5 4.7 %collective-permute-done.34.refs_3_ = f32[256,128]{1,0:T(8,128)S(1)} collective-permute-done((f32[256,128]{1,0:T(8,128)S(1)}, f32[256,128]{1,0:T(8,128)S(1)}, u32[]{:S(2)}, u32[]{:S(2)}) %collective-permute-start.34) | collective-permute-done | bytes 131104 | tf_op jit(solution)/shard_map/ppermute | solution.py:89
  76.6 3.4 %collective-permute-done.37 = f32[256,128]{1,0:T(8,128)S(1)} collective-permute-done((f32[256,128]{1,0:T(8,128)S(1)}, f32[256,128]{1,0:T(8,128)S(1)}, u32[]{:S(2)}, u32[]{:S(2)}) %collective-permute-start.37) | collective-permute-done | bytes 131104 | tf_op jit(solution)/shard_map/ppermute | solution.py:89
  80.0 5.3 %collective-permute-start.38 = (f32[256,128]{1,0:T(8,128)S(1)}, f32[256,128]{1,0:T(8,128)S(1)}, u32[]{:S(2)}, u32[]{:S(2)}) collective-permute-start(f32[256,128]{1,0:T(8,128)S(1)} %bitcast_subtract_fusion.2), channel_id=1, source_target_pairs={{0,16},{1,17},{8,24},{9,25},{4,20},{5,21},{12,28},{13,29},{18,2},{... | collective-permute-start | bytes 393224 | tf_op jit(solution)/shard_map/ppermute | solution.py:89
  85.4 2.3 %collective-permute-start.23 = (f32[256,128]{1,0:T(8,128)S(1)}, f32[256,128]{1,0:T(8,128)S(1)}, u32[]{:S(2)}, u32[]{:S(2)}) collective-permute-start(f32[256,128]{1,0:T(8,128)S(1)} %bitcast_subtract_fusion.3), channel_id=1, source_target_pairs={{0,16},{1,17},{8,24},{9,25},{4,20},{5,21},{12,28},{13,29},{18,2},{... | collective-permute-start | bytes 393224 | tf_op jit(solution)/shard_map/ppermute | solution.py:89
  88.2 6.6 %collective-permute-start.40 = (f32[256,128]{1,0:T(8,128)S(1)}, f32[256,128]{1,0:T(8,128)S(1)}, u32[]{:S(2)}, u32[]{:S(2)}) collective-permute-start(f32[256,128]{1,0:T(8,128)S(1)} %broadcast_select_fusion.4.refs_0_), channel_id=1, source_target_pairs={{0,8},{1,9},{8,0},{9,1},{16,24},{17,25},{24,16},{25,17},{4,12},{5,... | collective-permute-start | bytes 393224 | tf_op jit(solution)/shard_map/ppermute | solution.py:89
  101.9 2.1 %collective-permute-done.24.refs_1_ = f32[256,128]{1,0:T(8,128)S(1)} collective-permute-done((f32[256,128]{1,0:T(8,128)S(1)}, f32[256,128]{1,0:T(8,128)S(1)}, u32[]{:S(2)}, u32[]{:S(2)}) %collective-permute-start.24) | collective-permute-done | bytes 131104 | tf_op jit(solution)/shard_map/ppermute | solution.py:89
  104.0 3.0 %collective-permute-done.26.refs_3_ = f32[256,128]{1,0:T(8,128)S(1)} collective-permute-done((f32[256,128]{1,0:T(8,128)S(1)}, f32[256,128]{1,0:T(8,128)S(1)}, u32[]{:S(2)}, u32[]{:S(2)}) %collective-permute-start.26) | collective-permute-done | bytes 131104 | tf_op jit(solution)/shard_map/ppermute | solution.py:89
  113.6 4.1 %collective-permute-done.29 = f32[256,128]{1,0:T(8,128)S(1)} collective-permute-done((f32[256,128]{1,0:T(8,128)S(1)}, f32[256,128]{1,0:T(8,128)S(1)}, u32[]{:S(2)}, u32[]{:S(2)}) %collective-permute-start.29) | collective-permute-done | bytes 131104 | tf_op jit(solution)/shard_map/ppermute | solution.py:89
  117.7 5.3 %collective-permute-start.51 = (f32[256,128]{1,0:T(8,128)S(1)}, f32[256,128]{1,0:T(8,128)S(1)}, u32[]{:S(2)}, u32[]{:S(2)}) collective-permute-start(f32[256,128]{1,0:T(8,128)S(1)} %add.203), channel_id=1, source_target_pairs={{0,16},{1,17},{8,24},{9,25},{4,20},{5,21},{12,28},{13,29},{18,2},{... | collective-permute-start | bytes 393224 | tf_op jit(solution)/shard_map/ppermute | solution.py:89
  123.2 2.0 collective-permute-start.46
  125.7 5.2 %collective-permute-start.53 = (f32[256,128]{1,0:T(8,128)S(1)}, f32[256,128]{1,0:T(8,128)S(1)}, u32[]{:S(2)}, u32[]{:S(2)}) collective-permute-start(f32[256,128]{1,0:T(8,128)S(1)} %get-tuple-element.17.refs_0_), channel_id=1, source_target_pairs={{0,8},{1,9},{8,0},{9,1},{16,24},{17,25},{24,16},{25,17},{4,12},{5,... | collective-permute-start | bytes 393224 | tf_op jit(solution)/shard_map/ppermute | solution.py:89
  138.0 4.5 %collective-permute-done.54.refs_3_ = f32[256,128]{1,0:T(8,128)S(1)} collective-permute-done((f32[256,128]{1,0:T(8,128)S(1)}, f32[256,128]{1,0:T(8,128)S(1)}, u32[]{:S(2)}, u32[]{:S(2)}) %collective-permute-start.54) | collective-permute-done | bytes 131104 | tf_op jit(solution)/shard_map/ppermute | solution.py:89
  144.5 1.9 shard_map.145.refs_8_
  146.4 2.0 shard_map.146.refs_7_
  148.7 1.9 shard_map.147.refs_7_
  155.7 4.0 %collective-permute-done.64 = f32[256,128]{1,0:T(8,128)S(1)} collective-permute-done((f32[256,128]{1,0:T(8,128)S(1)}, f32[256,128]{1,0:T(8,128)S(1)}, u32[]{:S(2)}, u32[]{:S(2)}) %collective-permute-start.64) | collective-permute-done | bytes 131104 | tf_op jit(solution)/shard_map/ppermute | solution.py:89
  159.7 2.3 %collective-permute-done.57 = f32[256,128]{1,0:T(8,128)S(1)} collective-permute-done((f32[256,128]{1,0:T(8,128)S(1)}, f32[256,128]{1,0:T(8,128)S(1)}, u32[]{:S(2)}, u32[]{:S(2)}) %collective-permute-start.57) | collective-permute-done | bytes 131104 | tf_op jit(solution)/shard_map/ppermute | solution.py:89
  162.1 5.4 %collective-permute-start.65 = (f32[256,128]{1,0:T(8,128)S(1)}, f32[256,128]{1,0:T(8,128)S(1)}, u32[]{:S(2)}, u32[]{:S(2)}) collective-permute-start(f32[256,128]{1,0:T(8,128)S(1)} %get-tuple-element.3), channel_id=1, source_target_pairs={{0,16},{1,17},{8,24},{9,25},{4,20},{5,21},{12,28},{13,29},{18,2},{... | collective-permute-start | bytes 393224 | tf_op jit(solution)/shard_map/ppermute | solution.py:89
  168.8 2.6 %collective-permute-done.65 = f32[256,128]{1,0:T(8,128)S(1)} collective-permute-done((f32[256,128]{1,0:T(8,128)S(1)}, f32[256,128]{1,0:T(8,128)S(1)}, u32[]{:S(2)}, u32[]{:S(2)}) %collective-permute-start.65) | collective-permute-done | bytes 131104 | tf_op jit(solution)/shard_map/ppermute | solution.py:89
  171.4 5.8 %collective-permute-start.67 = (f32[256,128]{1,0:T(8,128)S(1)}, f32[256,128]{1,0:T(8,128)S(1)}, u32[]{:S(2)}, u32[]{:S(2)}) collective-permute-start(f32[256,128]{1,0:T(8,128)S(1)} %broadcast_select_fusion.refs_0_), channel_id=1, source_target_pairs={{0,8},{1,9},{8,0},{9,1},{16,24},{17,25},{24,16},{25,17},{4,12},{5,... | collective-permute-start | bytes 393224 | tf_op jit(solution)/shard_map/ppermute | solution.py:89
  184.3 3.8 %collective-permute-done.68.refs_3_ = f32[256,128]{1,0:T(8,128)S(1)} collective-permute-done((f32[256,128]{1,0:T(8,128)S(1)}, f32[256,128]{1,0:T(8,128)S(1)}, u32[]{:S(2)}, u32[]{:S(2)}) %collective-permute-start.68) | collective-permute-done | bytes 131104 | tf_op jit(solution)/shard_map/ppermute | solution.py:89
  189.8 2.3 %shard_map.150.refs_7_ = f32[1024,128]{1,0:T(8,128)S(1)} custom-call(f32[256,128]{1,0:T(8,128)S(1)} %broadcast_select_fusion.refs_0_, f32[256,128]{1,0:T(8,128)S(1)} %collective-permute-done.66.refs_1_, f32[256,128]{1,0:T(8,128)S(1)} %collective-permute-done.67.refs_2_, f32[256,128]{1,0:T(8,128)S(1)} %collective-permute-done.68.refs_3_, ...), custom_call_target="tpu_custom_call" | custom-call | flops 1073741824 | bytes 4194304 | tf_op jit(solution)/shard_map/pallas_call | solution.py:211
  198.6 3.2 %collective-permute-done.73 = f32[256,128]{1,0:T(8,128)S(1)} collective-permute-done((f32[256,128]{1,0:T(8,128)S(1)}, f32[256,128]{1,0:T(8,128)S(1)}, u32[]{:S(2)}, u32[]{:S(2)}) %collective-permute-start.73) | collective-permute-done | bytes 131104 | tf_op jit(solution)/shard_map/ppermute | solution.py:89
  201.9 2.2 %collective-permute-done.71 = f32[256,128]{1,0:T(8,128)S(1)} collective-permute-done((f32[256,128]{1,0:T(8,128)S(1)}, f32[256,128]{1,0:T(8,128)S(1)}, u32[]{:S(2)}, u32[]{:S(2)}) %collective-permute-start.71) | collective-permute-done | bytes 131104 | tf_op jit(solution)/shard_map/ppermute | solution.py:89
  (258 shorter events, 84.0 us)
Async XLA Ops:
  1.9 9.9 %collective-permute-start = (f32[256,128]{1,0:T(8,128)S(1)}, f32[256,128]{1,0:T(8,128)S(1)}, u32[]{:S(2)}, u32[]{:S(2)}) collective-permute-start(f32[256,128]{1,0:T(8,128)S(1)} %get-tuple-element.7), channel_id=1, source_target_pairs={{0,16},{1,17},{8,24},{9,25},{4,20},{5,21},{12,28},{13,29},{18,2},{... | collective-permute-start | bytes 393224 | tf_op jit(solution)/shard_map/ppermute | solution.py:89
  7.8 11.5 %collective-permute-start.8 = (f32[256,128]{1,0:T(8,128)S(1)}, f32[256,128]{1,0:T(8,128)S(1)}, u32[]{:S(2)}, u32[]{:S(2)}) collective-permute-start(f32[256,128]{1,0:T(8,128)S(1)} %get-tuple-element.8), channel_id=1, source_target_pairs={{0,16},{1,17},{8,24},{9,25},{4,20},{5,21},{12,28},{13,29},{18,2},{... | collective-permute-start | bytes 393224 | tf_op jit(solution)/shard_map/ppermute | solution.py:89
  11.7 10.3 %collective-permute-start.2 = (f32[256,128]{1,0:T(8,128)S(1)}, f32[256,128]{1,0:T(8,128)S(1)}, u32[]{:S(2)}, u32[]{:S(2)}) collective-permute-start(f32[256,128]{1,0:T(8,128)S(1)} %broadcast_select_fusion.9.refs_0_), channel_id=1, source_target_pairs={{0,8},{1,9},{8,0},{9,1},{16,24},{17,25},{24,16},{25,17},{4,12},{5,... | collective-permute-start | bytes 393224 | tf_op jit(solution)/shard_map/ppermute | solution.py:89
  17.8 13.6 %collective-permute-start.1 = (f32[256,128]{1,0:T(8,128)S(1)}, f32[256,128]{1,0:T(8,128)S(1)}, u32[]{:S(2)}, u32[]{:S(2)}) collective-permute-start(f32[256,128]{1,0:T(8,128)S(1)} %broadcast_select_fusion.9.refs_0_), channel_id=1, source_target_pairs={{0,4},{1,5},{8,12},{9,13},{16,20},{17,21},{24,28},{25,29},{4,0},{5... | collective-permute-start | bytes 393224 | tf_op jit(solution)/shard_map/ppermute | solution.py:89
  22.0 9.4 %collective-permute-start.3 = (f32[256,128]{1,0:T(8,128)S(1)}, f32[256,128]{1,0:T(8,128)S(1)}, u32[]{:S(2)}, u32[]{:S(2)}) collective-permute-start(f32[256,128]{1,0:T(8,128)S(1)} %collective-permute-done.2.refs_2_), channel_id=1, source_target_pairs={{0,4},{1,5},{8,12},{9,13},{16,20},{17,21},{24,28},{25,29},{4,0},{5... | collective-permute-start | bytes 393224 | tf_op jit(solution)/shard_map/ppermute | solution.py:89
  39.1 9.7 %collective-permute-start.6 = (f32[256,128]{1,0:T(8,128)S(1)}, f32[256,128]{1,0:T(8,128)S(1)}, u32[]{:S(2)}, u32[]{:S(2)}) collective-permute-start(f32[256,128]{1,0:T(8,128)S(1)} %add_bitcast_fusion.9), channel_id=1, source_target_pairs={{0,2},{1,3},{8,10},{9,11},{16,18},{17,19},{24,26},{25,27},{4,6},{5... | collective-permute-start | bytes 393224 | tf_op jit(solution)/shard_map/ppermute | solution.py:89
  43.3 7.9 %collective-permute-start.31 = (f32[256,128]{1,0:T(8,128)S(1)}, f32[256,128]{1,0:T(8,128)S(1)}, u32[]{:S(2)}, u32[]{:S(2)}) collective-permute-start(f32[256,128]{1,0:T(8,128)S(1)} %add.195), channel_id=1, source_target_pairs={{0,16},{1,17},{8,24},{9,25},{4,20},{5,21},{12,28},{13,29},{18,2},{... | collective-permute-start | bytes 393224 | tf_op jit(solution)/shard_map/ppermute | solution.py:89
  48.8 9.2 %collective-permute-start.16 = (f32[256,128]{1,0:T(8,128)S(1)}, f32[256,128]{1,0:T(8,128)S(1)}, u32[]{:S(2)}, u32[]{:S(2)}) collective-permute-start(f32[256,128]{1,0:T(8,128)S(1)} %add.191), channel_id=1, source_target_pairs={{0,16},{1,17},{8,24},{9,25},{4,20},{5,21},{12,28},{13,29},{18,2},{... | collective-permute-start | bytes 393224 | tf_op jit(solution)/shard_map/ppermute | solution.py:89
  50.6 7.4 %collective-permute-start.7 = (f32[256,128]{1,0:T(8,128)S(1)}, f32[256,128]{1,0:T(8,128)S(1)}, u32[]{:S(2)}, u32[]{:S(2)}) collective-permute-start(f32[256,128]{1,0:T(8,128)S(1)} %add.191), channel_id=1, source_target_pairs={{0,1},{1,0},{8,9},{9,8},{16,17},{17,16},{24,25},{25,24},{4,5},{5,4... | collective-permute-start | bytes 393224 | tf_op jit(solution)/shard_map/ppermute | solution.py:89
  51.3 10.1 %collective-permute-start.33 = (f32[256,128]{1,0:T(8,128)S(1)}, f32[256,128]{1,0:T(8,128)S(1)}, u32[]{:S(2)}, u32[]{:S(2)}) collective-permute-start(f32[256,128]{1,0:T(8,128)S(1)} %get-tuple-element.20.refs_0_), channel_id=1, source_target_pairs={{0,8},{1,9},{8,0},{9,1},{16,24},{17,25},{24,16},{25,17},{4,12},{5,... | collective-permute-start | bytes 393224 | tf_op jit(solution)/shard_map/ppermute | solution.py:89
  59.3 10.1 %collective-permute-start.17 = (f32[256,128]{1,0:T(8,128)S(1)}, f32[256,128]{1,0:T(8,128)S(1)}, u32[]{:S(2)}, u32[]{:S(2)}) collective-permute-start(f32[256,128]{1,0:T(8,128)S(1)} %get-tuple-element.19.refs_0_), channel_id=1, source_target_pairs={{0,4},{1,5},{8,12},{9,13},{16,20},{17,21},{24,28},{25,29},{4,0},{5... | collective-permute-start | bytes 393224 | tf_op jit(solution)/shard_map/ppermute | solution.py:89
  61.4 7.9 %collective-permute-start.34 = (f32[256,128]{1,0:T(8,128)S(1)}, f32[256,128]{1,0:T(8,128)S(1)}, u32[]{:S(2)}, u32[]{:S(2)}) collective-permute-start(f32[256,128]{1,0:T(8,128)S(1)} %collective-permute-done.33.refs_2_), channel_id=1, source_target_pairs={{0,4},{1,5},{8,12},{9,13},{16,20},{17,21},{24,28},{25,29},{4,0},{5... | collective-permute-start | bytes 393224 | tf_op jit(solution)/shard_map/ppermute | solution.py:89
  63.1 7.5 %collective-permute-start.19 = (f32[256,128]{1,0:T(8,128)S(1)}, f32[256,128]{1,0:T(8,128)S(1)}, u32[]{:S(2)}, u32[]{:S(2)}) collective-permute-start(f32[256,128]{1,0:T(8,128)S(1)} %collective-permute-done.18.refs_2_), channel_id=1, source_target_pairs={{0,4},{1,5},{8,12},{9,13},{16,20},{17,21},{24,28},{25,29},{4,0},{5... | collective-permute-start | bytes 393224 | tf_op jit(solution)/shard_map/ppermute | solution.py:89
  75.2 10.2 %collective-permute-start.22 = (f32[256,128]{1,0:T(8,128)S(1)}, f32[256,128]{1,0:T(8,128)S(1)}, u32[]{:S(2)}, u32[]{:S(2)}) collective-permute-start(f32[256,128]{1,0:T(8,128)S(1)} %add_bitcast_fusion.7), channel_id=1, source_target_pairs={{0,2},{1,3},{8,10},{9,11},{16,18},{17,19},{24,26},{25,27},{4,6},{5... | collective-permute-start | bytes 393224 | tf_op jit(solution)/shard_map/ppermute | solution.py:89
  80.0 8.1 %collective-permute-start.38 = (f32[256,128]{1,0:T(8,128)S(1)}, f32[256,128]{1,0:T(8,128)S(1)}, u32[]{:S(2)}, u32[]{:S(2)}) collective-permute-start(f32[256,128]{1,0:T(8,128)S(1)} %bitcast_subtract_fusion.2), channel_id=1, source_target_pairs={{0,16},{1,17},{8,24},{9,25},{4,20},{5,21},{12,28},{13,29},{18,2},{... | collective-permute-start | bytes 393224 | tf_op jit(solution)/shard_map/ppermute | solution.py:89
  85.4 10.0 %collective-permute-start.23 = (f32[256,128]{1,0:T(8,128)S(1)}, f32[256,128]{1,0:T(8,128)S(1)}, u32[]{:S(2)}, u32[]{:S(2)}) collective-permute-start(f32[256,128]{1,0:T(8,128)S(1)} %bitcast_subtract_fusion.3), channel_id=1, source_target_pairs={{0,16},{1,17},{8,24},{9,25},{4,20},{5,21},{12,28},{13,29},{18,2},{... | collective-permute-start | bytes 393224 | tf_op jit(solution)/shard_map/ppermute | solution.py:89
  88.2 10.4 %collective-permute-start.40 = (f32[256,128]{1,0:T(8,128)S(1)}, f32[256,128]{1,0:T(8,128)S(1)}, u32[]{:S(2)}, u32[]{:S(2)}) collective-permute-start(f32[256,128]{1,0:T(8,128)S(1)} %broadcast_select_fusion.4.refs_0_), channel_id=1, source_target_pairs={{0,8},{1,9},{8,0},{9,1},{16,24},{17,25},{24,16},{25,17},{4,12},{5,... | collective-permute-start | bytes 393224 | tf_op jit(solution)/shard_map/ppermute | solution.py:89
  94.8 12.4 %collective-permute-start.39 = (f32[256,128]{1,0:T(8,128)S(1)}, f32[256,128]{1,0:T(8,128)S(1)}, u32[]{:S(2)}, u32[]{:S(2)}) collective-permute-start(f32[256,128]{1,0:T(8,128)S(1)} %broadcast_select_fusion.4.refs_0_), channel_id=1, source_target_pairs={{0,4},{1,5},{8,12},{9,13},{16,20},{17,21},{24,28},{25,29},{4,0},{5... | collective-permute-start | bytes 393224 | tf_op jit(solution)/shard_map/ppermute | solution.py:89
  96.2 7.8 %collective-permute-start.24 = (f32[256,128]{1,0:T(8,128)S(1)}, f32[256,128]{1,0:T(8,128)S(1)}, u32[]{:S(2)}, u32[]{:S(2)}) collective-permute-start(f32[256,128]{1,0:T(8,128)S(1)} %broadcast_select_fusion.6.refs_0_), channel_id=1, source_target_pairs={{0,4},{1,5},{8,12},{9,13},{16,20},{17,21},{24,28},{25,29},{4,0},{5... | collective-permute-start | bytes 393224 | tf_op jit(solution)/shard_map/ppermute | solution.py:89
  98.5 8.6 %collective-permute-start.41 = (f32[256,128]{1,0:T(8,128)S(1)}, f32[256,128]{1,0:T(8,128)S(1)}, u32[]{:S(2)}, u32[]{:S(2)}) collective-permute-start(f32[256,128]{1,0:T(8,128)S(1)} %collective-permute-done.40.refs_2_), channel_id=1, source_target_pairs={{0,4},{1,5},{8,12},{9,13},{16,20},{17,21},{24,28},{25,29},{4,0},{5... | collective-permute-start | bytes 393224 | tf_op jit(solution)/shard_map/ppermute | solution.py:89
  112.5 10.7 %collective-permute-start.44 = (f32[256,128]{1,0:T(8,128)S(1)}, f32[256,128]{1,0:T(8,128)S(1)}, u32[]{:S(2)}, u32[]{:S(2)}) collective-permute-start(f32[256,128]{1,0:T(8,128)S(1)} %add_bitcast_fusion.4), channel_id=1, source_target_pairs={{0,2},{1,3},{8,10},{9,11},{16,18},{17,19},{24,26},{25,27},{4,6},{5... | collective-permute-start | bytes 393224 | tf_op jit(solution)/shard_map/ppermute | solution.py:89
  117.7 7.9 %collective-permute-start.51 = (f32[256,128]{1,0:T(8,128)S(1)}, f32[256,128]{1,0:T(8,128)S(1)}, u32[]{:S(2)}, u32[]{:S(2)}) collective-permute-start(f32[256,128]{1,0:T(8,128)S(1)} %add.203), channel_id=1, source_target_pairs={{0,16},{1,17},{8,24},{9,25},{4,20},{5,21},{12,28},{13,29},{18,2},{... | collective-permute-start | bytes 393224 | tf_op jit(solution)/shard_map/ppermute | solution.py:89
  123.2 8.5 %collective-permute-start.46 = (f32[256,128]{1,0:T(8,128)S(1)}, f32[256,128]{1,0:T(8,128)S(1)}, u32[]{:S(2)}, u32[]{:S(2)}) collective-permute-start(f32[256,128]{1,0:T(8,128)S(1)} %add.209), channel_id=1, source_target_pairs={{0,16},{1,17},{8,24},{9,25},{4,20},{5,21},{12,28},{13,29},{18,2},{... | collective-permute-start | bytes 393224 | tf_op jit(solution)/shard_map/ppermute | solution.py:89
  125.7 8.5 %collective-permute-start.53 = (f32[256,128]{1,0:T(8,128)S(1)}, f32[256,128]{1,0:T(8,128)S(1)}, u32[]{:S(2)}, u32[]{:S(2)}) collective-permute-start(f32[256,128]{1,0:T(8,128)S(1)} %get-tuple-element.17.refs_0_), channel_id=1, source_target_pairs={{0,8},{1,9},{8,0},{9,1},{16,24},{17,25},{24,16},{25,17},{4,12},{5,... | collective-permute-start | bytes 393224 | tf_op jit(solution)/shard_map/ppermute | solution.py:89
  133.3 9.4 %collective-permute-start.47 = (f32[256,128]{1,0:T(8,128)S(1)}, f32[256,128]{1,0:T(8,128)S(1)}, u32[]{:S(2)}, u32[]{:S(2)}) collective-permute-start(f32[256,128]{1,0:T(8,128)S(1)} %get-tuple-element.18.refs_0_), channel_id=1, source_target_pairs={{0,4},{1,5},{8,12},{9,13},{16,20},{17,21},{24,28},{25,29},{4,0},{5... | collective-permute-start | bytes 393224 | tf_op jit(solution)/shard_map/ppermute | solution.py:89
  134.2 8.4 %collective-permute-start.54 = (f32[256,128]{1,0:T(8,128)S(1)}, f32[256,128]{1,0:T(8,128)S(1)}, u32[]{:S(2)}, u32[]{:S(2)}) collective-permute-start(f32[256,128]{1,0:T(8,128)S(1)} %collective-permute-done.53.refs_2_), channel_id=1, source_target_pairs={{0,4},{1,5},{8,12},{9,13},{16,20},{17,21},{24,28},{25,29},{4,0},{5... | collective-permute-start | bytes 393224 | tf_op jit(solution)/shard_map/ppermute | solution.py:89
  136.8 7.5 %collective-permute-start.49 = (f32[256,128]{1,0:T(8,128)S(1)}, f32[256,128]{1,0:T(8,128)S(1)}, u32[]{:S(2)}, u32[]{:S(2)}) collective-permute-start(f32[256,128]{1,0:T(8,128)S(1)} %collective-permute-done.48.refs_2_), channel_id=1, source_target_pairs={{0,4},{1,5},{8,12},{9,13},{16,20},{17,21},{24,28},{25,29},{4,0},{5... | collective-permute-start | bytes 393224 | tf_op jit(solution)/shard_map/ppermute | solution.py:89
  162.1 9.3 %collective-permute-start.65 = (f32[256,128]{1,0:T(8,128)S(1)}, f32[256,128]{1,0:T(8,128)S(1)}, u32[]{:S(2)}, u32[]{:S(2)}) collective-permute-start(f32[256,128]{1,0:T(8,128)S(1)} %get-tuple-element.3), channel_id=1, source_target_pairs={{0,16},{1,17},{8,24},{9,25},{4,20},{5,21},{12,28},{13,29},{18,2},{... | collective-permute-start | bytes 393224 | tf_op jit(solution)/shard_map/ppermute | solution.py:89
  167.5 10.5 %collective-permute-start.58 = (f32[256,128]{1,0:T(8,128)S(1)}, f32[256,128]{1,0:T(8,128)S(1)}, u32[]{:S(2)}, u32[]{:S(2)}) collective-permute-start(f32[256,128]{1,0:T(8,128)S(1)} %get-tuple-element.4), channel_id=1, source_target_pairs={{0,16},{1,17},{8,24},{9,25},{4,20},{5,21},{12,28},{13,29},{18,2},{... | collective-permute-start | bytes 393224 | tf_op jit(solution)/shard_map/ppermute | solution.py:89
  171.4 9.6 %collective-permute-start.67 = (f32[256,128]{1,0:T(8,128)S(1)}, f32[256,128]{1,0:T(8,128)S(1)}, u32[]{:S(2)}, u32[]{:S(2)}) collective-permute-start(f32[256,128]{1,0:T(8,128)S(1)} %broadcast_select_fusion.refs_0_), channel_id=1, source_target_pairs={{0,8},{1,9},{8,0},{9,1},{16,24},{17,25},{24,16},{25,17},{4,12},{5,... | collective-permute-start | bytes 393224 | tf_op jit(solution)/shard_map/ppermute | solution.py:89
  178.6 9.6 %collective-permute-start.59 = (f32[256,128]{1,0:T(8,128)S(1)}, f32[256,128]{1,0:T(8,128)S(1)}, u32[]{:S(2)}, u32[]{:S(2)}) collective-permute-start(f32[256,128]{1,0:T(8,128)S(1)} %broadcast_select_fusion.1.refs_0_), channel_id=1, source_target_pairs={{0,4},{1,5},{8,12},{9,13},{16,20},{17,21},{24,28},{25,29},{4,0},{5... | collective-permute-start | bytes 393224 | tf_op jit(solution)/shard_map/ppermute | solution.py:89
  196.6 7.5 %collective-permute-start.71 = (f32[256,128]{1,0:T(8,128)S(1)}, f32[256,128]{1,0:T(8,128)S(1)}, u32[]{:S(2)}, u32[]{:S(2)}) collective-permute-start(f32[256,128]{1,0:T(8,128)S(1)} %add_bitcast_fusion.1), channel_id=1, source_target_pairs={{0,2},{1,3},{8,10},{9,11},{16,18},{17,19},{24,26},{25,27},{4,6},{5... | collective-permute-start | bytes 393224 | tf_op jit(solution)/shard_map/ppermute | solution.py:89
  (58 other events, 510.0 us)

commit v3 on v2

--- a/solution.py
+++ b/solution.py
@@ -82,7 +82,7 @@
 TO_Y = [(flat(x, y, z, k), flat(x, 1 - y, z, k)) for x, y, z, k in PLACES]
 TO_Z = [(flat(x, y, z, k), flat(x, y, z ^ 1, k)) for x, y, z, k in PLACES]
 TO_YZ = [(flat(x, y, z, k), flat(x, 1 - y, z ^ 1, k)) for x, y, z, k in PLACES]
-TO_FAR = [(flat(x, y, z, k), flat(x, y, z ^ 2, k)) for x, y, z, k in PLACES if z // 2 == x]
+TO_FAR = [(flat(x, y, z, k), flat(x, y, 3 - z, k)) for x, y, z, k in PLACES if z // 2 == x]
 
 
 def send(value, pairs):
@@ -108,15 +108,24 @@
     return jnp.stack([jnp.where(first, mine, other), jnp.where(first, other, mine)])
 
 
-def spread(mine):
+def gate(value, after):
+    return lax.optimization_barrier((value, after))[0]
+
+
+def spread(mine, make=None):
     x, y, z, k = place()
     far = send(mine, TO_FAR)
     own = jnp.where(z // 2 == x, mine, far)
+    made = None
+    if make is not None:
+        made = make(mine)
+        own = gate(own, made)
     beside, above = send(own, TO_Y), send(own, TO_Z)
     across = send(above, TO_Y)
-    same = (z % 2) == k
+    same = jnp.where(z // 2 == x, z % 2, 1 - z % 2) == k
     swapped = send(jnp.stack([jnp.where(same, above, own), jnp.where(same, across, beside)]), TO_CORE)
-    return own, beside, above, across, swapped
+    pieces = (own, beside, above, across, swapped)
+    return pieces if make is None else (pieces, made)
 
 
 def split(value):
@@ -141,7 +150,8 @@
     def _():
         r, c = lax.axis_index("rows"), lax.axis_index("cols")
         y, k = lax.rem(r, 2), lax.rem(c, 2)
-        same = lax.rem(r // 2, 2) == k
+        z = r // 2
+        same = jnp.where(z // 2 == c // 2, lax.rem(z, 2), 1 - lax.rem(z, 2)) == k
 
         def put(value, y_of, half):
             row = half * (2 * PIECE) + y_of * PIECE if leafwise else y_of * (2 * PIECE) + half * PIECE
@@ -274,19 +284,23 @@
         mine, other = halve(part.reshape(2, PIECE, n))
         right = lax.dynamic_index_in_dim(right_mid[s].reshape(2, PIECE, n), k, 0, False)
         mid_half.append(right - (mine + other))
-    resid_pieces = [spread(h) for h in mid_half]
-
-    root_part = None
+    root_part, resid_pieces = None, []
     for s in streams:
-        root_part = apply(
-            leaf_pieces[s],
-            pair(leaf_to_root, 256, s),
-            1024,
-            256,
-            mask=mask_lr[2 * s : 2 * s + 2],
-            add=root_part,
-            leafwise=True,
-        )
+
+        def make(mine, s=s, before=root_part):
+            p = leaf_pieces[s]
+            return apply(
+                (gate(p[0], mine),) + p[1:],
+                [(pltpu.with_memory_space_constraint(t[0], pltpu.MemorySpace.HBM),) + t[1:] for t in pair(leaf_to_root, 256, s)],
+                1024,
+                256,
+                mask=mask_lr[2 * s : 2 * s + 2],
+                add=before,
+                leafwise=True,
+            )
+
+        pieces, root_part = spread(mid_half[s], make)
+        resid_pieces.append(pieces)
 
     solved_half = []
     for s in streams:
@@ -297,13 +311,13 @@
     solved_mid = [both_halves(h) for h in solved_half]
 
     root_part = apply(
-        mid_pieces[0], one(mid_to_root, 256, 0), 1024, 256, mask=mask_mr[0:1], add=root_part
+        mid_pieces[0], one(mid_to_root[0:1], 256, 0), 1024, 256, mask=mask_mr[0:1], add=root_part
     )
     root_half = []
     for g in (0, 1):
         part = apply(
             mid_pieces[1],
-            one(mid_to_root, 256, 1),
+            one(mid_to_root[1:2], 256, 0),
             512,
             256,
             first_tile=2 * g,

time: 207 us -> 201 us (0.971)
  waiting for transfers between devices: 70.7 us -> 59.4 us
  starting transfers between devices: 107 us -> 99.3 us
  local copies, waits for them, and re-layouts: 4.29 us -> 10.8 us
  Pallas kernels: 17.9 us -> 22.2 us
    ppermute x76, waiting for transfers between devices: 70.7 us -> 59.4 us  [send(): return lax.ppermute(value, AXES, pairs)]
    slice x3 -> x4, local copies, waits for them, and re-layouts: 0.14 us -> 8.63 us  [the longest x1 8.49 us: grid_body(): mid_to_root[0:1]]
    ppermute x76, starting transfers between devices: 107 us -> 99.3 us  [send(): return lax.ppermute(value, AXES, pairs)]
    pallas_call x14, Pallas kernels: 17.9 us -> 22.2 us  [apply(): pl.pallas_call(functools.partial(kernel_body, tuple(((t[3], t[4]) for t i...]
  transfers between devices with their start and end apart: 76 -> 76, of which waited for: 39 -> 31; matrix products, arithmetic and copies ran while one was open for 3% -> 8% of each run, Pallas kernels for 8% -> 10%
where the time goes in v3:
time: 201 us
  starting transfers between devices  99.3 us (49%)
  waiting for transfers between devices  59.4 us (30%)
  Pallas kernels  22.2 us (11%)
  local copies, waits for them, and re-layouts  10.8 us (5%)
  other arithmetic  7.31 us (4%)
    ppermute x76, starting transfers between devices, send(): return lax.ppermute(value, AXES, pairs)  99.3 us
    ppermute x76, waiting for transfers between devices, send(): return lax.ppermute(value, AXES, pairs)  59.4 us
    pallas_call x14, Pallas kernels, apply(): pl.pallas_call(functools.partial(kernel_body, tuple(((t[3], t[4]) for t i...  22.2 us
    slice x1, local copies, waits for them, and re-layouts, grid_body(): mid_to_root[0:1]  8.49 us
  transfers between devices with their start and end apart: 76, of which 31 were waited for; matrix products, arithmetic and copies ran while one was open for 8% of the time, Pallas kernels for 10%

profile of v3, /device:TPU:0, one launch (start us, length us, event | category | flops | bytes accessed | tf_op | source)
XLA Modules:
  0.0 200.7 jit_solution(10989117671798173249)
XLA Ops:
  1.7 7.0 %collective-permute-start = (f32[256,128]{1,0:T(8,128)S(1)}, f32[256,128]{1,0:T(8,128)S(1)}, u32[]{:S(2)}, u32[]{:S(2)}) collective-permute-start(f32[256,128]{1,0:T(8,128)S(1)} %get-tuple-element.17), channel_id=1, source_target_pairs={{0,24},{1,25},{8,16},{9,17},{4,28},{5,29},{12,20},{13,21},{18,10},... | collective-permute-start | bytes 393224 | tf_op jit(solution)/shard_map/ppermute | solution.py:89
  10.1 8.5 %fusion.1 = (f32[1,1024,1024]{2,1,0:T(8,128)}, f32[1,1024,1024]{2,1,0:T(8,128)}) fusion(f32[2,1024,1024]{2,1,0:T(8,128)} %param.20), kind=kLoop, calls=%fused_computation.81 | loop fusion | bytes 16777216 | tf_op jit(solution)/shard_map/slice | solution.py:314
  22.8 2.2 %collective-permute-done.2.refs_2_ = f32[256,128]{1,0:T(8,128)S(1)} collective-permute-done((f32[256,128]{1,0:T(8,128)S(1)}, f32[256,128]{1,0:T(8,128)S(1)}, u32[]{:S(2)}, u32[]{:S(2)}) %collective-permute-start.2) | collective-permute-done | bytes 131104 | tf_op jit(solution)/shard_map/ppermute | solution.py:89
  28.0 2.8 %collective-permute-done.3.refs_3_ = f32[256,128]{1,0:T(8,128)S(1)} collective-permute-done((f32[256,128]{1,0:T(8,128)S(1)}, f32[256,128]{1,0:T(8,128)S(1)}, u32[]{:S(2)}, u32[]{:S(2)}) %collective-permute-start.3) | collective-permute-done | bytes 131104 | tf_op jit(solution)/shard_map/ppermute | solution.py:89
  38.8 3.0 %collective-permute-done.6 = f32[256,128]{1,0:T(8,128)S(1)} collective-permute-done((f32[256,128]{1,0:T(8,128)S(1)}, f32[256,128]{1,0:T(8,128)S(1)}, u32[]{:S(2)}, u32[]{:S(2)}) %collective-permute-start.6) | collective-permute-done | bytes 131104 | tf_op jit(solution)/shard_map/ppermute | solution.py:89
  41.8 3.7 %collective-permute-start.16 = (f32[256,128]{1,0:T(8,128)S(1)}, f32[256,128]{1,0:T(8,128)S(1)}, u32[]{:S(2)}, u32[]{:S(2)}) collective-permute-start(f32[256,128]{1,0:T(8,128)S(1)} %add.201), channel_id=1, source_target_pairs={{0,24},{1,25},{8,16},{9,17},{4,28},{5,29},{12,20},{13,21},{18,10},... | collective-permute-start | bytes 393224 | tf_op jit(solution)/shard_map/ppermute | solution.py:89
  48.0 5.1 %collective-permute-start.18 = (f32[256,128]{1,0:T(8,128)S(1)}, f32[256,128]{1,0:T(8,128)S(1)}, u32[]{:S(2)}, u32[]{:S(2)}) collective-permute-start(f32[256,128]{1,0:T(8,128)S(1)} %get-tuple-element.7.refs_0_), channel_id=1, source_target_pairs={{0,8},{1,9},{8,0},{9,1},{16,24},{17,25},{24,16},{25,17},{4,12},{5,... | collective-permute-start | bytes 393224 | tf_op jit(solution)/shard_map/ppermute | solution.py:89
  53.1 2.1 %collective-permute-start.17 = (f32[256,128]{1,0:T(8,128)S(1)}, f32[256,128]{1,0:T(8,128)S(1)}, u32[]{:S(2)}, u32[]{:S(2)}) collective-permute-start(f32[256,128]{1,0:T(8,128)S(1)} %get-tuple-element.7.refs_0_), channel_id=1, source_target_pairs={{0,4},{1,5},{8,12},{9,13},{16,20},{17,21},{24,28},{25,29},{4,0},{5... | collective-permute-start | bytes 393224 | tf_op jit(solution)/shard_map/ppermute | solution.py:89
  61.0 3.9 %collective-permute-done.19.refs_3_ = f32[256,128]{1,0:T(8,128)S(1)} collective-permute-done((f32[256,128]{1,0:T(8,128)S(1)}, f32[256,128]{1,0:T(8,128)S(1)}, u32[]{:S(2)}, u32[]{:S(2)}) %collective-permute-start.19) | collective-permute-done | bytes 131104 | tf_op jit(solution)/shard_map/ppermute | solution.py:89
  70.6 3.6 %collective-permute-start.22 = (f32[256,128]{1,0:T(8,128)S(1)}, f32[256,128]{1,0:T(8,128)S(1)}, u32[]{:S(2)}, u32[]{:S(2)}) collective-permute-start(f32[256,128]{1,0:T(8,128)S(1)} %add_bitcast_fusion.7), channel_id=1, source_target_pairs={{0,2},{1,3},{8,10},{9,11},{16,18},{17,19},{24,26},{25,27},{4,6},{5... | collective-permute-start | bytes 393224 | tf_op jit(solution)/shard_map/ppermute | solution.py:89
  75.7 2.6 %collective-permute-done.22 = f32[256,128]{1,0:T(8,128)S(1)} collective-permute-done((f32[256,128]{1,0:T(8,128)S(1)}, f32[256,128]{1,0:T(8,128)S(1)}, u32[]{:S(2)}, u32[]{:S(2)}) %collective-permute-start.22) | collective-permute-done | bytes 131104 | tf_op jit(solution)/shard_map/ppermute | solution.py:89
  78.3 4.2 %collective-permute-start.23 = (f32[256,128]{1,0:T(8,128)S(1)}, f32[256,128]{1,0:T(8,128)S(1)}, u32[]{:S(2)}, u32[]{:S(2)}) collective-permute-start(f32[256,128]{1,0:T(8,128)S(1)} %bitcast_subtract_fusion.3), channel_id=1, source_target_pairs={{0,24},{1,25},{8,16},{9,17},{4,28},{5,29},{12,20},{13,21},{18,10},... | collective-permute-start | bytes 393224 | tf_op jit(solution)/shard_map/ppermute | solution.py:89
  82.6 2.2 %collective-permute-start.38 = (f32[256,128]{1,0:T(8,128)S(1)}, f32[256,128]{1,0:T(8,128)S(1)}, u32[]{:S(2)}, u32[]{:S(2)}) collective-permute-start(f32[256,128]{1,0:T(8,128)S(1)} %bitcast_subtract_fusion.2), channel_id=1, source_target_pairs={{0,24},{1,25},{8,16},{9,17},{4,28},{5,29},{12,20},{13,21},{18,10},... | collective-permute-start | bytes 393224 | tf_op jit(solution)/shard_map/ppermute | solution.py:89
  84.8 4.0 %shard_map.142.refs_8_ = f32[1024,128]{1,0:T(8,128)S(1)} custom-call(f32[256,128]{1,0:T(8,128)S(1)} %get-tuple-element.7.refs_0_, f32[256,128]{1,0:T(8,128)S(1)} %collective-permute-done.17.refs_1_, f32[256,128]{1,0:T(8,128)S(1)} %collective-permute-done.18.refs_2_, f32[256,128]{1,0:T(8,128)S(1)} %collective-permute-done.19.refs_3_, ...), custom_call_target="tpu_custom_call" | custom-call | flops 1073741824 | bytes 4194304 | tf_op jit(solution)/shard_map/pallas_call | solution.py:221
  88.8 4.1 %shard_map.145.refs_7_ = f32[1024,128]{1,0:T(8,128)S(1)} custom-call(f32[256,128]{1,0:T(8,128)S(1)} %get-tuple-element.9.refs_0_, f32[256,128]{1,0:T(8,128)S(1)} %collective-permute-done.32.refs_1_, f32[256,128]{1,0:T(8,128)S(1)} %collective-permute-done.33.refs_2_, f32[256,128]{1,0:T(8,128)S(1)} %collective-permute-done.34.refs_3_, ...), custom_call_target="tpu_custom_call" | custom-call | flops 1073741824 | bytes 4194304 | tf_op jit(solution)/shard_map/pallas_call | solution.py:221
  97.2 2.1 %collective-permute-done.25.refs_2_ = f32[256,128]{1,0:T(8,128)S(1)} collective-permute-done((f32[256,128]{1,0:T(8,128)S(1)}, f32[256,128]{1,0:T(8,128)S(1)}, u32[]{:S(2)}, u32[]{:S(2)}) %collective-permute-start.25) | collective-permute-done | bytes 131104 | tf_op jit(solution)/shard_map/ppermute | solution.py:89
  102.5 2.6 %collective-permute-done.26.refs_3_ = f32[256,128]{1,0:T(8,128)S(1)} collective-permute-done((f32[256,128]{1,0:T(8,128)S(1)}, f32[256,128]{1,0:T(8,128)S(1)}, u32[]{:S(2)}, u32[]{:S(2)}) %collective-permute-start.26) | collective-permute-done | bytes 131104 | tf_op jit(solution)/shard_map/ppermute | solution.py:89
  111.8 4.1 %collective-permute-done.29 = f32[256,128]{1,0:T(8,128)S(1)} collective-permute-done((f32[256,128]{1,0:T(8,128)S(1)}, f32[256,128]{1,0:T(8,128)S(1)}, u32[]{:S(2)}, u32[]{:S(2)}) %collective-permute-start.29) | collective-permute-done | bytes 131104 | tf_op jit(solution)/shard_map/ppermute | solution.py:89
  116.1 3.6 %collective-permute-start.51 = (f32[256,128]{1,0:T(8,128)S(1)}, f32[256,128]{1,0:T(8,128)S(1)}, u32[]{:S(2)}, u32[]{:S(2)}) collective-permute-start(f32[256,128]{1,0:T(8,128)S(1)} %add.214), channel_id=1, source_target_pairs={{0,24},{1,25},{8,16},{9,17},{4,28},{5,29},{12,20},{13,21},{18,10},... | collective-permute-start | bytes 393224 | tf_op jit(solution)/shard_map/ppermute | solution.py:89
  120.0 2.4 %collective-permute-start.46 = (f32[256,128]{1,0:T(8,128)S(1)}, f32[256,128]{1,0:T(8,128)S(1)}, u32[]{:S(2)}, u32[]{:S(2)}) collective-permute-start(f32[256,128]{1,0:T(8,128)S(1)} %add.220), channel_id=1, source_target_pairs={{0,24},{1,25},{8,16},{9,17},{4,28},{5,29},{12,20},{13,21},{18,10},... | collective-permute-start | bytes 393224 | tf_op jit(solution)/shard_map/ppermute | solution.py:89
  123.5 6.3 %collective-permute-start.53 = (f32[256,128]{1,0:T(8,128)S(1)}, f32[256,128]{1,0:T(8,128)S(1)}, u32[]{:S(2)}, u32[]{:S(2)}) collective-permute-start(f32[256,128]{1,0:T(8,128)S(1)} %get-tuple-element.27.refs_0_), channel_id=1, source_target_pairs={{0,8},{1,9},{8,0},{9,1},{16,24},{17,25},{24,16},{25,17},{4,12},{5,... | collective-permute-start | bytes 393224 | tf_op jit(solution)/shard_map/ppermute | solution.py:89
  137.0 4.4 %collective-permute-done.54.refs_3_ = f32[256,128]{1,0:T(8,128)S(1)} collective-permute-done((f32[256,128]{1,0:T(8,128)S(1)}, f32[256,128]{1,0:T(8,128)S(1)}, u32[]{:S(2)}, u32[]{:S(2)}) %collective-permute-start.54) | collective-permute-done | bytes 131104 | tf_op jit(solution)/shard_map/ppermute | solution.py:89
  151.6 2.9 %collective-permute-done.57 = f32[256,128]{1,0:T(8,128)S(1)} collective-permute-done((f32[256,128]{1,0:T(8,128)S(1)}, f32[256,128]{1,0:T(8,128)S(1)}, u32[]{:S(2)}, u32[]{:S(2)}) %collective-permute-start.57) | collective-permute-done | bytes 131104 | tf_op jit(solution)/shard_map/ppermute | solution.py:89
  154.5 2.5 %collective-permute-done.64 = f32[256,128]{1,0:T(8,128)S(1)} collective-permute-done((f32[256,128]{1,0:T(8,128)S(1)}, f32[256,128]{1,0:T(8,128)S(1)}, u32[]{:S(2)}, u32[]{:S(2)}) %collective-permute-start.64) | collective-permute-done | bytes 131104 | tf_op jit(solution)/shard_map/ppermute | solution.py:89
  157.1 5.0 %collective-permute-start.65 = (f32[256,128]{1,0:T(8,128)S(1)}, f32[256,128]{1,0:T(8,128)S(1)}, u32[]{:S(2)}, u32[]{:S(2)}) collective-permute-start(f32[256,128]{1,0:T(8,128)S(1)} %get-tuple-element.13), channel_id=1, source_target_pairs={{0,24},{1,25},{8,16},{9,17},{4,28},{5,29},{12,20},{13,21},{18,10},... | collective-permute-start | bytes 393224 | tf_op jit(solution)/shard_map/ppermute | solution.py:89
  163.4 2.6 %collective-permute-done.65 = f32[256,128]{1,0:T(8,128)S(1)} collective-permute-done((f32[256,128]{1,0:T(8,128)S(1)}, f32[256,128]{1,0:T(8,128)S(1)}, u32[]{:S(2)}, u32[]{:S(2)}) %collective-permute-start.65) | collective-permute-done | bytes 131104 | tf_op jit(solution)/shard_map/ppermute | solution.py:89
  166.0 4.7 %collective-permute-start.67 = (f32[256,128]{1,0:T(8,128)S(1)}, f32[256,128]{1,0:T(8,128)S(1)}, u32[]{:S(2)}, u32[]{:S(2)}) collective-permute-start(f32[256,128]{1,0:T(8,128)S(1)} %broadcast_select_fusion.refs_0_), channel_id=1, source_target_pairs={{0,8},{1,9},{8,0},{9,1},{16,24},{17,25},{24,16},{25,17},{4,12},{5,... | collective-permute-start | bytes 393224 | tf_op jit(solution)/shard_map/ppermute | solution.py:89
  177.9 3.8 %collective-permute-done.68.refs_3_ = f32[256,128]{1,0:T(8,128)S(1)} collective-permute-done((f32[256,128]{1,0:T(8,128)S(1)}, f32[256,128]{1,0:T(8,128)S(1)}, u32[]{:S(2)}, u32[]{:S(2)}) %collective-permute-start.68) | collective-permute-done | bytes 131104 | tf_op jit(solution)/shard_map/ppermute | solution.py:89
  183.3 2.3 %shard_map.150.refs_7_ = f32[1024,128]{1,0:T(8,128)S(1)} custom-call(f32[256,128]{1,0:T(8,128)S(1)} %broadcast_select_fusion.refs_0_, f32[256,128]{1,0:T(8,128)S(1)} %collective-permute-done.66.refs_1_, f32[256,128]{1,0:T(8,128)S(1)} %collective-permute-done.67.refs_2_, f32[256,128]{1,0:T(8,128)S(1)} %collective-permute-done.68.refs_3_, ...), custom_call_target="tpu_custom_call" | custom-call | flops 1073741824 | bytes 4194304 | tf_op jit(solution)/shard_map/pallas_call | solution.py:221
  189.0 2.2 %collective-permute-start.71 = (f32[256,128]{1,0:T(8,128)S(1)}, f32[256,128]{1,0:T(8,128)S(1)}, u32[]{:S(2)}, u32[]{:S(2)}) collective-permute-start(f32[256,128]{1,0:T(8,128)S(1)} %add_bitcast_fusion.1), channel_id=1, source_target_pairs={{0,2},{1,3},{8,10},{9,11},{16,18},{17,19},{24,26},{25,27},{4,6},{5... | collective-permute-start | bytes 393224 | tf_op jit(solution)/shard_map/ppermute | solution.py:89
  193.3 2.3 %collective-permute-done.71 = f32[256,128]{1,0:T(8,128)S(1)} collective-permute-done((f32[256,128]{1,0:T(8,128)S(1)}, f32[256,128]{1,0:T(8,128)S(1)}, u32[]{:S(2)}, u32[]{:S(2)}) %collective-permute-start.71) | collective-permute-done | bytes 131104 | tf_op jit(solution)/shard_map/ppermute | solution.py:89
  195.6 2.4 %collective-permute-done.73 = f32[256,128]{1,0:T(8,128)S(1)} collective-permute-done((f32[256,128]{1,0:T(8,128)S(1)}, f32[256,128]{1,0:T(8,128)S(1)}, u32[]{:S(2)}, u32[]{:S(2)}) %collective-permute-start.73) | collective-permute-done | bytes 131104 | tf_op jit(solution)/shard_map/ppermute | solution.py:89
  (251 shorter events, 83.7 us)
Async XLA Ops:
  1.7 16.9 %collective-permute-start = (f32[256,128]{1,0:T(8,128)S(1)}, f32[256,128]{1,0:T(8,128)S(1)}, u32[]{:S(2)}, u32[]{:S(2)}) collective-permute-start(f32[256,128]{1,0:T(8,128)S(1)} %get-tuple-element.17), channel_id=1, source_target_pairs={{0,24},{1,25},{8,16},{9,17},{4,28},{5,29},{12,20},{13,21},{18,10},... | collective-permute-start | bytes 393224 | tf_op jit(solution)/shard_map/ppermute | solution.py:89
  8.6 11.6 %collective-permute-start.8 = (f32[256,128]{1,0:T(8,128)S(1)}, f32[256,128]{1,0:T(8,128)S(1)}, u32[]{:S(2)}, u32[]{:S(2)}) collective-permute-start(f32[256,128]{1,0:T(8,128)S(1)} %get-tuple-element.18), channel_id=1, source_target_pairs={{0,24},{1,25},{8,16},{9,17},{4,28},{5,29},{12,20},{13,21},{18,10},... | collective-permute-start | bytes 393224 | tf_op jit(solution)/shard_map/ppermute | solution.py:89
  18.7 9.3 %collective-permute-start.1 = (f32[256,128]{1,0:T(8,128)S(1)}, f32[256,128]{1,0:T(8,128)S(1)}, u32[]{:S(2)}, u32[]{:S(2)}) collective-permute-start(f32[256,128]{1,0:T(8,128)S(1)} %broadcast_select_fusion.9.refs_0_), channel_id=1, source_target_pairs={{0,4},{1,5},{8,12},{9,13},{16,20},{17,21},{24,28},{25,29},{4,0},{5... | collective-permute-start | bytes 393224 | tf_op jit(solution)/shard_map/ppermute | solution.py:89
  22.3 8.6 %collective-permute-start.9 = (f32[256,128]{1,0:T(8,128)S(1)}, f32[256,128]{1,0:T(8,128)S(1)}, u32[]{:S(2)}, u32[]{:S(2)}) collective-permute-start(f32[256,128]{1,0:T(8,128)S(1)} %broadcast_select_fusion.8.refs_0_), channel_id=1, source_target_pairs={{0,4},{1,5},{8,12},{9,13},{16,20},{17,21},{24,28},{25,29},{4,0},{5... | collective-permute-start | bytes 393224 | tf_op jit(solution)/shard_map/ppermute | solution.py:89
  37.7 7.8 %collective-permute-start.14 = (f32[256,128]{1,0:T(8,128)S(1)}, f32[256,128]{1,0:T(8,128)S(1)}, u32[]{:S(2)}, u32[]{:S(2)}) collective-permute-start(f32[256,128]{1,0:T(8,128)S(1)} %add_bitcast_fusion.8), channel_id=1, source_target_pairs={{0,2},{1,3},{8,10},{9,11},{16,18},{17,19},{24,26},{25,27},{4,6},{5... | collective-permute-start | bytes 393224 | tf_op jit(solution)/shard_map/ppermute | solution.py:89
  45.6 9.7 %collective-permute-start.15 = (f32[256,128]{1,0:T(8,128)S(1)}, f32[256,128]{1,0:T(8,128)S(1)}, u32[]{:S(2)}, u32[]{:S(2)}) collective-permute-start(f32[256,128]{1,0:T(8,128)S(1)} %add.205), channel_id=1, source_target_pairs={{0,1},{1,0},{8,9},{9,8},{16,17},{17,16},{24,25},{25,24},{4,5},{5,4... | collective-permute-start | bytes 393224 | tf_op jit(solution)/shard_map/ppermute | solution.py:89
  46.1 9.1 %collective-permute-start.31 = (f32[256,128]{1,0:T(8,128)S(1)}, f32[256,128]{1,0:T(8,128)S(1)}, u32[]{:S(2)}, u32[]{:S(2)}) collective-permute-start(f32[256,128]{1,0:T(8,128)S(1)} %add.205), channel_id=1, source_target_pairs={{0,24},{1,25},{8,16},{9,17},{4,28},{5,29},{12,20},{13,21},{18,10},... | collective-permute-start | bytes 393224 | tf_op jit(solution)/shard_map/ppermute | solution.py:89
  48.0 9.4 %collective-permute-start.18 = (f32[256,128]{1,0:T(8,128)S(1)}, f32[256,128]{1,0:T(8,128)S(1)}, u32[]{:S(2)}, u32[]{:S(2)}) collective-permute-start(f32[256,128]{1,0:T(8,128)S(1)} %get-tuple-element.7.refs_0_), channel_id=1, source_target_pairs={{0,8},{1,9},{8,0},{9,1},{16,24},{17,25},{24,16},{25,17},{4,12},{5,... | collective-permute-start | bytes 393224 | tf_op jit(solution)/shard_map/ppermute | solution.py:89
  53.1 7.9 %collective-permute-start.17 = (f32[256,128]{1,0:T(8,128)S(1)}, f32[256,128]{1,0:T(8,128)S(1)}, u32[]{:S(2)}, u32[]{:S(2)}) collective-permute-start(f32[256,128]{1,0:T(8,128)S(1)} %get-tuple-element.7.refs_0_), channel_id=1, source_target_pairs={{0,4},{1,5},{8,12},{9,13},{16,20},{17,21},{24,28},{25,29},{4,0},{5... | collective-permute-start | bytes 393224 | tf_op jit(solution)/shard_map/ppermute | solution.py:89
  55.7 9.4 %collective-permute-start.32 = (f32[256,128]{1,0:T(8,128)S(1)}, f32[256,128]{1,0:T(8,128)S(1)}, u32[]{:S(2)}, u32[]{:S(2)}) collective-permute-start(f32[256,128]{1,0:T(8,128)S(1)} %get-tuple-element.9.refs_0_), channel_id=1, source_target_pairs={{0,4},{1,5},{8,12},{9,13},{16,20},{17,21},{24,28},{25,29},{4,0},{5... | collective-permute-start | bytes 393224 | tf_op jit(solution)/shard_map/ppermute | solution.py:89
  57.4 7.5 %collective-permute-start.19 = (f32[256,128]{1,0:T(8,128)S(1)}, f32[256,128]{1,0:T(8,128)S(1)}, u32[]{:S(2)}, u32[]{:S(2)}) collective-permute-start(f32[256,128]{1,0:T(8,128)S(1)} %collective-permute-done.18.refs_2_), channel_id=1, source_target_pairs={{0,4},{1,5},{8,12},{9,13},{16,20},{17,21},{24,28},{25,29},{4,0},{5... | collective-permute-start | bytes 393224 | tf_op jit(solution)/shard_map/ppermute | solution.py:89
  70.6 7.7 %collective-permute-start.22 = (f32[256,128]{1,0:T(8,128)S(1)}, f32[256,128]{1,0:T(8,128)S(1)}, u32[]{:S(2)}, u32[]{:S(2)}) collective-permute-start(f32[256,128]{1,0:T(8,128)S(1)} %add_bitcast_fusion.7), channel_id=1, source_target_pairs={{0,2},{1,3},{8,10},{9,11},{16,18},{17,19},{24,26},{25,27},{4,6},{5... | collective-permute-start | bytes 393224 | tf_op jit(solution)/shard_map/ppermute | solution.py:89
  75.4 7.2 %collective-permute-start.37 = (f32[256,128]{1,0:T(8,128)S(1)}, f32[256,128]{1,0:T(8,128)S(1)}, u32[]{:S(2)}, u32[]{:S(2)}) collective-permute-start(f32[256,128]{1,0:T(8,128)S(1)} %add_bitcast_fusion.5), channel_id=1, source_target_pairs={{0,2},{1,3},{8,10},{9,11},{16,18},{17,19},{24,26},{25,27},{4,6},{5... | collective-permute-start | bytes 393224 | tf_op jit(solution)/shard_map/ppermute | solution.py:89
  78.3 14.6 %collective-permute-start.23 = (f32[256,128]{1,0:T(8,128)S(1)}, f32[256,128]{1,0:T(8,128)S(1)}, u32[]{:S(2)}, u32[]{:S(2)}) collective-permute-start(f32[256,128]{1,0:T(8,128)S(1)} %bitcast_subtract_fusion.3), channel_id=1, source_target_pairs={{0,24},{1,25},{8,16},{9,17},{4,28},{5,29},{12,20},{13,21},{18,10},... | collective-permute-start | bytes 393224 | tf_op jit(solution)/shard_map/ppermute | solution.py:89
  82.6 12.4 %collective-permute-start.38 = (f32[256,128]{1,0:T(8,128)S(1)}, f32[256,128]{1,0:T(8,128)S(1)}, u32[]{:S(2)}, u32[]{:S(2)}) collective-permute-start(f32[256,128]{1,0:T(8,128)S(1)} %bitcast_subtract_fusion.2), channel_id=1, source_target_pairs={{0,24},{1,25},{8,16},{9,17},{4,28},{5,29},{12,20},{13,21},{18,10},... | collective-permute-start | bytes 393224 | tf_op jit(solution)/shard_map/ppermute | solution.py:89
  93.1 9.4 %collective-permute-start.24 = (f32[256,128]{1,0:T(8,128)S(1)}, f32[256,128]{1,0:T(8,128)S(1)}, u32[]{:S(2)}, u32[]{:S(2)}) collective-permute-start(f32[256,128]{1,0:T(8,128)S(1)} %broadcast_select_fusion.6.refs_0_), channel_id=1, source_target_pairs={{0,4},{1,5},{8,12},{9,13},{16,20},{17,21},{24,28},{25,29},{4,0},{5... | collective-permute-start | bytes 393224 | tf_op jit(solution)/shard_map/ppermute | solution.py:89
  97.1 8.2 %collective-permute-start.39 = (f32[256,128]{1,0:T(8,128)S(1)}, f32[256,128]{1,0:T(8,128)S(1)}, u32[]{:S(2)}, u32[]{:S(2)}) collective-permute-start(f32[256,128]{1,0:T(8,128)S(1)} %broadcast_select_fusion.4.refs_0_), channel_id=1, source_target_pairs={{0,4},{1,5},{8,12},{9,13},{16,20},{17,21},{24,28},{25,29},{4,0},{5... | collective-permute-start | bytes 393224 | tf_op jit(solution)/shard_map/ppermute | solution.py:89
  111.0 8.8 %collective-permute-start.44 = (f32[256,128]{1,0:T(8,128)S(1)}, f32[256,128]{1,0:T(8,128)S(1)}, u32[]{:S(2)}, u32[]{:S(2)}) collective-permute-start(f32[256,128]{1,0:T(8,128)S(1)} %add_bitcast_fusion.4), channel_id=1, source_target_pairs={{0,2},{1,3},{8,10},{9,11},{16,18},{17,19},{24,26},{25,27},{4,6},{5... | collective-permute-start | bytes 393224 | tf_op jit(solution)/shard_map/ppermute | solution.py:89
  116.1 7.4 %collective-permute-start.51 = (f32[256,128]{1,0:T(8,128)S(1)}, f32[256,128]{1,0:T(8,128)S(1)}, u32[]{:S(2)}, u32[]{:S(2)}) collective-permute-start(f32[256,128]{1,0:T(8,128)S(1)} %add.214), channel_id=1, source_target_pairs={{0,24},{1,25},{8,16},{9,17},{4,28},{5,29},{12,20},{13,21},{18,10},... | collective-permute-start | bytes 393224 | tf_op jit(solution)/shard_map/ppermute | solution.py:89
  119.8 11.5 %collective-permute-start.45 = (f32[256,128]{1,0:T(8,128)S(1)}, f32[256,128]{1,0:T(8,128)S(1)}, u32[]{:S(2)}, u32[]{:S(2)}) collective-permute-start(f32[256,128]{1,0:T(8,128)S(1)} %add.220), channel_id=1, source_target_pairs={{0,1},{1,0},{8,9},{9,8},{16,17},{17,16},{24,25},{25,24},{4,5},{5,4... | collective-permute-start | bytes 393224 | tf_op jit(solution)/shard_map/ppermute | solution.py:89
  120.0 11.2 %collective-permute-start.46 = (f32[256,128]{1,0:T(8,128)S(1)}, f32[256,128]{1,0:T(8,128)S(1)}, u32[]{:S(2)}, u32[]{:S(2)}) collective-permute-start(f32[256,128]{1,0:T(8,128)S(1)} %add.220), channel_id=1, source_target_pairs={{0,24},{1,25},{8,16},{9,17},{4,28},{5,29},{12,20},{13,21},{18,10},... | collective-permute-start | bytes 393224 | tf_op jit(solution)/shard_map/ppermute | solution.py:89
  123.5 10.2 %collective-permute-start.53 = (f32[256,128]{1,0:T(8,128)S(1)}, f32[256,128]{1,0:T(8,128)S(1)}, u32[]{:S(2)}, u32[]{:S(2)}) collective-permute-start(f32[256,128]{1,0:T(8,128)S(1)} %get-tuple-element.27.refs_0_), channel_id=1, source_target_pairs={{0,8},{1,9},{8,0},{9,1},{16,24},{17,25},{24,16},{25,17},{4,12},{5,... | collective-permute-start | bytes 393224 | tf_op jit(solution)/shard_map/ppermute | solution.py:89
  129.7 7.3 %collective-permute-start.52 = (f32[256,128]{1,0:T(8,128)S(1)}, f32[256,128]{1,0:T(8,128)S(1)}, u32[]{:S(2)}, u32[]{:S(2)}) collective-permute-start(f32[256,128]{1,0:T(8,128)S(1)} %get-tuple-element.27.refs_0_), channel_id=1, source_target_pairs={{0,4},{1,5},{8,12},{9,13},{16,20},{17,21},{24,28},{25,29},{4,0},{5... | collective-permute-start | bytes 393224 | tf_op jit(solution)/shard_map/ppermute | solution.py:89
  132.1 9.4 %collective-permute-start.47 = (f32[256,128]{1,0:T(8,128)S(1)}, f32[256,128]{1,0:T(8,128)S(1)}, u32[]{:S(2)}, u32[]{:S(2)}) collective-permute-start(f32[256,128]{1,0:T(8,128)S(1)} %get-tuple-element.28.refs_0_), channel_id=1, source_target_pairs={{0,4},{1,5},{8,12},{9,13},{16,20},{17,21},{24,28},{25,29},{4,0},{5... | collective-permute-start | bytes 393224 | tf_op jit(solution)/shard_map/ppermute | solution.py:89
  133.6 7.7 %collective-permute-start.54 = (f32[256,128]{1,0:T(8,128)S(1)}, f32[256,128]{1,0:T(8,128)S(1)}, u32[]{:S(2)}, u32[]{:S(2)}) collective-permute-start(f32[256,128]{1,0:T(8,128)S(1)} %collective-permute-done.53.refs_2_), channel_id=1, source_target_pairs={{0,4},{1,5},{8,12},{9,13},{16,20},{17,21},{24,28},{25,29},{4,0},{5... | collective-permute-start | bytes 393224 | tf_op jit(solution)/shard_map/ppermute | solution.py:89
  157.1 8.9 %collective-permute-start.65 = (f32[256,128]{1,0:T(8,128)S(1)}, f32[256,128]{1,0:T(8,128)S(1)}, u32[]{:S(2)}, u32[]{:S(2)}) collective-permute-start(f32[256,128]{1,0:T(8,128)S(1)} %get-tuple-element.13), channel_id=1, source_target_pairs={{0,24},{1,25},{8,16},{9,17},{4,28},{5,29},{12,20},{13,21},{18,10},... | collective-permute-start | bytes 393224 | tf_op jit(solution)/shard_map/ppermute | solution.py:89
  162.1 10.1 %collective-permute-start.58 = (f32[256,128]{1,0:T(8,128)S(1)}, f32[256,128]{1,0:T(8,128)S(1)}, u32[]{:S(2)}, u32[]{:S(2)}) collective-permute-start(f32[256,128]{1,0:T(8,128)S(1)} %get-tuple-element.14), channel_id=1, source_target_pairs={{0,24},{1,25},{8,16},{9,17},{4,28},{5,29},{12,20},{13,21},{18,10},... | collective-permute-start | bytes 393224 | tf_op jit(solution)/shard_map/ppermute | solution.py:89
  166.0 8.6 %collective-permute-start.67 = (f32[256,128]{1,0:T(8,128)S(1)}, f32[256,128]{1,0:T(8,128)S(1)}, u32[]{:S(2)}, u32[]{:S(2)}) collective-permute-start(f32[256,128]{1,0:T(8,128)S(1)} %broadcast_select_fusion.refs_0_), channel_id=1, source_target_pairs={{0,8},{1,9},{8,0},{9,1},{16,24},{17,25},{24,16},{25,17},{4,12},{5,... | collective-permute-start | bytes 393224 | tf_op jit(solution)/shard_map/ppermute | solution.py:89
  170.8 7.1 %collective-permute-start.66 = (f32[256,128]{1,0:T(8,128)S(1)}, f32[256,128]{1,0:T(8,128)S(1)}, u32[]{:S(2)}, u32[]{:S(2)}) collective-permute-start(f32[256,128]{1,0:T(8,128)S(1)} %broadcast_select_fusion.refs_0_), channel_id=1, source_target_pairs={{0,4},{1,5},{8,12},{9,13},{16,20},{17,21},{24,28},{25,29},{4,0},{5... | collective-permute-start | bytes 393224 | tf_op jit(solution)/shard_map/ppermute | solution.py:89
  172.4 9.4 %collective-permute-start.59 = (f32[256,128]{1,0:T(8,128)S(1)}, f32[256,128]{1,0:T(8,128)S(1)}, u32[]{:S(2)}, u32[]{:S(2)}) collective-permute-start(f32[256,128]{1,0:T(8,128)S(1)} %broadcast_select_fusion.1.refs_0_), channel_id=1, source_target_pairs={{0,4},{1,5},{8,12},{9,13},{16,20},{17,21},{24,28},{25,29},{4,0},{5... | collective-permute-start | bytes 393224 | tf_op jit(solution)/shard_map/ppermute | solution.py:89
  174.6 7.1 %collective-permute-start.68 = (f32[256,128]{1,0:T(8,128)S(1)}, f32[256,128]{1,0:T(8,128)S(1)}, u32[]{:S(2)}, u32[]{:S(2)}) collective-permute-start(f32[256,128]{1,0:T(8,128)S(1)} %collective-permute-done.67.refs_2_), channel_id=1, source_target_pairs={{0,4},{1,5},{8,12},{9,13},{16,20},{17,21},{24,28},{25,29},{4,0},{5... | collective-permute-start | bytes 393224 | tf_op jit(solution)/shard_map/ppermute | solution.py:89
  191.2 6.9 %collective-permute-start.73 = (f32[256,128]{1,0:T(8,128)S(1)}, f32[256,128]{1,0:T(8,128)S(1)}, u32[]{:S(2)}, u32[]{:S(2)}) collective-permute-start(f32[256,128]{1,0:T(8,128)S(1)} %add_bitcast_fusion), channel_id=1, source_target_pairs={{0,2},{1,3},{8,10},{9,11},{16,18},{17,19},{24,26},{25,27},{4,6},{5... | collective-permute-start | bytes 393224 | tf_op jit(solution)/shard_map/ppermute | solution.py:89
  (55 other events, 477.5 us)

commit v4 on v3

--- a/solution.py
+++ b/solution.py
@@ -120,8 +120,7 @@
     if make is not None:
         made = make(mine)
         own = gate(own, made)
-    beside, above = send(own, TO_Y), send(own, TO_Z)
-    across = send(above, TO_Y)
+    beside, above, across = send(own, TO_Y), send(own, TO_Z), send(own, TO_YZ)
     same = jnp.where(z // 2 == x, z % 2, 1 - z % 2) == k
     swapped = send(jnp.stack([jnp.where(same, above, own), jnp.where(same, across, beside)]), TO_CORE)
     pieces = (own, beside, above, across, swapped)
@@ -291,7 +290,7 @@
             p = leaf_pieces[s]
             return apply(
                 (gate(p[0], mine),) + p[1:],
-                [(pltpu.with_memory_space_constraint(t[0], pltpu.MemorySpace.HBM),) + t[1:] for t in pair(leaf_to_root, 256, s)],
+                [(t[0],) + t[1:] for t in pair(leaf_to_root, 256, s)],
                 1024,
                 256,
                 mask=mask_lr[2 * s : 2 * s + 2],

time: 201 us -> 200 us (level)
  Pallas kernels: 22.2 us -> 18.1 us
  local copies, waits for them, and re-layouts: 10.8 us -> 14.1 us
    pallas_call x14, Pallas kernels: 22.2 us -> 18.1 us  [apply(): pl.pallas_call(functools.partial(kernel_body, tuple(((t[3], t[4]) for t i...]
    unnamed x23 -> x25, local copies, waits for them, and re-layouts: 0.14 us -> 3.51 us
  transfers between devices with their start and end apart: 76 -> 76, of which waited for: 31 -> 29; matrix products, arithmetic and copies ran while one was open for 8% -> 8% of each run, Pallas kernels for 10% -> 8%
where the time goes in v4:
time: 200 us; the launch traced here: 199 us
  starting transfers between devices  99.8 us (50%)
  waiting for transfers between devices  58.2 us (29%)
  Pallas kernels  18.1 us (9%)
  local copies, waits for them, and re-layouts  14.1 us (7%)
  other arithmetic  7.32 us (4%)
    ppermute x76, starting transfers between devices, send(): return lax.ppermute(value, AXES, pairs)  99.8 us
    ppermute x76, waiting for transfers between devices, send(): return lax.ppermute(value, AXES, pairs)  58.2 us
    pallas_call x14, Pallas kernels, apply(): pl.pallas_call(functools.partial(kernel_body, tuple(((t[3], t[4]) for t i...  18.1 us
    slice x1, local copies, waits for them, and re-layouts, grid_body(): mid_to_root[0:1]  8.48 us
  transfers between devices with their start and end apart: 76, of which 29 were waited for; matrix products, arithmetic and copies ran while one was open for 8% of the time, Pallas kernels for 8%

profile of v4, /device:TPU:0, one launch (start us, length us, event | category | flops | bytes accessed | tf_op | source)
XLA Modules:
  0.0 199.2 jit_solution(1972474923467242243)
XLA Ops:
  1.7 7.0 %collective-permute-start = (f32[256,128]{1,0:T(8,128)S(1)}, f32[256,128]{1,0:T(8,128)S(1)}, u32[]{:S(2)}, u32[]{:S(2)}) collective-permute-start(f32[256,128]{1,0:T(8,128)S(1)} %get-tuple-element.17), channel_id=1, source_target_pairs={{0,24},{1,25},{8,16},{9,17},{4,28},{5,29},{12,20},{13,21},{18,10},... | collective-permute-start | bytes 393224 | tf_op jit(solution)/shard_map/ppermute | solution.py:89
  10.1 8.5 %fusion.1 = (f32[1,1024,1024]{2,1,0:T(8,128)}, f32[1,1024,1024]{2,1,0:T(8,128)}) fusion(f32[2,1024,1024]{2,1,0:T(8,128)} %param.20), kind=kLoop, calls=%fused_computation.81 | loop fusion | bytes 16777216 | tf_op jit(solution)/shard_map/slice | solution.py:313
  22.3 2.9 %collective-permute-start.11 = (f32[256,128]{1,0:T(8,128)S(1)}, f32[256,128]{1,0:T(8,128)S(1)}, u32[]{:S(2)}, u32[]{:S(2)}) collective-permute-start(f32[256,128]{1,0:T(8,128)S(1)} %broadcast_select_fusion.8.refs_0_), channel_id=1, source_target_pairs={{0,12},{1,13},{8,4},{9,5},{16,28},{17,29},{24,20},{25,21},{4,8},{5... | collective-permute-start | bytes 393224 | tf_op jit(solution)/shard_map/ppermute | solution.py:89
  25.2 4.1 %collective-permute-done.2.refs_2_ = f32[256,128]{1,0:T(8,128)S(1)} collective-permute-done((f32[256,128]{1,0:T(8,128)S(1)}, f32[256,128]{1,0:T(8,128)S(1)}, u32[]{:S(2)}, u32[]{:S(2)}) %collective-permute-start.2) | collective-permute-done | bytes 131104 | tf_op jit(solution)/shard_map/ppermute | solution.py:89
  31.9 2.4 %collective-permute-done.11.refs_3_ = f32[256,128]{1,0:T(8,128)S(1)} collective-permute-done((f32[256,128]{1,0:T(8,128)S(1)}, f32[256,128]{1,0:T(8,128)S(1)}, u32[]{:S(2)}, u32[]{:S(2)}) %collective-permute-start.11) | collective-permute-done | bytes 131104 | tf_op jit(solution)/shard_map/ppermute | solution.py:89
  42.3 3.0 %collective-permute-done.6 = f32[256,128]{1,0:T(8,128)S(1)} collective-permute-done((f32[256,128]{1,0:T(8,128)S(1)}, f32[256,128]{1,0:T(8,128)S(1)}, u32[]{:S(2)}, u32[]{:S(2)}) %collective-permute-start.6) | collective-permute-done | bytes 131104 | tf_op jit(solution)/shard_map/ppermute | solution.py:89
  49.7 6.2 %collective-permute-start.18 = (f32[256,128]{1,0:T(8,128)S(1)}, f32[256,128]{1,0:T(8,128)S(1)}, u32[]{:S(2)}, u32[]{:S(2)}) collective-permute-start(f32[256,128]{1,0:T(8,128)S(1)} %get-tuple-element.7.refs_0_), channel_id=1, source_target_pairs={{0,8},{1,9},{8,0},{9,1},{16,24},{17,25},{24,16},{25,17},{4,12},{5,... | collective-permute-start | bytes 393224 | tf_op jit(solution)/shard_map/ppermute | solution.py:89
  62.6 2.3 %collective-permute-done.17.refs_1_ = f32[256,128]{1,0:T(8,128)S(1)} collective-permute-done((f32[256,128]{1,0:T(8,128)S(1)}, f32[256,128]{1,0:T(8,128)S(1)}, u32[]{:S(2)}, u32[]{:S(2)}) %collective-permute-start.17) | collective-permute-done | bytes 131104 | tf_op jit(solution)/shard_map/ppermute | solution.py:89
  65.1 2.6 %collective-permute-done.32.refs_1_ = f32[256,128]{1,0:T(8,128)S(1)} collective-permute-done((f32[256,128]{1,0:T(8,128)S(1)}, f32[256,128]{1,0:T(8,128)S(1)}, u32[]{:S(2)}, u32[]{:S(2)}) %collective-permute-start.32) | collective-permute-done | bytes 131104 | tf_op jit(solution)/shard_map/ppermute | solution.py:89
  71.7 2.4 %collective-permute-start.22 = (f32[256,128]{1,0:T(8,128)S(1)}, f32[256,128]{1,0:T(8,128)S(1)}, u32[]{:S(2)}, u32[]{:S(2)}) collective-permute-start(f32[256,128]{1,0:T(8,128)S(1)} %add_bitcast_fusion.7), channel_id=1, source_target_pairs={{0,2},{1,3},{8,10},{9,11},{16,18},{17,19},{24,26},{25,27},{4,6},{5... | collective-permute-start | bytes 393224 | tf_op jit(solution)/shard_map/ppermute | solution.py:89
  75.5 2.6 %collective-permute-done.22 = f32[256,128]{1,0:T(8,128)S(1)} collective-permute-done((f32[256,128]{1,0:T(8,128)S(1)}, f32[256,128]{1,0:T(8,128)S(1)}, u32[]{:S(2)}, u32[]{:S(2)}) %collective-permute-start.22) | collective-permute-done | bytes 131104 | tf_op jit(solution)/shard_map/ppermute | solution.py:89
  78.2 5.3 %collective-permute-start.23 = (f32[256,128]{1,0:T(8,128)S(1)}, f32[256,128]{1,0:T(8,128)S(1)}, u32[]{:S(2)}, u32[]{:S(2)}) collective-permute-start(f32[256,128]{1,0:T(8,128)S(1)} %bitcast_subtract_fusion.3), channel_id=1, source_target_pairs={{0,24},{1,25},{8,16},{9,17},{4,28},{5,29},{12,20},{13,21},{18,10},... | collective-permute-start | bytes 393224 | tf_op jit(solution)/shard_map/ppermute | solution.py:89
  85.7 3.4 %copy-done.2 = f32[4,1024,512]{2,1,0:T(8,128)S(1)} copy-done((f32[4,1024,512]{2,1,0:T(8,128)S(1)}, f32[4,1024,512]{2,1,0:T(8,128)}, u32[]{:S(2)}) %copy-start.2) | copy-done | bytes 8388632
  93.9 2.7 %collective-permute-start.26 = (f32[256,128]{1,0:T(8,128)S(1)}, f32[256,128]{1,0:T(8,128)S(1)}, u32[]{:S(2)}, u32[]{:S(2)}) collective-permute-start(f32[256,128]{1,0:T(8,128)S(1)} %broadcast_select_fusion.6.refs_0_), channel_id=1, source_target_pairs={{0,12},{1,13},{8,4},{9,5},{16,28},{17,29},{24,20},{25,21},{4,8},{5... | collective-permute-start | bytes 393224 | tf_op jit(solution)/shard_map/ppermute | solution.py:89
  102.4 2.4 %collective-permute-done.40.refs_2_ = f32[256,128]{1,0:T(8,128)S(1)} collective-permute-done((f32[256,128]{1,0:T(8,128)S(1)}, f32[256,128]{1,0:T(8,128)S(1)}, u32[]{:S(2)}, u32[]{:S(2)}) %collective-permute-start.40) | collective-permute-done | bytes 131104 | tf_op jit(solution)/shard_map/ppermute | solution.py:89
  111.5 4.1 %collective-permute-done.29 = f32[256,128]{1,0:T(8,128)S(1)} collective-permute-done((f32[256,128]{1,0:T(8,128)S(1)}, f32[256,128]{1,0:T(8,128)S(1)}, u32[]{:S(2)}, u32[]{:S(2)}) %collective-permute-start.29) | collective-permute-done | bytes 131104 | tf_op jit(solution)/shard_map/ppermute | solution.py:89
  115.7 3.8 %collective-permute-start.51 = (f32[256,128]{1,0:T(8,128)S(1)}, f32[256,128]{1,0:T(8,128)S(1)}, u32[]{:S(2)}, u32[]{:S(2)}) collective-permute-start(f32[256,128]{1,0:T(8,128)S(1)} %add.214), channel_id=1, source_target_pairs={{0,24},{1,25},{8,16},{9,17},{4,28},{5,29},{12,20},{13,21},{18,10},... | collective-permute-start | bytes 393224 | tf_op jit(solution)/shard_map/ppermute | solution.py:89
  119.8 2.4 %collective-permute-start.46 = (f32[256,128]{1,0:T(8,128)S(1)}, f32[256,128]{1,0:T(8,128)S(1)}, u32[]{:S(2)}, u32[]{:S(2)}) collective-permute-start(f32[256,128]{1,0:T(8,128)S(1)} %add.220), channel_id=1, source_target_pairs={{0,24},{1,25},{8,16},{9,17},{4,28},{5,29},{12,20},{13,21},{18,10},... | collective-permute-start | bytes 393224 | tf_op jit(solution)/shard_map/ppermute | solution.py:89
  123.2 6.0 %collective-permute-start.53 = (f32[256,128]{1,0:T(8,128)S(1)}, f32[256,128]{1,0:T(8,128)S(1)}, u32[]{:S(2)}, u32[]{:S(2)}) collective-permute-start(f32[256,128]{1,0:T(8,128)S(1)} %get-tuple-element.27.refs_0_), channel_id=1, source_target_pairs={{0,8},{1,9},{8,0},{9,1},{16,24},{17,25},{24,16},{25,17},{4,12},{5,... | collective-permute-start | bytes 393224 | tf_op jit(solution)/shard_map/ppermute | solution.py:89
  134.0 2.3 %collective-permute-start.49 = (f32[256,128]{1,0:T(8,128)S(1)}, f32[256,128]{1,0:T(8,128)S(1)}, u32[]{:S(2)}, u32[]{:S(2)}) collective-permute-start(f32[256,128]{1,0:T(8,128)S(1)} %get-tuple-element.28.refs_0_), channel_id=1, source_target_pairs={{0,12},{1,13},{8,4},{9,5},{16,28},{17,29},{24,20},{25,21},{4,8},{5... | collective-permute-start | bytes 393224 | tf_op jit(solution)/shard_map/ppermute | solution.py:89
  136.3 3.2 %collective-permute-done.52.refs_1_ = f32[256,128]{1,0:T(8,128)S(1)} collective-permute-done((f32[256,128]{1,0:T(8,128)S(1)}, f32[256,128]{1,0:T(8,128)S(1)}, u32[]{:S(2)}, u32[]{:S(2)}) %collective-permute-start.52) | collective-permute-done | bytes 131104 | tf_op jit(solution)/shard_map/ppermute | solution.py:89
  139.7 2.8 %collective-permute-done.47.refs_1_ = f32[256,128]{1,0:T(8,128)S(1)} collective-permute-done((f32[256,128]{1,0:T(8,128)S(1)}, f32[256,128]{1,0:T(8,128)S(1)}, u32[]{:S(2)}, u32[]{:S(2)}) %collective-permute-start.47) | collective-permute-done | bytes 131104 | tf_op jit(solution)/shard_map/ppermute | solution.py:89
  147.5 2.3 %collective-permute-start.57 = (f32[256,128]{1,0:T(8,128)S(1)}, f32[256,128]{1,0:T(8,128)S(1)}, u32[]{:S(2)}, u32[]{:S(2)}) collective-permute-start(f32[256,128]{1,0:T(8,128)S(1)} %add_bitcast_fusion.3), channel_id=1, source_target_pairs={{0,2},{1,3},{8,10},{9,11},{16,18},{17,19},{24,26},{25,27},{4,6},{5... | collective-permute-start | bytes 393224 | tf_op jit(solution)/shard_map/ppermute | solution.py:89
  151.2 2.9 %collective-permute-done.57 = f32[256,128]{1,0:T(8,128)S(1)} collective-permute-done((f32[256,128]{1,0:T(8,128)S(1)}, f32[256,128]{1,0:T(8,128)S(1)}, u32[]{:S(2)}, u32[]{:S(2)}) %collective-permute-start.57) | collective-permute-done | bytes 131104 | tf_op jit(solution)/shard_map/ppermute | solution.py:89
  154.2 2.5 %collective-permute-done.64 = f32[256,128]{1,0:T(8,128)S(1)} collective-permute-done((f32[256,128]{1,0:T(8,128)S(1)}, f32[256,128]{1,0:T(8,128)S(1)}, u32[]{:S(2)}, u32[]{:S(2)}) %collective-permute-start.64) | collective-permute-done | bytes 131104 | tf_op jit(solution)/shard_map/ppermute | solution.py:89
  156.7 4.8 %collective-permute-start.65 = (f32[256,128]{1,0:T(8,128)S(1)}, f32[256,128]{1,0:T(8,128)S(1)}, u32[]{:S(2)}, u32[]{:S(2)}) collective-permute-start(f32[256,128]{1,0:T(8,128)S(1)} %get-tuple-element.13), channel_id=1, source_target_pairs={{0,24},{1,25},{8,16},{9,17},{4,28},{5,29},{12,20},{13,21},{18,10},... | collective-permute-start | bytes 393224 | tf_op jit(solution)/shard_map/ppermute | solution.py:89
  162.9 2.6 %collective-permute-done.65 = f32[256,128]{1,0:T(8,128)S(1)} collective-permute-done((f32[256,128]{1,0:T(8,128)S(1)}, f32[256,128]{1,0:T(8,128)S(1)}, u32[]{:S(2)}, u32[]{:S(2)}) %collective-permute-start.65) | collective-permute-done | bytes 131104 | tf_op jit(solution)/shard_map/ppermute | solution.py:89
  165.5 5.2 %collective-permute-start.67 = (f32[256,128]{1,0:T(8,128)S(1)}, f32[256,128]{1,0:T(8,128)S(1)}, u32[]{:S(2)}, u32[]{:S(2)}) collective-permute-start(f32[256,128]{1,0:T(8,128)S(1)} %broadcast_select_fusion.refs_0_), channel_id=1, source_target_pairs={{0,8},{1,9},{8,0},{9,1},{16,24},{17,25},{24,16},{25,17},{4,12},{5,... | collective-permute-start | bytes 393224 | tf_op jit(solution)/shard_map/ppermute | solution.py:89
  179.0 2.6 %collective-permute-done.59.refs_1_ = f32[256,128]{1,0:T(8,128)S(1)} collective-permute-done((f32[256,128]{1,0:T(8,128)S(1)}, f32[256,128]{1,0:T(8,128)S(1)}, u32[]{:S(2)}, u32[]{:S(2)}) %collective-permute-start.59) | collective-permute-done | bytes 131104 | tf_op jit(solution)/shard_map/ppermute | solution.py:89
  181.8 2.3 %shard_map.150.refs_7_ = f32[1024,128]{1,0:T(8,128)S(1)} custom-call(f32[256,128]{1,0:T(8,128)S(1)} %broadcast_select_fusion.refs_0_, f32[256,128]{1,0:T(8,128)S(1)} %collective-permute-done.66.refs_1_, f32[256,128]{1,0:T(8,128)S(1)} %collective-permute-done.67.refs_2_, f32[256,128]{1,0:T(8,128)S(1)} %collective-permute-done.68.refs_3_, ...), custom_call_target="tpu_custom_call" | custom-call | flops 1073741824 | bytes 4194304 | tf_op jit(solution)/shard_map/pallas_call | solution.py:220
  187.5 2.2 %collective-permute-start.71 = (f32[256,128]{1,0:T(8,128)S(1)}, f32[256,128]{1,0:T(8,128)S(1)}, u32[]{:S(2)}, u32[]{:S(2)}) collective-permute-start(f32[256,128]{1,0:T(8,128)S(1)} %add_bitcast_fusion.1), channel_id=1, source_target_pairs={{0,2},{1,3},{8,10},{9,11},{16,18},{17,19},{24,26},{25,27},{4,6},{5... | collective-permute-start | bytes 393224 | tf_op jit(solution)/shard_map/ppermute | solution.py:89
  194.1 2.5 %collective-permute-done.73 = f32[256,128]{1,0:T(8,128)S(1)} collective-permute-done((f32[256,128]{1,0:T(8,128)S(1)}, f32[256,128]{1,0:T(8,128)S(1)}, u32[]{:S(2)}, u32[]{:S(2)}) %collective-permute-start.73) | collective-permute-done | bytes 131104 | tf_op jit(solution)/shard_map/ppermute | solution.py:89
  (253 shorter events, 85.0 us)
Async XLA Ops:
  1.7 16.9 %collective-permute-start = (f32[256,128]{1,0:T(8,128)S(1)}, f32[256,128]{1,0:T(8,128)S(1)}, u32[]{:S(2)}, u32[]{:S(2)}) collective-permute-start(f32[256,128]{1,0:T(8,128)S(1)} %get-tuple-element.17), channel_id=1, source_target_pairs={{0,24},{1,25},{8,16},{9,17},{4,28},{5,29},{12,20},{13,21},{18,10},... | collective-permute-start | bytes 393224 | tf_op jit(solution)/shard_map/ppermute | solution.py:89
  8.6 13.5 %collective-permute-start.8 = (f32[256,128]{1,0:T(8,128)S(1)}, f32[256,128]{1,0:T(8,128)S(1)}, u32[]{:S(2)}, u32[]{:S(2)}) collective-permute-start(f32[256,128]{1,0:T(8,128)S(1)} %get-tuple-element.18), channel_id=1, source_target_pairs={{0,24},{1,25},{8,16},{9,17},{4,28},{5,29},{12,20},{13,21},{18,10},... | collective-permute-start | bytes 393224 | tf_op jit(solution)/shard_map/ppermute | solution.py:89
  18.6 12.3 %collective-permute-start.1 = (f32[256,128]{1,0:T(8,128)S(1)}, f32[256,128]{1,0:T(8,128)S(1)}, u32[]{:S(2)}, u32[]{:S(2)}) collective-permute-start(f32[256,128]{1,0:T(8,128)S(1)} %broadcast_select_fusion.9.refs_0_), channel_id=1, source_target_pairs={{0,4},{1,5},{8,12},{9,13},{16,20},{17,21},{24,28},{25,29},{4,0},{5... | collective-permute-start | bytes 393224 | tf_op jit(solution)/shard_map/ppermute | solution.py:89
  20.2 10.7 %collective-permute-start.3 = (f32[256,128]{1,0:T(8,128)S(1)}, f32[256,128]{1,0:T(8,128)S(1)}, u32[]{:S(2)}, u32[]{:S(2)}) collective-permute-start(f32[256,128]{1,0:T(8,128)S(1)} %broadcast_select_fusion.9.refs_0_), channel_id=1, source_target_pairs={{0,12},{1,13},{8,4},{9,5},{16,28},{17,29},{24,20},{25,21},{4,8},{5... | collective-permute-start | bytes 393224 | tf_op jit(solution)/shard_map/ppermute | solution.py:89
  20.2 9.2 %collective-permute-start.2 = (f32[256,128]{1,0:T(8,128)S(1)}, f32[256,128]{1,0:T(8,128)S(1)}, u32[]{:S(2)}, u32[]{:S(2)}) collective-permute-start(f32[256,128]{1,0:T(8,128)S(1)} %broadcast_select_fusion.9.refs_0_), channel_id=1, source_target_pairs={{0,8},{1,9},{8,0},{9,1},{16,24},{17,25},{24,16},{25,17},{4,12},{5,... | collective-permute-start | bytes 393224 | tf_op jit(solution)/shard_map/ppermute | solution.py:89
  22.2 9.7 %collective-permute-start.10 = (f32[256,128]{1,0:T(8,128)S(1)}, f32[256,128]{1,0:T(8,128)S(1)}, u32[]{:S(2)}, u32[]{:S(2)}) collective-permute-start(f32[256,128]{1,0:T(8,128)S(1)} %broadcast_select_fusion.8.refs_0_), channel_id=1, source_target_pairs={{0,8},{1,9},{8,0},{9,1},{16,24},{17,25},{24,16},{25,17},{4,12},{5,... | collective-permute-start | bytes 393224 | tf_op jit(solution)/shard_map/ppermute | solution.py:89
  22.3 12.0 %collective-permute-start.11 = (f32[256,128]{1,0:T(8,128)S(1)}, f32[256,128]{1,0:T(8,128)S(1)}, u32[]{:S(2)}, u32[]{:S(2)}) collective-permute-start(f32[256,128]{1,0:T(8,128)S(1)} %broadcast_select_fusion.8.refs_0_), channel_id=1, source_target_pairs={{0,12},{1,13},{8,4},{9,5},{16,28},{17,29},{24,20},{25,21},{4,8},{5... | collective-permute-start | bytes 393224 | tf_op jit(solution)/shard_map/ppermute | solution.py:89
  47.6 9.8 %collective-permute-start.15 = (f32[256,128]{1,0:T(8,128)S(1)}, f32[256,128]{1,0:T(8,128)S(1)}, u32[]{:S(2)}, u32[]{:S(2)}) collective-permute-start(f32[256,128]{1,0:T(8,128)S(1)} %add.205), channel_id=1, source_target_pairs={{0,1},{1,0},{8,9},{9,8},{16,17},{17,16},{24,25},{25,24},{4,5},{5,4... | collective-permute-start | bytes 393224 | tf_op jit(solution)/shard_map/ppermute | solution.py:89
  47.7 9.7 %collective-permute-start.31 = (f32[256,128]{1,0:T(8,128)S(1)}, f32[256,128]{1,0:T(8,128)S(1)}, u32[]{:S(2)}, u32[]{:S(2)}) collective-permute-start(f32[256,128]{1,0:T(8,128)S(1)} %add.205), channel_id=1, source_target_pairs={{0,24},{1,25},{8,16},{9,17},{4,28},{5,29},{12,20},{13,21},{18,10},... | collective-permute-start | bytes 393224 | tf_op jit(solution)/shard_map/ppermute | solution.py:89
  49.7 10.8 %collective-permute-start.18 = (f32[256,128]{1,0:T(8,128)S(1)}, f32[256,128]{1,0:T(8,128)S(1)}, u32[]{:S(2)}, u32[]{:S(2)}) collective-permute-start(f32[256,128]{1,0:T(8,128)S(1)} %get-tuple-element.7.refs_0_), channel_id=1, source_target_pairs={{0,8},{1,9},{8,0},{9,1},{16,24},{17,25},{24,16},{25,17},{4,12},{5,... | collective-permute-start | bytes 393224 | tf_op jit(solution)/shard_map/ppermute | solution.py:89
  55.9 9.0 %collective-permute-start.17 = (f32[256,128]{1,0:T(8,128)S(1)}, f32[256,128]{1,0:T(8,128)S(1)}, u32[]{:S(2)}, u32[]{:S(2)}) collective-permute-start(f32[256,128]{1,0:T(8,128)S(1)} %get-tuple-element.7.refs_0_), channel_id=1, source_target_pairs={{0,4},{1,5},{8,12},{9,13},{16,20},{17,21},{24,28},{25,29},{4,0},{5... | collective-permute-start | bytes 393224 | tf_op jit(solution)/shard_map/ppermute | solution.py:89
  59.5 8.2 %collective-permute-start.32 = (f32[256,128]{1,0:T(8,128)S(1)}, f32[256,128]{1,0:T(8,128)S(1)}, u32[]{:S(2)}, u32[]{:S(2)}) collective-permute-start(f32[256,128]{1,0:T(8,128)S(1)} %get-tuple-element.9.refs_0_), channel_id=1, source_target_pairs={{0,4},{1,5},{8,12},{9,13},{16,20},{17,21},{24,28},{25,29},{4,0},{5... | collective-permute-start | bytes 393224 | tf_op jit(solution)/shard_map/ppermute | solution.py:89
  75.3 8.2 %collective-permute-start.37 = (f32[256,128]{1,0:T(8,128)S(1)}, f32[256,128]{1,0:T(8,128)S(1)}, u32[]{:S(2)}, u32[]{:S(2)}) collective-permute-start(f32[256,128]{1,0:T(8,128)S(1)} %add_bitcast_fusion.5), channel_id=1, source_target_pairs={{0,2},{1,3},{8,10},{9,11},{16,18},{17,19},{24,26},{25,27},{4,6},{5... | collective-permute-start | bytes 393224 | tf_op jit(solution)/shard_map/ppermute | solution.py:89
  78.2 14.8 %collective-permute-start.23 = (f32[256,128]{1,0:T(8,128)S(1)}, f32[256,128]{1,0:T(8,128)S(1)}, u32[]{:S(2)}, u32[]{:S(2)}) collective-permute-start(f32[256,128]{1,0:T(8,128)S(1)} %bitcast_subtract_fusion.3), channel_id=1, source_target_pairs={{0,24},{1,25},{8,16},{9,17},{4,28},{5,29},{12,20},{13,21},{18,10},... | collective-permute-start | bytes 393224 | tf_op jit(solution)/shard_map/ppermute | solution.py:89
  83.5 13.1 %collective-permute-start.38 = (f32[256,128]{1,0:T(8,128)S(1)}, f32[256,128]{1,0:T(8,128)S(1)}, u32[]{:S(2)}, u32[]{:S(2)}) collective-permute-start(f32[256,128]{1,0:T(8,128)S(1)} %bitcast_subtract_fusion.2), channel_id=1, source_target_pairs={{0,24},{1,25},{8,16},{9,17},{4,28},{5,29},{12,20},{13,21},{18,10},... | collective-permute-start | bytes 393224 | tf_op jit(solution)/shard_map/ppermute | solution.py:89
  93.1 8.1 %collective-permute-start.24 = (f32[256,128]{1,0:T(8,128)S(1)}, f32[256,128]{1,0:T(8,128)S(1)}, u32[]{:S(2)}, u32[]{:S(2)}) collective-permute-start(f32[256,128]{1,0:T(8,128)S(1)} %broadcast_select_fusion.6.refs_0_), channel_id=1, source_target_pairs={{0,4},{1,5},{8,12},{9,13},{16,20},{17,21},{24,28},{25,29},{4,0},{5... | collective-permute-start | bytes 393224 | tf_op jit(solution)/shard_map/ppermute | solution.py:89
  93.9 8.4 %collective-permute-start.26 = (f32[256,128]{1,0:T(8,128)S(1)}, f32[256,128]{1,0:T(8,128)S(1)}, u32[]{:S(2)}, u32[]{:S(2)}) collective-permute-start(f32[256,128]{1,0:T(8,128)S(1)} %broadcast_select_fusion.6.refs_0_), channel_id=1, source_target_pairs={{0,12},{1,13},{8,4},{9,5},{16,28},{17,29},{24,20},{25,21},{4,8},{5... | collective-permute-start | bytes 393224 | tf_op jit(solution)/shard_map/ppermute | solution.py:89
  96.6 8.2 %collective-permute-start.40 = (f32[256,128]{1,0:T(8,128)S(1)}, f32[256,128]{1,0:T(8,128)S(1)}, u32[]{:S(2)}, u32[]{:S(2)}) collective-permute-start(f32[256,128]{1,0:T(8,128)S(1)} %broadcast_select_fusion.4.refs_0_), channel_id=1, source_target_pairs={{0,8},{1,9},{8,0},{9,1},{16,24},{17,25},{24,16},{25,17},{4,12},{5,... | collective-permute-start | bytes 393224 | tf_op jit(solution)/shard_map/ppermute | solution.py:89
  96.7 9.5 %collective-permute-start.39 = (f32[256,128]{1,0:T(8,128)S(1)}, f32[256,128]{1,0:T(8,128)S(1)}, u32[]{:S(2)}, u32[]{:S(2)}) collective-permute-start(f32[256,128]{1,0:T(8,128)S(1)} %broadcast_select_fusion.4.refs_0_), channel_id=1, source_target_pairs={{0,4},{1,5},{8,12},{9,13},{16,20},{17,21},{24,28},{25,29},{4,0},{5... | collective-permute-start | bytes 393224 | tf_op jit(solution)/shard_map/ppermute | solution.py:89
  110.7 8.9 %collective-permute-start.44 = (f32[256,128]{1,0:T(8,128)S(1)}, f32[256,128]{1,0:T(8,128)S(1)}, u32[]{:S(2)}, u32[]{:S(2)}) collective-permute-start(f32[256,128]{1,0:T(8,128)S(1)} %add_bitcast_fusion.4), channel_id=1, source_target_pairs={{0,2},{1,3},{8,10},{9,11},{16,18},{17,19},{24,26},{25,27},{4,6},{5... | collective-permute-start | bytes 393224 | tf_op jit(solution)/shard_map/ppermute | solution.py:89
  119.6 11.2 %collective-permute-start.45 = (f32[256,128]{1,0:T(8,128)S(1)}, f32[256,128]{1,0:T(8,128)S(1)}, u32[]{:S(2)}, u32[]{:S(2)}) collective-permute-start(f32[256,128]{1,0:T(8,128)S(1)} %add.220), channel_id=1, source_target_pairs={{0,1},{1,0},{8,9},{9,8},{16,17},{17,16},{24,25},{25,24},{4,5},{5,4... | collective-permute-start | bytes 393224 | tf_op jit(solution)/shard_map/ppermute | solution.py:89
  119.8 10.9 %collective-permute-start.46 = (f32[256,128]{1,0:T(8,128)S(1)}, f32[256,128]{1,0:T(8,128)S(1)}, u32[]{:S(2)}, u32[]{:S(2)}) collective-permute-start(f32[256,128]{1,0:T(8,128)S(1)} %add.220), channel_id=1, source_target_pairs={{0,24},{1,25},{8,16},{9,17},{4,28},{5,29},{12,20},{13,21},{18,10},... | collective-permute-start | bytes 393224 | tf_op jit(solution)/shard_map/ppermute | solution.py:89
  123.2 10.8 %collective-permute-start.53 = (f32[256,128]{1,0:T(8,128)S(1)}, f32[256,128]{1,0:T(8,128)S(1)}, u32[]{:S(2)}, u32[]{:S(2)}) collective-permute-start(f32[256,128]{1,0:T(8,128)S(1)} %get-tuple-element.27.refs_0_), channel_id=1, source_target_pairs={{0,8},{1,9},{8,0},{9,1},{16,24},{17,25},{24,16},{25,17},{4,12},{5,... | collective-permute-start | bytes 393224 | tf_op jit(solution)/shard_map/ppermute | solution.py:89
  129.2 10.3 %collective-permute-start.52 = (f32[256,128]{1,0:T(8,128)S(1)}, f32[256,128]{1,0:T(8,128)S(1)}, u32[]{:S(2)}, u32[]{:S(2)}) collective-permute-start(f32[256,128]{1,0:T(8,128)S(1)} %get-tuple-element.27.refs_0_), channel_id=1, source_target_pairs={{0,4},{1,5},{8,12},{9,13},{16,20},{17,21},{24,28},{25,29},{4,0},{5... | collective-permute-start | bytes 393224 | tf_op jit(solution)/shard_map/ppermute | solution.py:89
  130.4 9.1 %collective-permute-start.54 = (f32[256,128]{1,0:T(8,128)S(1)}, f32[256,128]{1,0:T(8,128)S(1)}, u32[]{:S(2)}, u32[]{:S(2)}) collective-permute-start(f32[256,128]{1,0:T(8,128)S(1)} %get-tuple-element.27.refs_0_), channel_id=1, source_target_pairs={{0,12},{1,13},{8,4},{9,5},{16,28},{17,29},{24,20},{25,21},{4,8},{5... | collective-permute-start | bytes 393224 | tf_op jit(solution)/shard_map/ppermute | solution.py:89
  130.8 8.9 %collective-permute-start.48 = (f32[256,128]{1,0:T(8,128)S(1)}, f32[256,128]{1,0:T(8,128)S(1)}, u32[]{:S(2)}, u32[]{:S(2)}) collective-permute-start(f32[256,128]{1,0:T(8,128)S(1)} %get-tuple-element.28.refs_0_), channel_id=1, source_target_pairs={{0,8},{1,9},{8,0},{9,1},{16,24},{17,25},{24,16},{25,17},{4,12},{5,... | collective-permute-start | bytes 393224 | tf_op jit(solution)/shard_map/ppermute | solution.py:89
  132.8 9.8 %collective-permute-start.47 = (f32[256,128]{1,0:T(8,128)S(1)}, f32[256,128]{1,0:T(8,128)S(1)}, u32[]{:S(2)}, u32[]{:S(2)}) collective-permute-start(f32[256,128]{1,0:T(8,128)S(1)} %get-tuple-element.28.refs_0_), channel_id=1, source_target_pairs={{0,4},{1,5},{8,12},{9,13},{16,20},{17,21},{24,28},{25,29},{4,0},{5... | collective-permute-start | bytes 393224 | tf_op jit(solution)/shard_map/ppermute | solution.py:89
  134.0 8.5 %collective-permute-start.49 = (f32[256,128]{1,0:T(8,128)S(1)}, f32[256,128]{1,0:T(8,128)S(1)}, u32[]{:S(2)}, u32[]{:S(2)}) collective-permute-start(f32[256,128]{1,0:T(8,128)S(1)} %get-tuple-element.28.refs_0_), channel_id=1, source_target_pairs={{0,12},{1,13},{8,4},{9,5},{16,28},{17,29},{24,20},{25,21},{4,8},{5... | collective-permute-start | bytes 393224 | tf_op jit(solution)/shard_map/ppermute | solution.py:89
  156.7 8.8 %collective-permute-start.65 = (f32[256,128]{1,0:T(8,128)S(1)}, f32[256,128]{1,0:T(8,128)S(1)}, u32[]{:S(2)}, u32[]{:S(2)}) collective-permute-start(f32[256,128]{1,0:T(8,128)S(1)} %get-tuple-element.13), channel_id=1, source_target_pairs={{0,24},{1,25},{8,16},{9,17},{4,28},{5,29},{12,20},{13,21},{18,10},... | collective-permute-start | bytes 393224 | tf_op jit(solution)/shard_map/ppermute | solution.py:89
  161.6 10.7 %collective-permute-start.58 = (f32[256,128]{1,0:T(8,128)S(1)}, f32[256,128]{1,0:T(8,128)S(1)}, u32[]{:S(2)}, u32[]{:S(2)}) collective-permute-start(f32[256,128]{1,0:T(8,128)S(1)} %get-tuple-element.14), channel_id=1, source_target_pairs={{0,24},{1,25},{8,16},{9,17},{4,28},{5,29},{12,20},{13,21},{18,10},... | collective-permute-start | bytes 393224 | tf_op jit(solution)/shard_map/ppermute | solution.py:89
  165.5 9.4 %collective-permute-start.67 = (f32[256,128]{1,0:T(8,128)S(1)}, f32[256,128]{1,0:T(8,128)S(1)}, u32[]{:S(2)}, u32[]{:S(2)}) collective-permute-start(f32[256,128]{1,0:T(8,128)S(1)} %broadcast_select_fusion.refs_0_), channel_id=1, source_target_pairs={{0,8},{1,9},{8,0},{9,1},{16,24},{17,25},{24,16},{25,17},{4,12},{5,... | collective-permute-start | bytes 393224 | tf_op jit(solution)/shard_map/ppermute | solution.py:89
  170.7 8.1 %collective-permute-start.66 = (f32[256,128]{1,0:T(8,128)S(1)}, f32[256,128]{1,0:T(8,128)S(1)}, u32[]{:S(2)}, u32[]{:S(2)}) collective-permute-start(f32[256,128]{1,0:T(8,128)S(1)} %broadcast_select_fusion.refs_0_), channel_id=1, source_target_pairs={{0,4},{1,5},{8,12},{9,13},{16,20},{17,21},{24,28},{25,29},{4,0},{5... | collective-permute-start | bytes 393224 | tf_op jit(solution)/shard_map/ppermute | solution.py:89
  (56 other events, 502.9 us)

commit v5 on v4

--- a/solution.py
+++ b/solution.py
@@ -132,9 +132,8 @@
     return high, (value - high.astype(F32)).astype(BF16)
 
 
-def kernel_body(spans, has_mask, has_add, separate, leafwise, *refs):
-    own, beside, above, across, swapped = refs[:5]
-    refs = refs[5:]
+def kernel_body(spans, has_mask, has_add, separate, leafwise, groups, *refs):
+    sets, refs = refs[: 5 * groups], refs[5 * groups :]
     count = len(spans)
     mats, refs = refs[:count], refs[count:]
     if has_mask:
@@ -152,25 +151,28 @@
         z = r // 2
         same = jnp.where(z // 2 == c // 2, lax.rem(z, 2), 1 - lax.rem(z, 2)) == k
 
-        def put(value, y_of, half):
-            row = half * (2 * PIECE) + y_of * PIECE if leafwise else y_of * (2 * PIECE) + half * PIECE
-            row = pl.multiple_of(row, PIECE)
-            high, low = split(value)
-            held[pl.ds(row, PIECE), :n] = high
-            held[pl.ds(row, PIECE), n:] = low
-
-        @pl.when(same)
-        def _():
-            put(own[...], y, k)
-            put(beside[...], 1 - y, k)
-
-        @pl.when(jnp.logical_not(same))
-        def _():
-            put(above[...], y, k)
-            put(across[...], 1 - y, k)
-
-        put(swapped[0], y, 1 - k)
-        put(swapped[1], 1 - y, 1 - k)
+        for s in range(groups):
+            own, beside, above, across, swapped = sets[5 * s : 5 * s + 5]
+
+            def put(value, y_of, half, s=s):
+                row = half * (2 * PIECE) + y_of * PIECE if leafwise else y_of * (2 * PIECE) + half * PIECE
+                row = pl.multiple_of(row + s * (4 * PIECE), PIECE)
+                high, low = split(value)
+                held[pl.ds(row, PIECE), :n] = high
+                held[pl.ds(row, PIECE), n:] = low
+
+            @pl.when(same)
+            def _():
+                put(own[...], y, k)
+                put(beside[...], 1 - y, k)
+
+            @pl.when(jnp.logical_not(same))
+            def _():
+                put(above[...], y, k)
+                put(across[...], 1 - y, k)
+
+            put(swapped[0], y, 1 - k)
+            put(swapped[1], 1 - y, 1 - k)
 
     total = None
     for t, (start, width) in enumerate(spans):
@@ -219,7 +221,7 @@
     work = sum(rows * t[4] for t in terms)
     return pl.pallas_call(
         functools.partial(
-            kernel_body, tuple((t[3], t[4]) for t in terms), mask is not None, add is not None, separate, leafwise
+            kernel_body, tuple((t[3], t[4]) for t in terms), mask is not None, add is not None, separate, leafwise, len(pieces) // 5
         ),
         out_shape=jax.ShapeDtypeStruct(shape, F32),
         grid_spec=pltpu.PrefetchScalarGridSpec(
@@ -227,7 +229,7 @@
             grid=(steps,),
             in_specs=specs,
             out_specs=out_spec,
-            scratch_shapes=[pltpu.VMEM((4 * PIECE, 2 * n), BF16)],
+            scratch_shapes=[pltpu.VMEM((len(pieces) // 5 * 4 * PIECE, 2 * n), BF16)],
         ),
         compiler_params=pltpu.CompilerParams(vmem_limit_bytes=32 << 20),
         cost_estimate=pl.CostEstimate(flops=8 * work * n, bytes_accessed=4 * work, transcendentals=0),
@@ -328,13 +330,14 @@
         root_half.append(right - (mine + other))
     root_pieces = [spread(h) for h in root_half]
 
-    columns = lambda g: [
-        (inverse_root, (256, 512), lambda i, b=b: (i, 2 * b + g), 2 * PIECE * b, 2 * PIECE) for b in (0, 1)
+    columns = [
+        (inverse_root, (256, 512), lambda i, b=b, s=s: (i, 2 * b + s), 4 * PIECE * s + 2 * PIECE * b, 2 * PIECE)
+        for s in (0, 1)
+        for b in (0, 1)
     ]
-    part = apply(root_pieces[0], columns(0), 1024, 256)
     mine, theirs = [], []
     for g in (0, 1):
-        final = apply(root_pieces[1], columns(1), 512, 256, first_tile=2 * g, add=part)
+        final = apply(root_pieces[0] + root_pieces[1], columns, 512, 256, first_tile=2 * g)
         one_half, other = halve(final.reshape(2, PIECE, n))
         mine.append(one_half + other)
         theirs.append(send(mine[g], TO_CORE))

time: 200 us -> 200 us (level)
    pallas_call x14 -> x13, Pallas kernels: 18.1 us -> 17.4 us  [apply(): pl.pallas_call(functools.partial(kernel_body, tuple(((t[3], t[4]) for t i...]
  transfers between devices with their start and end apart: 76 -> 76, of which waited for: 29 -> 30; matrix products, arithmetic and copies ran while one was open for 8% -> 8% of each run, Pallas kernels for 8% -> 7%
where the time goes in v5:
time: 200 us
  starting transfers between devices  99.5 us (50%)
  waiting for transfers between devices  59.7 us (30%)
  Pallas kernels  17.4 us (9%)
  local copies, waits for them, and re-layouts  14.1 us (7%)
  other arithmetic  7.32 us (4%)
    ppermute x76, starting transfers between devices, send(): return lax.ppermute(value, AXES, pairs)  99.5 us
    ppermute x76, waiting for transfers between devices, send(): return lax.ppermute(value, AXES, pairs)  59.7 us
    pallas_call x13, Pallas kernels, apply(): pl.pallas_call(functools.partial(kernel_body, tuple(((t[3], t[4]) for t i...  17.4 us
    slice x1, local copies, waits for them, and re-layouts, grid_body(): mid_to_root[0:1]  8.48 us
  transfers between devices with their start and end apart: 76, of which 30 were waited for; matrix products, arithmetic and copies ran while one was open for 8% of the time, Pallas kernels for 7%

profile of v5, /device:TPU:0, one launch (start us, length us, event | category | flops | bytes accessed | tf_op | source)
XLA Modules:
  0.0 199.7 jit_solution(4542833616336600572)
XLA Ops:
  1.7 7.0 %collective-permute-start = (f32[256,128]{1,0:T(8,128)S(1)}, f32[256,128]{1,0:T(8,128)S(1)}, u32[]{:S(2)}, u32[]{:S(2)}) collective-permute-start(f32[256,128]{1,0:T(8,128)S(1)} %get-tuple-element.17), channel_id=1, source_target_pairs={{0,24},{1,25},{8,16},{9,17},{4,28},{5,29},{12,20},{13,21},{18,10},... | collective-permute-start | bytes 393224 | tf_op jit(solution)/shard_map/ppermute | solution.py:89
  10.1 8.5 %fusion.1 = (f32[1,1024,1024]{2,1,0:T(8,128)}, f32[1,1024,1024]{2,1,0:T(8,128)}) fusion(f32[2,1024,1024]{2,1,0:T(8,128)} %param.20), kind=kLoop, calls=%fused_computation.81 | loop fusion | bytes 16777216 | tf_op jit(solution)/shard_map/slice | solution.py:315
  22.3 2.9 %collective-permute-start.11 = (f32[256,128]{1,0:T(8,128)S(1)}, f32[256,128]{1,0:T(8,128)S(1)}, u32[]{:S(2)}, u32[]{:S(2)}) collective-permute-start(f32[256,128]{1,0:T(8,128)S(1)} %broadcast_select_fusion.8.refs_0_), channel_id=1, source_target_pairs={{0,12},{1,13},{8,4},{9,5},{16,28},{17,29},{24,20},{25,21},{4,8},{5... | collective-permute-start | bytes 393224 | tf_op jit(solution)/shard_map/ppermute | solution.py:89
  25.2 4.1 %collective-permute-done.2.refs_2_ = f32[256,128]{1,0:T(8,128)S(1)} collective-permute-done((f32[256,128]{1,0:T(8,128)S(1)}, f32[256,128]{1,0:T(8,128)S(1)}, u32[]{:S(2)}, u32[]{:S(2)}) %collective-permute-start.2) | collective-permute-done | bytes 131104 | tf_op jit(solution)/shard_map/ppermute | solution.py:89
  31.9 2.4 %collective-permute-done.11.refs_3_ = f32[256,128]{1,0:T(8,128)S(1)} collective-permute-done((f32[256,128]{1,0:T(8,128)S(1)}, f32[256,128]{1,0:T(8,128)S(1)}, u32[]{:S(2)}, u32[]{:S(2)}) %collective-permute-start.11) | collective-permute-done | bytes 131104 | tf_op jit(solution)/shard_map/ppermute | solution.py:89
  42.3 3.0 %collective-permute-done.6 = f32[256,128]{1,0:T(8,128)S(1)} collective-permute-done((f32[256,128]{1,0:T(8,128)S(1)}, f32[256,128]{1,0:T(8,128)S(1)}, u32[]{:S(2)}, u32[]{:S(2)}) %collective-permute-start.6) | collective-permute-done | bytes 131104 | tf_op jit(solution)/shard_map/ppermute | solution.py:89
  49.7 6.2 %collective-permute-start.18 = (f32[256,128]{1,0:T(8,128)S(1)}, f32[256,128]{1,0:T(8,128)S(1)}, u32[]{:S(2)}, u32[]{:S(2)}) collective-permute-start(f32[256,128]{1,0:T(8,128)S(1)} %get-tuple-element.7.refs_0_), channel_id=1, source_target_pairs={{0,8},{1,9},{8,0},{9,1},{16,24},{17,25},{24,16},{25,17},{4,12},{5,... | collective-permute-start | bytes 393224 | tf_op jit(solution)/shard_map/ppermute | solution.py:89
  62.6 2.3 %collective-permute-done.17.refs_1_ = f32[256,128]{1,0:T(8,128)S(1)} collective-permute-done((f32[256,128]{1,0:T(8,128)S(1)}, f32[256,128]{1,0:T(8,128)S(1)}, u32[]{:S(2)}, u32[]{:S(2)}) %collective-permute-start.17) | collective-permute-done | bytes 131104 | tf_op jit(solution)/shard_map/ppermute | solution.py:89
  65.1 2.6 %collective-permute-done.32.refs_1_ = f32[256,128]{1,0:T(8,128)S(1)} collective-permute-done((f32[256,128]{1,0:T(8,128)S(1)}, f32[256,128]{1,0:T(8,128)S(1)}, u32[]{:S(2)}, u32[]{:S(2)}) %collective-permute-start.32) | collective-permute-done | bytes 131104 | tf_op jit(solution)/shard_map/ppermute | solution.py:89
  71.7 2.4 %collective-permute-start.22 = (f32[256,128]{1,0:T(8,128)S(1)}, f32[256,128]{1,0:T(8,128)S(1)}, u32[]{:S(2)}, u32[]{:S(2)}) collective-permute-start(f32[256,128]{1,0:T(8,128)S(1)} %add_bitcast_fusion.7), channel_id=1, source_target_pairs={{0,2},{1,3},{8,10},{9,11},{16,18},{17,19},{24,26},{25,27},{4,6},{5... | collective-permute-start | bytes 393224 | tf_op jit(solution)/shard_map/ppermute | solution.py:89
  75.5 2.6 %collective-permute-done.22 = f32[256,128]{1,0:T(8,128)S(1)} collective-permute-done((f32[256,128]{1,0:T(8,128)S(1)}, f32[256,128]{1,0:T(8,128)S(1)}, u32[]{:S(2)}, u32[]{:S(2)}) %collective-permute-start.22) | collective-permute-done | bytes 131104 | tf_op jit(solution)/shard_map/ppermute | solution.py:89
  78.2 5.3 %collective-permute-start.23 = (f32[256,128]{1,0:T(8,128)S(1)}, f32[256,128]{1,0:T(8,128)S(1)}, u32[]{:S(2)}, u32[]{:S(2)}) collective-permute-start(f32[256,128]{1,0:T(8,128)S(1)} %bitcast_subtract_fusion.3), channel_id=1, source_target_pairs={{0,24},{1,25},{8,16},{9,17},{4,28},{5,29},{12,20},{13,21},{18,10},... | collective-permute-start | bytes 393224 | tf_op jit(solution)/shard_map/ppermute | solution.py:89
  85.7 3.4 %copy-done.2 = f32[4,1024,512]{2,1,0:T(8,128)S(1)} copy-done((f32[4,1024,512]{2,1,0:T(8,128)S(1)}, f32[4,1024,512]{2,1,0:T(8,128)}, u32[]{:S(2)}) %copy-start.2) | copy-done | bytes 8388632
  93.9 2.7 %collective-permute-start.26 = (f32[256,128]{1,0:T(8,128)S(1)}, f32[256,128]{1,0:T(8,128)S(1)}, u32[]{:S(2)}, u32[]{:S(2)}) collective-permute-start(f32[256,128]{1,0:T(8,128)S(1)} %broadcast_select_fusion.6.refs_0_), channel_id=1, source_target_pairs={{0,12},{1,13},{8,4},{9,5},{16,28},{17,29},{24,20},{25,21},{4,8},{5... | collective-permute-start | bytes 393224 | tf_op jit(solution)/shard_map/ppermute | solution.py:89
  102.4 2.4 %collective-permute-done.40.refs_2_ = f32[256,128]{1,0:T(8,128)S(1)} collective-permute-done((f32[256,128]{1,0:T(8,128)S(1)}, f32[256,128]{1,0:T(8,128)S(1)}, u32[]{:S(2)}, u32[]{:S(2)}) %collective-permute-start.40) | collective-permute-done | bytes 131104 | tf_op jit(solution)/shard_map/ppermute | solution.py:89
  111.5 4.1 %collective-permute-done.29 = f32[256,128]{1,0:T(8,128)S(1)} collective-permute-done((f32[256,128]{1,0:T(8,128)S(1)}, f32[256,128]{1,0:T(8,128)S(1)}, u32[]{:S(2)}, u32[]{:S(2)}) %collective-permute-start.29) | collective-permute-done | bytes 131104 | tf_op jit(solution)/shard_map/ppermute | solution.py:89
  115.7 3.8 %collective-permute-start.51 = (f32[256,128]{1,0:T(8,128)S(1)}, f32[256,128]{1,0:T(8,128)S(1)}, u32[]{:S(2)}, u32[]{:S(2)}) collective-permute-start(f32[256,128]{1,0:T(8,128)S(1)} %add.214), channel_id=1, source_target_pairs={{0,24},{1,25},{8,16},{9,17},{4,28},{5,29},{12,20},{13,21},{18,10},... | collective-permute-start | bytes 393224 | tf_op jit(solution)/shard_map/ppermute | solution.py:89
  119.8 2.4 %collective-permute-start.46 = (f32[256,128]{1,0:T(8,128)S(1)}, f32[256,128]{1,0:T(8,128)S(1)}, u32[]{:S(2)}, u32[]{:S(2)}) collective-permute-start(f32[256,128]{1,0:T(8,128)S(1)} %add.220), channel_id=1, source_target_pairs={{0,24},{1,25},{8,16},{9,17},{4,28},{5,29},{12,20},{13,21},{18,10},... | collective-permute-start | bytes 393224 | tf_op jit(solution)/shard_map/ppermute | solution.py:89
  123.2 6.0 %collective-permute-start.53 = (f32[256,128]{1,0:T(8,128)S(1)}, f32[256,128]{1,0:T(8,128)S(1)}, u32[]{:S(2)}, u32[]{:S(2)}) collective-permute-start(f32[256,128]{1,0:T(8,128)S(1)} %get-tuple-element.27.refs_0_), channel_id=1, source_target_pairs={{0,8},{1,9},{8,0},{9,1},{16,24},{17,25},{24,16},{25,17},{4,12},{5,... | collective-permute-start | bytes 393224 | tf_op jit(solution)/shard_map/ppermute | solution.py:89
  134.0 2.3 %collective-permute-start.49 = (f32[256,128]{1,0:T(8,128)S(1)}, f32[256,128]{1,0:T(8,128)S(1)}, u32[]{:S(2)}, u32[]{:S(2)}) collective-permute-start(f32[256,128]{1,0:T(8,128)S(1)} %get-tuple-element.28.refs_0_), channel_id=1, source_target_pairs={{0,12},{1,13},{8,4},{9,5},{16,28},{17,29},{24,20},{25,21},{4,8},{5... | collective-permute-start | bytes 393224 | tf_op jit(solution)/shard_map/ppermute | solution.py:89
  136.3 3.2 %collective-permute-done.52.refs_1_ = f32[256,128]{1,0:T(8,128)S(1)} collective-permute-done((f32[256,128]{1,0:T(8,128)S(1)}, f32[256,128]{1,0:T(8,128)S(1)}, u32[]{:S(2)}, u32[]{:S(2)}) %collective-permute-start.52) | collective-permute-done | bytes 131104 | tf_op jit(solution)/shard_map/ppermute | solution.py:89
  139.7 2.8 %collective-permute-done.47.refs_1_ = f32[256,128]{1,0:T(8,128)S(1)} collective-permute-done((f32[256,128]{1,0:T(8,128)S(1)}, f32[256,128]{1,0:T(8,128)S(1)}, u32[]{:S(2)}, u32[]{:S(2)}) %collective-permute-start.47) | collective-permute-done | bytes 131104 | tf_op jit(solution)/shard_map/ppermute | solution.py:89
  147.5 2.3 %collective-permute-start.57 = (f32[256,128]{1,0:T(8,128)S(1)}, f32[256,128]{1,0:T(8,128)S(1)}, u32[]{:S(2)}, u32[]{:S(2)}) collective-permute-start(f32[256,128]{1,0:T(8,128)S(1)} %add_bitcast_fusion.3), channel_id=1, source_target_pairs={{0,2},{1,3},{8,10},{9,11},{16,18},{17,19},{24,26},{25,27},{4,6},{5... | collective-permute-start | bytes 393224 | tf_op jit(solution)/shard_map/ppermute | solution.py:89
  151.2 2.9 %collective-permute-done.57 = f32[256,128]{1,0:T(8,128)S(1)} collective-permute-done((f32[256,128]{1,0:T(8,128)S(1)}, f32[256,128]{1,0:T(8,128)S(1)}, u32[]{:S(2)}, u32[]{:S(2)}) %collective-permute-start.57) | collective-permute-done | bytes 131104 | tf_op jit(solution)/shard_map/ppermute | solution.py:89
  154.2 2.5 %collective-permute-done.64 = f32[256,128]{1,0:T(8,128)S(1)} collective-permute-done((f32[256,128]{1,0:T(8,128)S(1)}, f32[256,128]{1,0:T(8,128)S(1)}, u32[]{:S(2)}, u32[]{:S(2)}) %collective-permute-start.64) | collective-permute-done | bytes 131104 | tf_op jit(solution)/shard_map/ppermute | solution.py:89
  156.7 4.8 %collective-permute-start.65 = (f32[256,128]{1,0:T(8,128)S(1)}, f32[256,128]{1,0:T(8,128)S(1)}, u32[]{:S(2)}, u32[]{:S(2)}) collective-permute-start(f32[256,128]{1,0:T(8,128)S(1)} %get-tuple-element.13), channel_id=1, source_target_pairs={{0,24},{1,25},{8,16},{9,17},{4,28},{5,29},{12,20},{13,21},{18,10},... | collective-permute-start | bytes 393224 | tf_op jit(solution)/shard_map/ppermute | solution.py:89
  162.9 2.6 %collective-permute-done.65 = f32[256,128]{1,0:T(8,128)S(1)} collective-permute-done((f32[256,128]{1,0:T(8,128)S(1)}, f32[256,128]{1,0:T(8,128)S(1)}, u32[]{:S(2)}, u32[]{:S(2)}) %collective-permute-start.65) | collective-permute-done | bytes 131104 | tf_op jit(solution)/shard_map/ppermute | solution.py:89
  165.5 5.2 %collective-permute-start.67 = (f32[256,128]{1,0:T(8,128)S(1)}, f32[256,128]{1,0:T(8,128)S(1)}, u32[]{:S(2)}, u32[]{:S(2)}) collective-permute-start(f32[256,128]{1,0:T(8,128)S(1)} %broadcast_select_fusion.refs_5_), channel_id=1, source_target_pairs={{0,8},{1,9},{8,0},{9,1},{16,24},{17,25},{24,16},{25,17},{4,12},{5,... | collective-permute-start | bytes 393224 | tf_op jit(solution)/shard_map/ppermute | solution.py:89
  179.0 2.6 %collective-permute-done.59.refs_1_ = f32[256,128]{1,0:T(8,128)S(1)} collective-permute-done((f32[256,128]{1,0:T(8,128)S(1)}, f32[256,128]{1,0:T(8,128)S(1)}, u32[]{:S(2)}, u32[]{:S(2)}) %collective-permute-start.59) | collective-permute-done | bytes 131104 | tf_op jit(solution)/shard_map/ppermute | solution.py:89
  188.2 2.3 %collective-permute-start.71 = (f32[256,128]{1,0:T(8,128)S(1)}, f32[256,128]{1,0:T(8,128)S(1)}, u32[]{:S(2)}, u32[]{:S(2)}) collective-permute-start(f32[256,128]{1,0:T(8,128)S(1)} %add_bitcast_fusion.1), channel_id=1, source_target_pairs={{0,2},{1,3},{8,10},{9,11},{16,18},{17,19},{24,26},{25,27},{4,6},{5... | collective-permute-start | bytes 393224 | tf_op jit(solution)/shard_map/ppermute | solution.py:89
  192.3 2.5 %collective-permute-done.71 = f32[256,128]{1,0:T(8,128)S(1)} collective-permute-done((f32[256,128]{1,0:T(8,128)S(1)}, f32[256,128]{1,0:T(8,128)S(1)}, u32[]{:S(2)}, u32[]{:S(2)}) %collective-permute-start.71) | collective-permute-done | bytes 131104 | tf_op jit(solution)/shard_map/ppermute | solution.py:89
  194.9 2.2 %collective-permute-done.73 = f32[256,128]{1,0:T(8,128)S(1)} collective-permute-done((f32[256,128]{1,0:T(8,128)S(1)}, f32[256,128]{1,0:T(8,128)S(1)}, u32[]{:S(2)}, u32[]{:S(2)}) %collective-permute-start.73) | collective-permute-done | bytes 131104 | tf_op jit(solution)/shard_map/ppermute | solution.py:89
  (252 shorter events, 85.6 us)
Async XLA Ops:
  1.7 16.9 %collective-permute-start = (f32[256,128]{1,0:T(8,128)S(1)}, f32[256,128]{1,0:T(8,128)S(1)}, u32[]{:S(2)}, u32[]{:S(2)}) collective-permute-start(f32[256,128]{1,0:T(8,128)S(1)} %get-tuple-element.17), channel_id=1, source_target_pairs={{0,24},{1,25},{8,16},{9,17},{4,28},{5,29},{12,20},{13,21},{18,10},... | collective-permute-start | bytes 393224 | tf_op jit(solution)/shard_map/ppermute | solution.py:89
  8.6 13.5 %collective-permute-start.8 = (f32[256,128]{1,0:T(8,128)S(1)}, f32[256,128]{1,0:T(8,128)S(1)}, u32[]{:S(2)}, u32[]{:S(2)}) collective-permute-start(f32[256,128]{1,0:T(8,128)S(1)} %get-tuple-element.18), channel_id=1, source_target_pairs={{0,24},{1,25},{8,16},{9,17},{4,28},{5,29},{12,20},{13,21},{18,10},... | collective-permute-start | bytes 393224 | tf_op jit(solution)/shard_map/ppermute | solution.py:89
  18.6 12.3 %collective-permute-start.1 = (f32[256,128]{1,0:T(8,128)S(1)}, f32[256,128]{1,0:T(8,128)S(1)}, u32[]{:S(2)}, u32[]{:S(2)}) collective-permute-start(f32[256,128]{1,0:T(8,128)S(1)} %broadcast_select_fusion.9.refs_0_), channel_id=1, source_target_pairs={{0,4},{1,5},{8,12},{9,13},{16,20},{17,21},{24,28},{25,29},{4,0},{5... | collective-permute-start | bytes 393224 | tf_op jit(solution)/shard_map/ppermute | solution.py:89
  20.2 10.7 %collective-permute-start.3 = (f32[256,128]{1,0:T(8,128)S(1)}, f32[256,128]{1,0:T(8,128)S(1)}, u32[]{:S(2)}, u32[]{:S(2)}) collective-permute-start(f32[256,128]{1,0:T(8,128)S(1)} %broadcast_select_fusion.9.refs_0_), channel_id=1, source_target_pairs={{0,12},{1,13},{8,4},{9,5},{16,28},{17,29},{24,20},{25,21},{4,8},{5... | collective-permute-start | bytes 393224 | tf_op jit(solution)/shard_map/ppermute | solution.py:89
  20.2 9.2 %collective-permute-start.2 = (f32[256,128]{1,0:T(8,128)S(1)}, f32[256,128]{1,0:T(8,128)S(1)}, u32[]{:S(2)}, u32[]{:S(2)}) collective-permute-start(f32[256,128]{1,0:T(8,128)S(1)} %broadcast_select_fusion.9.refs_0_), channel_id=1, source_target_pairs={{0,8},{1,9},{8,0},{9,1},{16,24},{17,25},{24,16},{25,17},{4,12},{5,... | collective-permute-start | bytes 393224 | tf_op jit(solution)/shard_map/ppermute | solution.py:89
  22.2 9.7 %collective-permute-start.10 = (f32[256,128]{1,0:T(8,128)S(1)}, f32[256,128]{1,0:T(8,128)S(1)}, u32[]{:S(2)}, u32[]{:S(2)}) collective-permute-start(f32[256,128]{1,0:T(8,128)S(1)} %broadcast_select_fusion.8.refs_0_), channel_id=1, source_target_pairs={{0,8},{1,9},{8,0},{9,1},{16,24},{17,25},{24,16},{25,17},{4,12},{5,... | collective-permute-start | bytes 393224 | tf_op jit(solution)/shard_map/ppermute | solution.py:89
  22.3 12.0 %collective-permute-start.11 = (f32[256,128]{1,0:T(8,128)S(1)}, f32[256,128]{1,0:T(8,128)S(1)}, u32[]{:S(2)}, u32[]{:S(2)}) collective-permute-start(f32[256,128]{1,0:T(8,128)S(1)} %broadcast_select_fusion.8.refs_0_), channel_id=1, source_target_pairs={{0,12},{1,13},{8,4},{9,5},{16,28},{17,29},{24,20},{25,21},{4,8},{5... | collective-permute-start | bytes 393224 | tf_op jit(solution)/shard_map/ppermute | solution.py:89
  47.6 9.8 %collective-permute-start.15 = (f32[256,128]{1,0:T(8,128)S(1)}, f32[256,128]{1,0:T(8,128)S(1)}, u32[]{:S(2)}, u32[]{:S(2)}) collective-permute-start(f32[256,128]{1,0:T(8,128)S(1)} %add.205), channel_id=1, source_target_pairs={{0,1},{1,0},{8,9},{9,8},{16,17},{17,16},{24,25},{25,24},{4,5},{5,4... | collective-permute-start | bytes 393224 | tf_op jit(solution)/shard_map/ppermute | solution.py:89
  47.7 9.7 %collective-permute-start.31 = (f32[256,128]{1,0:T(8,128)S(1)}, f32[256,128]{1,0:T(8,128)S(1)}, u32[]{:S(2)}, u32[]{:S(2)}) collective-permute-start(f32[256,128]{1,0:T(8,128)S(1)} %add.205), channel_id=1, source_target_pairs={{0,24},{1,25},{8,16},{9,17},{4,28},{5,29},{12,20},{13,21},{18,10},... | collective-permute-start | bytes 393224 | tf_op jit(solution)/shard_map/ppermute | solution.py:89
  49.7 10.8 %collective-permute-start.18 = (f32[256,128]{1,0:T(8,128)S(1)}, f32[256,128]{1,0:T(8,128)S(1)}, u32[]{:S(2)}, u32[]{:S(2)}) collective-permute-start(f32[256,128]{1,0:T(8,128)S(1)} %get-tuple-element.7.refs_0_), channel_id=1, source_target_pairs={{0,8},{1,9},{8,0},{9,1},{16,24},{17,25},{24,16},{25,17},{4,12},{5,... | collective-permute-start | bytes 393224 | tf_op jit(solution)/shard_map/ppermute | solution.py:89
  55.9 9.0 %collective-permute-start.17 = (f32[256,128]{1,0:T(8,128)S(1)}, f32[256,128]{1,0:T(8,128)S(1)}, u32[]{:S(2)}, u32[]{:S(2)}) collective-permute-start(f32[256,128]{1,0:T(8,128)S(1)} %get-tuple-element.7.refs_0_), channel_id=1, source_target_pairs={{0,4},{1,5},{8,12},{9,13},{16,20},{17,21},{24,28},{25,29},{4,0},{5... | collective-permute-start | bytes 393224 | tf_op jit(solution)/shard_map/ppermute | solution.py:89
  59.5 8.2 %collective-permute-start.32 = (f32[256,128]{1,0:T(8,128)S(1)}, f32[256,128]{1,0:T(8,128)S(1)}, u32[]{:S(2)}, u32[]{:S(2)}) collective-permute-start(f32[256,128]{1,0:T(8,128)S(1)} %get-tuple-element.9.refs_0_), channel_id=1, source_target_pairs={{0,4},{1,5},{8,12},{9,13},{16,20},{17,21},{24,28},{25,29},{4,0},{5... | collective-permute-start | bytes 393224 | tf_op jit(solution)/shard_map/ppermute | solution.py:89
  75.3 8.2 %collective-permute-start.37 = (f32[256,128]{1,0:T(8,128)S(1)}, f32[256,128]{1,0:T(8,128)S(1)}, u32[]{:S(2)}, u32[]{:S(2)}) collective-permute-start(f32[256,128]{1,0:T(8,128)S(1)} %add_bitcast_fusion.5), channel_id=1, source_target_pairs={{0,2},{1,3},{8,10},{9,11},{16,18},{17,19},{24,26},{25,27},{4,6},{5... | collective-permute-start | bytes 393224 | tf_op jit(solution)/shard_map/ppermute | solution.py:89
  78.2 14.8 %collective-permute-start.23 = (f32[256,128]{1,0:T(8,128)S(1)}, f32[256,128]{1,0:T(8,128)S(1)}, u32[]{:S(2)}, u32[]{:S(2)}) collective-permute-start(f32[256,128]{1,0:T(8,128)S(1)} %bitcast_subtract_fusion.3), channel_id=1, source_target_pairs={{0,24},{1,25},{8,16},{9,17},{4,28},{5,29},{12,20},{13,21},{18,10},... | collective-permute-start | bytes 393224 | tf_op jit(solution)/shard_map/ppermute | solution.py:89
  83.5 13.1 %collective-permute-start.38 = (f32[256,128]{1,0:T(8,128)S(1)}, f32[256,128]{1,0:T(8,128)S(1)}, u32[]{:S(2)}, u32[]{:S(2)}) collective-permute-start(f32[256,128]{1,0:T(8,128)S(1)} %bitcast_subtract_fusion.2), channel_id=1, source_target_pairs={{0,24},{1,25},{8,16},{9,17},{4,28},{5,29},{12,20},{13,21},{18,10},... | collective-permute-start | bytes 393224 | tf_op jit(solution)/shard_map/ppermute | solution.py:89
  93.1 8.1 %collective-permute-start.24 = (f32[256,128]{1,0:T(8,128)S(1)}, f32[256,128]{1,0:T(8,128)S(1)}, u32[]{:S(2)}, u32[]{:S(2)}) collective-permute-start(f32[256,128]{1,0:T(8,128)S(1)} %broadcast_select_fusion.6.refs_0_), channel_id=1, source_target_pairs={{0,4},{1,5},{8,12},{9,13},{16,20},{17,21},{24,28},{25,29},{4,0},{5... | collective-permute-start | bytes 393224 | tf_op jit(solution)/shard_map/ppermute | solution.py:89
  93.9 8.4 %collective-permute-start.26 = (f32[256,128]{1,0:T(8,128)S(1)}, f32[256,128]{1,0:T(8,128)S(1)}, u32[]{:S(2)}, u32[]{:S(2)}) collective-permute-start(f32[256,128]{1,0:T(8,128)S(1)} %broadcast_select_fusion.6.refs_0_), channel_id=1, source_target_pairs={{0,12},{1,13},{8,4},{9,5},{16,28},{17,29},{24,20},{25,21},{4,8},{5... | collective-permute-start | bytes 393224 | tf_op jit(solution)/shard_map/ppermute | solution.py:89
  96.6 8.2 %collective-permute-start.40 = (f32[256,128]{1,0:T(8,128)S(1)}, f32[256,128]{1,0:T(8,128)S(1)}, u32[]{:S(2)}, u32[]{:S(2)}) collective-permute-start(f32[256,128]{1,0:T(8,128)S(1)} %broadcast_select_fusion.4.refs_0_), channel_id=1, source_target_pairs={{0,8},{1,9},{8,0},{9,1},{16,24},{17,25},{24,16},{25,17},{4,12},{5,... | collective-permute-start | bytes 393224 | tf_op jit(solution)/shard_map/ppermute | solution.py:89
  96.7 9.5 %collective-permute-start.39 = (f32[256,128]{1,0:T(8,128)S(1)}, f32[256,128]{1,0:T(8,128)S(1)}, u32[]{:S(2)}, u32[]{:S(2)}) collective-permute-start(f32[256,128]{1,0:T(8,128)S(1)} %broadcast_select_fusion.4.refs_0_), channel_id=1, source_target_pairs={{0,4},{1,5},{8,12},{9,13},{16,20},{17,21},{24,28},{25,29},{4,0},{5... | collective-permute-start | bytes 393224 | tf_op jit(solution)/shard_map/ppermute | solution.py:89
  110.7 8.9 %collective-permute-start.44 = (f32[256,128]{1,0:T(8,128)S(1)}, f32[256,128]{1,0:T(8,128)S(1)}, u32[]{:S(2)}, u32[]{:S(2)}) collective-permute-start(f32[256,128]{1,0:T(8,128)S(1)} %add_bitcast_fusion.4), channel_id=1, source_target_pairs={{0,2},{1,3},{8,10},{9,11},{16,18},{17,19},{24,26},{25,27},{4,6},{5... | collective-permute-start | bytes 393224 | tf_op jit(solution)/shard_map/ppermute | solution.py:89
  119.6 11.2 %collective-permute-start.45 = (f32[256,128]{1,0:T(8,128)S(1)}, f32[256,128]{1,0:T(8,128)S(1)}, u32[]{:S(2)}, u32[]{:S(2)}) collective-permute-start(f32[256,128]{1,0:T(8,128)S(1)} %add.220), channel_id=1, source_target_pairs={{0,1},{1,0},{8,9},{9,8},{16,17},{17,16},{24,25},{25,24},{4,5},{5,4... | collective-permute-start | bytes 393224 | tf_op jit(solution)/shard_map/ppermute | solution.py:89
  119.8 10.9 %collective-permute-start.46 = (f32[256,128]{1,0:T(8,128)S(1)}, f32[256,128]{1,0:T(8,128)S(1)}, u32[]{:S(2)}, u32[]{:S(2)}) collective-permute-start(f32[256,128]{1,0:T(8,128)S(1)} %add.220), channel_id=1, source_target_pairs={{0,24},{1,25},{8,16},{9,17},{4,28},{5,29},{12,20},{13,21},{18,10},... | collective-permute-start | bytes 393224 | tf_op jit(solution)/shard_map/ppermute | solution.py:89
  123.2 10.8 %collective-permute-start.53 = (f32[256,128]{1,0:T(8,128)S(1)}, f32[256,128]{1,0:T(8,128)S(1)}, u32[]{:S(2)}, u32[]{:S(2)}) collective-permute-start(f32[256,128]{1,0:T(8,128)S(1)} %get-tuple-element.27.refs_0_), channel_id=1, source_target_pairs={{0,8},{1,9},{8,0},{9,1},{16,24},{17,25},{24,16},{25,17},{4,12},{5,... | collective-permute-start | bytes 393224 | tf_op jit(solution)/shard_map/ppermute | solution.py:89
  129.2 10.3 %collective-permute-start.52 = (f32[256,128]{1,0:T(8,128)S(1)}, f32[256,128]{1,0:T(8,128)S(1)}, u32[]{:S(2)}, u32[]{:S(2)}) collective-permute-start(f32[256,128]{1,0:T(8,128)S(1)} %get-tuple-element.27.refs_0_), channel_id=1, source_target_pairs={{0,4},{1,5},{8,12},{9,13},{16,20},{17,21},{24,28},{25,29},{4,0},{5... | collective-permute-start | bytes 393224 | tf_op jit(solution)/shard_map/ppermute | solution.py:89
  130.4 9.1 %collective-permute-start.54 = (f32[256,128]{1,0:T(8,128)S(1)}, f32[256,128]{1,0:T(8,128)S(1)}, u32[]{:S(2)}, u32[]{:S(2)}) collective-permute-start(f32[256,128]{1,0:T(8,128)S(1)} %get-tuple-element.27.refs_0_), channel_id=1, source_target_pairs={{0,12},{1,13},{8,4},{9,5},{16,28},{17,29},{24,20},{25,21},{4,8},{5... | collective-permute-start | bytes 393224 | tf_op jit(solution)/shard_map/ppermute | solution.py:89
  130.8 8.9 %collective-permute-start.48 = (f32[256,128]{1,0:T(8,128)S(1)}, f32[256,128]{1,0:T(8,128)S(1)}, u32[]{:S(2)}, u32[]{:S(2)}) collective-permute-start(f32[256,128]{1,0:T(8,128)S(1)} %get-tuple-element.28.refs_0_), channel_id=1, source_target_pairs={{0,8},{1,9},{8,0},{9,1},{16,24},{17,25},{24,16},{25,17},{4,12},{5,... | collective-permute-start | bytes 393224 | tf_op jit(solution)/shard_map/ppermute | solution.py:89
  132.8 9.8 %collective-permute-start.47 = (f32[256,128]{1,0:T(8,128)S(1)}, f32[256,128]{1,0:T(8,128)S(1)}, u32[]{:S(2)}, u32[]{:S(2)}) collective-permute-start(f32[256,128]{1,0:T(8,128)S(1)} %get-tuple-element.28.refs_0_), channel_id=1, source_target_pairs={{0,4},{1,5},{8,12},{9,13},{16,20},{17,21},{24,28},{25,29},{4,0},{5... | collective-permute-start | bytes 393224 | tf_op jit(solution)/shard_map/ppermute | solution.py:89
  134.0 8.5 %collective-permute-start.49 = (f32[256,128]{1,0:T(8,128)S(1)}, f32[256,128]{1,0:T(8,128)S(1)}, u32[]{:S(2)}, u32[]{:S(2)}) collective-permute-start(f32[256,128]{1,0:T(8,128)S(1)} %get-tuple-element.28.refs_0_), channel_id=1, source_target_pairs={{0,12},{1,13},{8,4},{9,5},{16,28},{17,29},{24,20},{25,21},{4,8},{5... | collective-permute-start | bytes 393224 | tf_op jit(solution)/shard_map/ppermute | solution.py:89
  156.7 8.8 %collective-permute-start.65 = (f32[256,128]{1,0:T(8,128)S(1)}, f32[256,128]{1,0:T(8,128)S(1)}, u32[]{:S(2)}, u32[]{:S(2)}) collective-permute-start(f32[256,128]{1,0:T(8,128)S(1)} %get-tuple-element.13), channel_id=1, source_target_pairs={{0,24},{1,25},{8,16},{9,17},{4,28},{5,29},{12,20},{13,21},{18,10},... | collective-permute-start | bytes 393224 | tf_op jit(solution)/shard_map/ppermute | solution.py:89
  161.6 10.7 %collective-permute-start.58 = (f32[256,128]{1,0:T(8,128)S(1)}, f32[256,128]{1,0:T(8,128)S(1)}, u32[]{:S(2)}, u32[]{:S(2)}) collective-permute-start(f32[256,128]{1,0:T(8,128)S(1)} %get-tuple-element.14), channel_id=1, source_target_pairs={{0,24},{1,25},{8,16},{9,17},{4,28},{5,29},{12,20},{13,21},{18,10},... | collective-permute-start | bytes 393224 | tf_op jit(solution)/shard_map/ppermute | solution.py:89
  165.5 9.4 %collective-permute-start.67 = (f32[256,128]{1,0:T(8,128)S(1)}, f32[256,128]{1,0:T(8,128)S(1)}, u32[]{:S(2)}, u32[]{:S(2)}) collective-permute-start(f32[256,128]{1,0:T(8,128)S(1)} %broadcast_select_fusion.refs_5_), channel_id=1, source_target_pairs={{0,8},{1,9},{8,0},{9,1},{16,24},{17,25},{24,16},{25,17},{4,12},{5,... | collective-permute-start | bytes 393224 | tf_op jit(solution)/shard_map/ppermute | solution.py:89
  170.7 8.1 %collective-permute-start.66 = (f32[256,128]{1,0:T(8,128)S(1)}, f32[256,128]{1,0:T(8,128)S(1)}, u32[]{:S(2)}, u32[]{:S(2)}) collective-permute-start(f32[256,128]{1,0:T(8,128)S(1)} %broadcast_select_fusion.refs_5_), channel_id=1, source_target_pairs={{0,4},{1,5},{8,12},{9,13},{16,20},{17,21},{24,28},{25,29},{4,0},{5... | collective-permute-start | bytes 393224 | tf_op jit(solution)/shard_map/ppermute | solution.py:89
  (56 other events, 506.4 us)
